TPU v7x, 32 devices: a whole 2x2x4 slice. The times are simulated.
32 devices in a mesh: wide: 16 (over z, y, x), narrow: 2 (over core).
Axes of the slice: x: 2, y: 2, z: 4, core: 2. Of those that a mesh axis runs over, the one named last changes fastest.
Arguments:
- tokens: bfloat16 [4096, 1280], P(('wide', 'narrow')), may hold values from -6 to 6
- cotangent: bfloat16 [4096, 1280], P(('wide', 'narrow')), may hold values from -6 to 6
- lengths: int32 [16, 3], P('wide'), may hold values from 1 to 170, 256 in all within a row
- routes: int32 [4096, 7], P(('wide', 'narrow')), may hold values from 0 to 15, all different within a row; in each aligned block of 128 rows (0 to 127, 128 to 255, ...) at most 88 rows name the same one
- keep: int32 [4096, 7], P(('wide', 'narrow')), may hold values 0 or 1
- attn_gain: bfloat16 [1280], P('narrow'), may hold values from 0.099609375 to 1.8984375
- w_query: bfloat16 [1280, 1280], P('narrow'), may hold values from -0.15625 to 0.15625
- w_key: bfloat16 [1280, 1280], P('narrow'), may hold values from -0.15625 to 0.15625
- w_value: bfloat16 [1280, 1280], P('narrow'), may hold values from -0.15625 to 0.15625
- w_out: bfloat16 [1280, 1280], P('narrow'), may hold values from -1 to 1
- ffn_gain: bfloat16 [1280], P('narrow'), may hold values from 0.099609375 to 1.8984375
- w_router: bfloat16 [1280, 16], P('narrow'), may hold values from -0.078125 to 0.078125
- shared_gate: bfloat16 [1280, 896], P('narrow'), may hold values from -0.15625 to 0.15625
- shared_up: bfloat16 [1280, 896], P('narrow'), may hold values from -0.15625 to 0.15625
- shared_down: bfloat16 [896, 1280], P('narrow'), may hold values from -0.25 to 0.25
- expert_gate: bfloat16 [16, 1280, 896], P('wide', None, 'narrow'), may hold values from -0.15625 to 0.15625
- expert_up: bfloat16 [16, 1280, 896], P('wide', None, 'narrow'), may hold values from -0.15625 to 0.15625
- expert_down: bfloat16 [16, 896, 1280], P('wide', 'narrow'), may hold values from -0.5 to 0.5
Outputs:
- out: bfloat16 [4096, 1280], P(('wide', 'narrow'))
- grad_tokens: float32 [4096, 1280], P(('wide', 'narrow'))
- grad_attn_gain: float32 [1280], P('narrow')
- grad_w_query: float32 [1280, 1280], P('narrow')
- grad_w_key: float32 [1280, 1280], P('narrow')
- grad_w_value: float32 [1280, 1280], P('narrow')
- grad_w_out: float32 [1280, 1280], P('narrow')
- grad_ffn_gain: float32 [1280], P('narrow')
- grad_w_router: float32 [1280, 16], P('narrow')
- grad_shared_gate: float32 [1280, 896], P('narrow')
- grad_shared_up: float32 [1280, 896], P('narrow')
- grad_shared_down: float32 [896, 1280], P('narrow')
- grad_expert_gate: float32 [16, 1280, 896], P('wide', None, 'narrow')
- grad_expert_up: float32 [16, 1280, 896], P('wide', None, 'narrow')
- grad_expert_down: float32 [16, 896, 1280], P('wide', 'narrow')
Inputs may be any that keep to these rules, and one draw needn't show every extreme that they name: `lengths`: each row sums to 256; the longest document of every row has exactly 170 tokens. `routes`: each token names 7 different experts. Among the 128 tokens of one device no expert is named more than 88 times, and in every draw some device names some expert exactly 88 times.
All inputs are finite; a program needn't handle non-finite values. No bound on the sum of `keep` on one device may be relied on, other than what follows from the above.
Results may differ from a plain program's by a relative error of at most 0.018.
Values may be sent and summed in bfloat16 or wider, within the bound.
A program may use at most 256 MiB of HBM per device.

v0:
```python
import math

import jax
import jax.numpy as jnp
from jax import lax
from jax.sharding import PartitionSpec as P

HEAD_DIM = 128
TOPK = 7


EPS = 1e-06
MASKED = -1e30


def matmul(left, right):
    return jnp.dot(left, right, preferred_element_type=jnp.float32)


def matmul_left(left, right):
    return lax.dot_general(
        left, right, (((0,), (0,)), ((), ())), preferred_element_type=jnp.float32
    )


def matmul_right(left, right):
    return lax.dot_general(
        left, right, (((1,), (1,)), ((), ())), preferred_element_type=jnp.float32
    )


def doc_layout(positions, doc_lens):
    doc_ends = jnp.cumsum(doc_lens)
    passed = (positions[:, None] >= doc_ends[None, :]).astype(jnp.int32)
    doc_ids = jnp.sum(passed, axis=1)
    return (doc_ids, positions - jnp.sum(passed * doc_lens[None, :], axis=1))


def rotary_angles(positions):
    half_dim = HEAD_DIM // 2
    inverse = jnp.exp(
        jnp.arange(half_dim, dtype=jnp.float32) * (-2.0 * math.log(10000.0) / HEAD_DIM)
    )
    angles = positions.astype(jnp.float32)[:, None] * inverse[None, :]
    return (jnp.cos(angles), jnp.sin(angles))


def rotate(values, cosine, sine_table):
    half_dim = values.shape[-1] // 2
    lower_half = values[..., :half_dim]
    upper_half = values[..., half_dim:]
    cos_b = cosine[:, None, :]
    sin_b = sine_table[:, None, :]
    return jnp.concatenate(
        [lower_half * cos_b - upper_half * sin_b, upper_half * cos_b + lower_half * sin_b], axis=-1
    )


def norm_forward(values, gain_vec):
    row_scale = lax.rsqrt(jnp.mean(values * values, axis=-1, keepdims=True) + EPS)
    unit_rows = values * row_scale
    return (unit_rows * gain_vec, unit_rows, row_scale)


def norm_backward(grad_rows, unit_rows, row_scale, gain_vec):
    scaled = grad_rows * gain_vec
    grad_gain = jnp.sum(grad_rows * unit_rows, axis=0)
    grad_input = row_scale * (
        scaled - unit_rows * jnp.mean(scaled * unit_rows, axis=-1, keepdims=True)
    )
    return (grad_input, grad_gain)


def silu_parts(gate_vals):
    sigmoid_vals = jax.nn.sigmoid(gate_vals)
    return (gate_vals * sigmoid_vals, sigmoid_vals * (1.0 + gate_vals * (1.0 - sigmoid_vals)))


def expert_forward(in_rows, gate_mat, upper_mat):
    gate_vals = matmul(in_rows, gate_mat)
    upper = matmul(in_rows, upper_mat)
    act_vals, unused = silu_parts(gate_vals)
    return (gate_vals, upper, (act_vals * upper).astype(jnp.bfloat16))


def expert_backward(in_rows, grad_rows, gate_vals, upper, active, gate_mat, upper_mat, down_mat):
    grad_act = matmul_right(grad_rows, down_mat)
    act_vals, slope_vals = silu_parts(gate_vals)
    grad_gate = (grad_act * upper * slope_vals).astype(jnp.bfloat16)
    grad_upper = (grad_act * act_vals).astype(jnp.bfloat16)
    grad_down_mat = matmul_left(active, grad_rows)
    grad_gate_mat = matmul_left(in_rows, grad_gate)
    grad_upper_mat = matmul_left(in_rows, grad_upper)
    grad_input = matmul_right(grad_gate, gate_mat) + matmul_right(grad_upper, upper_mat)
    return (grad_input, grad_gate_mat, grad_upper_mat, grad_down_mat)


def attend_block(queries, keys_all, values_all, allowed):
    scores = jnp.einsum("qhd,khd->hqk", queries, keys_all, preferred_element_type=jnp.float32)
    masked = jnp.where(allowed[None], scores, MASKED)
    row_max = jnp.max(masked, axis=-1, keepdims=True)
    weights = jnp.exp(masked - row_max)
    row_total = jnp.sum(weights, axis=-1, keepdims=True)
    prob_rows = (weights / row_total).astype(jnp.bfloat16)
    attended = jnp.einsum("hqk,khd->qhd", prob_rows, values_all, preferred_element_type=jnp.float32)
    return (attended.astype(jnp.bfloat16), (row_max + jnp.log(row_total))[..., 0])


def attend_back(queries, keys_all, values_all, allowed, logsum, grad_attended):
    scores = jnp.einsum("qhd,khd->hqk", queries, keys_all, preferred_element_type=jnp.float32)
    masked = jnp.where(allowed[None], scores, MASKED)
    prob_rows = jnp.exp(masked - logsum[..., None])
    grad_probs = jnp.einsum(
        "qhd,khd->hqk", grad_attended, values_all, preferred_element_type=jnp.float32
    )
    row_delta = jnp.sum(prob_rows * grad_probs, axis=-1, keepdims=True)
    grad_scores = (prob_rows * (grad_probs - row_delta)).astype(jnp.bfloat16)
    grad_queries = jnp.einsum(
        "hqk,khd->qhd", grad_scores, keys_all, preferred_element_type=jnp.float32
    )
    grad_keys = jnp.einsum("hqk,qhd->khd", grad_scores, queries, preferred_element_type=jnp.float32)
    grad_values = jnp.einsum(
        "hqk,qhd->khd",
        prob_rows.astype(jnp.bfloat16),
        grad_attended,
        preferred_element_type=jnp.float32,
    )
    return (grad_queries, grad_keys, grad_values)


def per_device(
    tokens,
    cotangent,
    lengths,
    routes,
    keep,
    attn_gain,
    w_query,
    w_key,
    w_value,
    w_out,
    ffn_gain,
    w_router,
    shared_gate,
    shared_up,
    shared_down,
    expert_gate,
    expert_up,
    expert_down,
):
    narrow_size = lax.axis_size("narrow")
    narrow_index = lax.axis_index("narrow")
    wide_size = lax.axis_size("wide")
    local_rows = tokens.shape[0]
    model_width = tokens.shape[1]
    head_count = model_width // HEAD_DIM
    row_length = local_rows * narrow_size
    capacity = 8 * (3 * local_rows * TOPK // (16 * wide_size) + 1)
    gathered = (
        lax.all_gather(attn_gain, "narrow", axis=0, tiled=True),
        lax.all_gather(w_query, "narrow", axis=0, tiled=True),
        lax.all_gather(w_key, "narrow", axis=0, tiled=True),
        lax.all_gather(w_value, "narrow", axis=0, tiled=True),
        lax.all_gather(w_out, "narrow", axis=0, tiled=True),
        lax.all_gather(ffn_gain, "narrow", axis=0, tiled=True),
        lax.all_gather(w_router, "narrow", axis=0, tiled=True),
        lax.all_gather(shared_gate, "narrow", axis=0, tiled=True),
        lax.all_gather(shared_up, "narrow", axis=0, tiled=True),
        lax.all_gather(shared_down, "narrow", axis=0, tiled=True),
    )
    attn_scale = gathered[0].astype(jnp.float32)
    query_proj = gathered[1]
    key_proj = gathered[2]
    value_proj = gathered[3]
    output_proj = gathered[4]
    ffn_scale = gathered[5].astype(jnp.float32)
    router_proj = gathered[6]
    common_gate = gathered[7]
    common_upper = gathered[8]
    common_down = gathered[9]
    expert_mats = (expert_gate, expert_up, expert_down)
    routed_gate = expert_mats[0][0]
    routed_upper = expert_mats[1][0]
    routed_down = expert_mats[2][0]
    doc_lens = lengths[0]
    key_index = jnp.arange(row_length, dtype=jnp.int32)
    key_doc, unused = doc_layout(key_index, doc_lens)
    query_index = narrow_index * local_rows + jnp.arange(local_rows, dtype=jnp.int32)
    query_doc, query_pos = doc_layout(query_index, doc_lens)
    cosine, sine_table = rotary_angles(query_pos)
    inputs = tokens.astype(jnp.float32)
    normed, unit_one, scale_one = norm_forward(inputs, attn_scale)
    normed_one = normed.astype(jnp.bfloat16)
    head_shape = (local_rows, head_count, HEAD_DIM)
    query_rows = rotate(matmul(normed_one, query_proj).reshape(head_shape), cosine, sine_table)
    query_rows = (query_rows * HEAD_DIM ** (-0.5)).astype(jnp.bfloat16)
    key_rows = rotate(matmul(normed_one, key_proj).reshape(head_shape), cosine, sine_table).astype(
        jnp.bfloat16
    )
    valued = matmul(normed_one, value_proj).astype(jnp.bfloat16)
    all_keys, all_values = (
        lax.all_gather(key_rows.reshape(local_rows, model_width), "narrow", axis=0, tiled=True),
        lax.all_gather(valued, "narrow", axis=0, tiled=True),
    )
    all_keys = all_keys.reshape(row_length, head_count, HEAD_DIM)
    all_values = all_values.reshape(row_length, head_count, HEAD_DIM)
    block_rows = min(local_rows, 512)
    blocks = local_rows // block_rows
    query_blocks = query_rows.reshape(blocks, block_rows, head_count, HEAD_DIM)
    doc_blocks = query_doc.reshape(blocks, block_rows)
    index_blocks = query_index.reshape(blocks, block_rows)

    def allowed_for(doc_rows, index_rows):
        return (doc_rows[:, None] == key_doc[None, :]) & (key_index[None, :] <= index_rows[:, None])

    def forward_block(map_item):
        return attend_block(
            map_item[0], all_keys, all_values, allowed_for(map_item[1], map_item[2])
        )

    attended, logsum = lax.map(forward_block, (query_blocks, doc_blocks, index_blocks))
    attended = attended.reshape(local_rows, model_width)
    hidden = inputs + matmul(attended, output_proj)
    normed, unit_two, scale_two = norm_forward(hidden, ffn_scale)
    normed_two = normed.astype(jnp.bfloat16)
    logits = matmul(normed_two, router_proj)
    experts = router_proj.shape[1]
    pick_table = (routes[:, :, None] == jnp.arange(experts, dtype=jnp.int32)[None, None, :]).astype(
        jnp.float32
    )
    chosen = jnp.sum(pick_table * logits[:, None, :], axis=2)
    gate_probs = jax.nn.softmax(chosen, axis=1)
    keep_float = keep.astype(jnp.float32)
    mixing = gate_probs * keep_float
    common_gate_vals, common_upper_vals, common_act = expert_forward(
        normed_two, common_gate, common_upper
    )
    shared_out = matmul(common_act, common_down)
    pair_expert = routes.reshape(-1)
    pair_total = pair_expert.shape[0]
    onehot = (pair_expert[:, None] == jnp.arange(experts, dtype=jnp.int32)[None, :]).astype(
        jnp.int32
    )
    earlier = jnp.cumsum(onehot, axis=0) - onehot
    slot_place = jnp.sum(earlier * onehot, axis=1)
    slot_index = pair_expert * capacity + slot_place
    slot_total = experts * capacity
    source = (
        jnp.full((slot_total,), -1, jnp.int32)
        .at[slot_index]
        .set(jnp.arange(pair_total, dtype=jnp.int32))
    )
    filled = source >= 0
    pair_index = jnp.maximum(source, 0)

    def fill_slots(in_rows, row_index):
        taken = jnp.take(in_rows, row_index, axis=0)
        return jnp.where(filled[:, None], taken, jnp.zeros((), in_rows.dtype)).reshape(
            experts, capacity, model_width
        )

    received = lax.all_to_all(
        fill_slots(normed_two, pair_index // TOPK), "wide", split_axis=0, concat_axis=0, tiled=True
    )
    expert_in = lax.all_gather(received, "narrow", axis=0, tiled=True).reshape(-1, model_width)
    routed_gate_vals, routed_upper_vals, routed_act = expert_forward(
        expert_in, routed_gate, routed_upper
    )
    partial_value = matmul(routed_act, routed_down)
    expert_out = lax.psum_scatter(partial_value, "narrow", scatter_dimension=0, tiled=True)
    returned = lax.all_to_all(
        expert_out.astype(jnp.bfloat16).reshape(wide_size, capacity, model_width),
        "wide",
        split_axis=0,
        concat_axis=0,
        tiled=True,
    )
    pair_out = (
        jnp.take(returned.reshape(slot_total, model_width), slot_index, axis=0)
        .astype(jnp.float32)
        .reshape(local_rows, TOPK, model_width)
    )
    routed = jnp.sum(mixing[:, :, None] * pair_out, axis=1)
    output = (hidden + shared_out + routed).astype(jnp.bfloat16)
    grad_output = cotangent.astype(jnp.float32)
    grad_pairs = (
        (mixing[:, :, None] * grad_output[:, None, :])
        .astype(jnp.bfloat16)
        .reshape(pair_total, model_width)
    )
    grad_mixing = jnp.sum(pair_out * grad_output[:, None, :], axis=2)
    grad_received = lax.all_to_all(
        fill_slots(grad_pairs, pair_index), "wide", split_axis=0, concat_axis=0, tiled=True
    )
    grad_expert_out = lax.all_gather(grad_received, "narrow", axis=0, tiled=True).reshape(
        -1, model_width
    )
    grad_expert_in, grad_rgate, grad_rupper, grad_rdown = expert_backward(
        expert_in,
        grad_expert_out,
        routed_gate_vals,
        routed_upper_vals,
        routed_act,
        routed_gate,
        routed_upper,
        routed_down,
    )
    grad_slot_rows = lax.psum_scatter(grad_expert_in, "narrow", scatter_dimension=0, tiled=True)
    expert_grads = (grad_rgate, grad_rupper, grad_rdown)
    grad_back = lax.all_to_all(
        grad_slot_rows.astype(jnp.bfloat16).reshape(wide_size, capacity, model_width),
        "wide",
        split_axis=0,
        concat_axis=0,
        tiled=True,
    )
    grad_pair_rows = jnp.take(
        grad_back.reshape(slot_total, model_width), slot_index, axis=0
    ).astype(jnp.float32)
    grad_normed = jnp.sum(grad_pair_rows.reshape(local_rows, TOPK, model_width), axis=1)
    grad_gates = grad_mixing * keep_float
    grad_chosen = gate_probs * (
        grad_gates - jnp.sum(gate_probs * grad_gates, axis=1, keepdims=True)
    )
    grad_logits = jnp.sum(pick_table * grad_chosen[:, :, None], axis=1).astype(jnp.bfloat16)
    grad_router = matmul_left(normed_two, grad_logits)
    grad_normed = grad_normed + matmul_right(grad_logits, router_proj)
    grad_common_in, grad_cgate, grad_cupper, grad_cdown = expert_backward(
        normed_two,
        cotangent,
        common_gate_vals,
        common_upper_vals,
        common_act,
        common_gate,
        common_upper,
        common_down,
    )
    grad_normed = grad_normed + grad_common_in
    grad_hidden_norm, grad_ffn = norm_backward(grad_normed, unit_two, scale_two, ffn_scale)
    grad_hidden = grad_output + grad_hidden_norm
    grad_branch = grad_hidden.astype(jnp.bfloat16)
    grad_output_proj = matmul_left(attended, grad_branch)
    grad_attended = (
        matmul_right(grad_branch, output_proj)
        .astype(jnp.bfloat16)
        .reshape(blocks, block_rows, head_count, HEAD_DIM)
    )

    def backward_block(running, map_item):
        grad_queries, grad_keys, grad_values = attend_back(
            map_item[0],
            all_keys,
            all_values,
            allowed_for(map_item[1], map_item[2]),
            map_item[3],
            map_item[4],
        )
        return ((running[0] + grad_keys, running[1] + grad_values), grad_queries)

    empty_keys = jnp.zeros((row_length, head_count, HEAD_DIM), jnp.float32)
    sums_kv, grad_query_rows = lax.scan(
        backward_block,
        (empty_keys, empty_keys),
        (query_blocks, doc_blocks, index_blocks, logsum, grad_attended),
    )
    grad_key_own, grad_value_own = (
        lax.psum_scatter(
            sums_kv[0].reshape(row_length, model_width).astype(jnp.bfloat16),
            "narrow",
            scatter_dimension=0,
            tiled=True,
        ).astype(jnp.float32),
        lax.psum_scatter(
            sums_kv[1].reshape(row_length, model_width).astype(jnp.bfloat16),
            "narrow",
            scatter_dimension=0,
            tiled=True,
        ).astype(jnp.float32),
    )
    grad_query_rows = rotate(
        grad_query_rows.reshape(head_shape) * HEAD_DIM ** (-0.5), cosine, -sine_table
    )
    grad_query_rows = grad_query_rows.reshape(local_rows, model_width).astype(jnp.bfloat16)
    grad_key_rows = (
        rotate(grad_key_own.reshape(head_shape), cosine, -sine_table)
        .reshape(local_rows, model_width)
        .astype(jnp.bfloat16)
    )
    grad_value_rows = grad_value_own.astype(jnp.bfloat16)
    grad_query_proj = matmul_left(normed_one, grad_query_rows)
    grad_key_proj = matmul_left(normed_one, grad_key_rows)
    grad_value_proj = matmul_left(normed_one, grad_value_rows)
    grad_normed_one = (
        matmul_right(grad_query_rows, query_proj)
        + matmul_right(grad_key_rows, key_proj)
        + matmul_right(grad_value_rows, value_proj)
    )
    grad_input_norm, grad_attn = norm_backward(grad_normed_one, unit_one, scale_one, attn_scale)
    grad_tokens = grad_hidden + grad_input_norm
    halves = (
        lax.psum_scatter(
            grad_attn.astype(jnp.bfloat16), "narrow", scatter_dimension=0, tiled=True
        ).astype(jnp.float32),
        lax.psum_scatter(
            grad_query_proj.astype(jnp.bfloat16), "narrow", scatter_dimension=0, tiled=True
        ).astype(jnp.float32),
        lax.psum_scatter(
            grad_key_proj.astype(jnp.bfloat16), "narrow", scatter_dimension=0, tiled=True
        ).astype(jnp.float32),
        lax.psum_scatter(
            grad_value_proj.astype(jnp.bfloat16), "narrow", scatter_dimension=0, tiled=True
        ).astype(jnp.float32),
        lax.psum_scatter(
            grad_output_proj.astype(jnp.bfloat16), "narrow", scatter_dimension=0, tiled=True
        ).astype(jnp.float32),
        lax.psum_scatter(
            grad_ffn.astype(jnp.bfloat16), "narrow", scatter_dimension=0, tiled=True
        ).astype(jnp.float32),
        lax.psum_scatter(
            grad_router.astype(jnp.bfloat16), "narrow", scatter_dimension=0, tiled=True
        ).astype(jnp.float32),
        lax.psum_scatter(
            grad_cgate.astype(jnp.bfloat16), "narrow", scatter_dimension=0, tiled=True
        ).astype(jnp.float32),
        lax.psum_scatter(
            grad_cupper.astype(jnp.bfloat16), "narrow", scatter_dimension=0, tiled=True
        ).astype(jnp.float32),
        lax.psum_scatter(
            grad_cdown.astype(jnp.bfloat16), "narrow", scatter_dimension=0, tiled=True
        ).astype(jnp.float32),
    )
    owned = lax.psum(
        (
            halves[0],
            halves[1],
            halves[2],
            halves[3],
            halves[4],
            halves[5],
            halves[6],
            halves[7],
            halves[8],
            halves[9],
        ),
        "wide",
    )
    return (
        output,
        grad_tokens,
        owned[0],
        owned[1],
        owned[2],
        owned[3],
        owned[4],
        owned[5],
        owned[6],
        owned[7],
        owned[8],
        owned[9],
        expert_grads[0][None],
        expert_grads[1][None],
        expert_grads[2][None],
    )


def solution(mesh):
    in_specs = (
        P(("wide", "narrow"), None),
        P(("wide", "narrow"), None),
        P("wide", None),
        P(("wide", "narrow"), None),
        P(("wide", "narrow"), None),
        P("narrow"),
        P("narrow", None),
        P("narrow", None),
        P("narrow", None),
        P("narrow", None),
        P("narrow"),
        P("narrow", None),
        P("narrow", None),
        P("narrow", None),
        P("narrow", None),
        P("wide", None, "narrow"),
        P("wide", None, "narrow"),
        P("wide", "narrow", None),
    )
    out_specs = (
        P(("wide", "narrow"), None),
        P(("wide", "narrow"), None),
        P("narrow"),
        P("narrow", None),
        P("narrow", None),
        P("narrow", None),
        P("narrow", None),
        P("narrow"),
        P("narrow", None),
        P("narrow", None),
        P("narrow", None),
        P("narrow", None),
        P("wide", None, "narrow"),
        P("wide", None, "narrow"),
        P("wide", "narrow", None),
    )
    return jax.shard_map(
        per_device, mesh=mesh, in_specs=in_specs, out_specs=out_specs, check_vma=False
    )
```

profile of v0, /device:TPU:0, one launch (start us, length us, event | category | flops | bytes accessed | tf_op | source)
XLA Modules:
  0.0 1524.1 jit_solution(9163160603198860076)
XLA Ops:
  85.1 11.0 gather_fusion.1
  101.0 88.4 %all_to_all.20 = bf16[16,88,1280]{2,1,0:T(8,128)(2,1)} all-to-all(bf16[16,88,1280]{2,1,0:T(8,128)(2,1)S(1)} %get-tuple-element.134), channel_id=1, replica_groups=mesh['wide'=16,'narrow'=2] {'wide'}, dimensions={0} | all-to-all | bytes 7208960 | tf_op jit(solution)/shard_map/all_to_all | solution.py:262
  189.5 84.5 %all_to_all.21 = bf16[16,88,1280]{2,1,0:T(8,128)(2,1)} all-to-all(bf16[16,88,1280]{2,1,0:T(8,128)(2,1)} %get-tuple-element.133), channel_id=1, replica_groups=mesh['wide'=16,'narrow'=2] {'wide'}, dimensions={0} | all-to-all | bytes 7208960 | tf_op jit(solution)/shard_map/all_to_all | solution.py:292
  274.6 9.6 fusion.11
  290.5 10.4 multiply_convert_fusion
  305.0 7.4 convolution_add_fusion
  312.6 10.1 fusion.8
  322.8 15.5 %reduce-scatter.21.cloned.1.call-done = f32[1408,1280]{1,0:T(8,128)} async-done(((f32[2816,1280]{1,0:T(8,128)}), f32[1408,1280]{1,0:T(8,128)}) %reduce-scatter.21.cloned.1.call-update) | async-done | bytes 7208976 | tf_op jit(solution)/shard_map/reduce_scatter | solution.py:308
  343.4 6.9 all-to-all-start.3
  351.1 15.2 reduce-scatter.19.cloned.1.call-done
  371.5 48.6 %all-to-all-done.3 = bf16[16,88,1280]{2,1,0:T(8,128)(2,1)} async-done(((bf16[16,88,1280]{2,1,0:T(8,128)(2,1)}), bf16[16,88,1280]{2,1,0:T(8,128)(2,1)}, u32[]{:S(2)}, u32[]{:S(2)}) %all-to-all-start.3) | async-done | bytes 3604512 | tf_op jit(solution)/shard_map/all_to_all | solution.py:310
  420.1 18.0 %all-to-all-start.1 = ((bf16[16,88,1280]{2,1,0:T(8,128)(2,1)}), bf16[16,88,1280]{2,1,0:T(8,128)(2,1)}, u32[]{:S(2)}, u32[]{:S(2)}) async-start(bf16[16,88,1280]{2,1,0:T(8,128)(2,1)} %bitcast.144), calls=%async_computation.2 | async-start | bytes 7208960 | tf_op jit(solution)/shard_map/all_to_all | solution.py:271
  442.5 9.7 all-gather.20.cloned.1.call-done
  455.2 10.7 all-gather.24.cloned.1.call-done
  471.1 8.8 gather_fusion.3
  479.9 26.6 %all-to-all-done.1 = bf16[16,88,1280]{2,1,0:T(8,128)(2,1)} async-done(((bf16[16,88,1280]{2,1,0:T(8,128)(2,1)}), bf16[16,88,1280]{2,1,0:T(8,128)(2,1)}, u32[]{:S(2)}, u32[]{:S(2)}) %all-to-all-start.1) | async-done | bytes 3604512 | tf_op jit(solution)/shard_map/all_to_all | solution.py:271
  506.5 8.8 gather_fusion.2
  593.5 13.8 reduce-scatter.31.cloned.1.call-done
  607.3 14.0 reduce-scatter.35.cloned.1.call-done
  621.3 8.8 convolution_bitcast_fusion.2
  630.1 8.1 convolution_bitcast_fusion
  665.8 12.7 reduce-scatter.25.cloned.1.call-done
  678.5 15.5 %reduce-scatter.23.cloned.1.call-done = bf16[640,1280]{1,0:T(8,128)(2,1)} async-done(((bf16[1280,1280]{1,0:T(8,128)(2,1)}), bf16[640,1280]{1,0:T(8,128)(2,1)}) %reduce-scatter.23.cloned.1.call-update) | async-done | bytes 1638416 | tf_op jit(solution)/shard_map/reduce_scatter | solution.py:404
  694.0 823.0 %all-reduce.5 = (f32[640]{0:T(1024)}, f32[640,1280]{1,0:T(8,128)}, f32[640,1280]{1,0:T(8,128)}, f32[640,1280]{1,0:T(8,128)}, f32[640,1280]{1,0:T(8,128)}, /*inde...) all-reduce(f32[640]{0:T(1024)S(1)} %dynamic-slice_convert_fusion.1,, ...), channel_id=1, replica_groups=mesh['wide'=16,'narrow'=2] {'wide'}, use_global_device_ids=true, to_apply=%region_29.31 | all-reduce | flops 5008640 | bytes 30054400 | tf_op jit(solution)/shard_map/psum | solution.py:432
  (348 shorter events, 221.7 us)
Async XLA Ops:
  7.2 31.0 %all-gather.12.cloned.1.call-start = ((), (), s32[]{:S(2)}) async-start(), calls=%async_computation.16 | async-start | bytes 4915200 | tf_op jit(solution)/shard_map/all_gather | solution.py:163
  8.0 36.1 %all-gather.14.cloned.1.call-start = ((), (), s32[]{:S(2)}) async-start(), calls=%async_computation.17 | async-start | bytes 4915200 | tf_op jit(solution)/shard_map/all_gather | solution.py:161
  8.8 46.0 %all-gather.16.cloned.1.call-start = ((), (), s32[]{:S(2)}) async-start(), calls=%async_computation.18 | async-start | bytes 4915200 | tf_op jit(solution)/shard_map/all_gather | solution.py:162
  9.5 60.2 %all-gather.18.cloned.1.call-start = ((), (), s32[]{:S(2)}) async-start(), calls=%async_computation.19 | async-start | bytes 4915200 | tf_op jit(solution)/shard_map/all_gather | solution.py:164
  10.1 264.5 %all-gather.26.cloned.1.call-start = ((), (), s32[]{:S(2)}) async-start(), calls=%async_computation.23 | async-start | bytes 10813440 | tf_op jit(solution)/shard_map/all_gather | solution.py:265
  189.4 101.1 %all-gather.28.cloned.1.call-start = ((), (), s32[]{:S(2)}) async-start(), calls=%async_computation.25 | async-start | bytes 10813440 | tf_op jit(solution)/shard_map/all_gather | solution.py:295
  274.0 64.3 %reduce-scatter.21.cloned.1.call-start = ((), (), s32[]{:S(2)}) async-start(), calls=%async_computation.26 | async-start | bytes 21626880 | tf_op jit(solution)/shard_map/reduce_scatter | solution.py:308
  312.4 53.9 %reduce-scatter.19.cloned.1.call-start = ((), (), s32[]{:S(2)}) async-start(), calls=%async_computation.24 | async-start | bytes 21626880 | tf_op jit(solution)/shard_map/reduce_scatter | solution.py:270
  343.4 76.6 %all-to-all-start.3 = ((bf16[16,88,1280]{2,1,0:T(8,128)(2,1)}), bf16[16,88,1280]{2,1,0:T(8,128)(2,1)}, u32[]{:S(2)}, u32[]{:S(2)}) async-start(bf16[16,88,1280]{2,1,0:T(8,128)(2,1)} %bitcast.145), calls=%async_computation.5 | async-start | bytes 7208960 | tf_op jit(solution)/shard_map/all_to_all | solution.py:310
  350.4 89.2 %all-gather.22.cloned.1.call-start = ((), (), s32[]{:S(2)}) async-start(), calls=%async_computation.21 | async-start | bytes 3440640 | tf_op jit(solution)/shard_map/all_gather | solution.py:168
  420.1 86.4 %all-to-all-start.1 = ((bf16[16,88,1280]{2,1,0:T(8,128)(2,1)}), bf16[16,88,1280]{2,1,0:T(8,128)(2,1)}, u32[]{:S(2)}, u32[]{:S(2)}) async-start(bf16[16,88,1280]{2,1,0:T(8,128)(2,1)} %bitcast.144), calls=%async_computation.2 | async-start | bytes 7208960 | tf_op jit(solution)/shard_map/all_to_all | solution.py:271
  438.1 14.2 all-gather.20.cloned.1.call-start
  438.7 27.2 %all-gather.24.cloned.1.call-start = ((), (), s32[]{:S(2)}) async-start(), calls=%async_computation.22 | async-start | bytes 3440640 | tf_op jit(solution)/shard_map/all_gather | solution.py:169
  439.4 128.0 %reduce-scatter.39.cloned.1.call-start = ((), (), s32[]{:S(2)}) async-start(), calls=%async_computation.35 | async-start | bytes 983040
  548.2 31.2 %reduce-scatter.37.cloned.1.call-start = ((), (), s32[]{:S(2)}) async-start(), calls=%async_computation.34 | async-start | bytes 983040
  553.0 40.5 %reduce-scatter.33.cloned.1.call-start = ((), (), s32[]{:S(2)}) async-start(), calls=%async_computation.32 | async-start | bytes 3440640 | tf_op jit(solution)/shard_map/reduce_scatter | solution.py:425
  555.3 52.0 %reduce-scatter.31.cloned.1.call-start = ((), (), s32[]{:S(2)}) async-start(), calls=%async_computation.31 | async-start | bytes 3440640 | tf_op jit(solution)/shard_map/reduce_scatter | solution.py:422
  557.5 63.8 %reduce-scatter.35.cloned.1.call-start = ((), (), s32[]{:S(2)}) async-start(), calls=%async_computation.33 | async-start | bytes 3440640 | tf_op jit(solution)/shard_map/reduce_scatter | solution.py:428
  559.8 94.4 %reduce-scatter.41.cloned.1.call-start = ((), (), s32[]{:S(2)}) async-start(), calls=%async_computation.36 | async-start | bytes 491520
  561.0 104.8 %reduce-scatter.29.cloned.1.call-start = ((), (), s32[]{:S(2)}) async-start(), calls=%async_computation.30 | async-start | bytes 4915200 | tf_op jit(solution)/shard_map/reduce_scatter | solution.py:413
  563.8 102.0 %reduce-scatter.27.cloned.1.call-start = ((), (), s32[]{:S(2)}) async-start(), calls=%async_computation.29 | async-start | bytes 4915200 | tf_op jit(solution)/shard_map/reduce_scatter | solution.py:410
  571.2 107.3 %reduce-scatter.25.cloned.1.call-start = ((), (), s32[]{:S(2)}) async-start(), calls=%async_computation.28 | async-start | bytes 4915200 | tf_op jit(solution)/shard_map/reduce_scatter | solution.py:407
  588.1 106.0 %reduce-scatter.23.cloned.1.call-start = ((), (), s32[]{:S(2)}) async-start(), calls=%async_computation.27 | async-start | bytes 4915200 | tf_op jit(solution)/shard_map/reduce_scatter | solution.py:404
  664.7 852.3 %copy-start.1 = (bf16[1,448,1280]{2,1,0:T(8,128)(2,1)S(1)}, bf16[1,448,1280]{2,1,0:T(8,128)(2,1)}, u32[]{:S(2)}) copy-start(bf16[1,448,1280]{2,1,0:T(8,128)(2,1)} %param.37) | copy-start | bytes 3440644
  (76 other events, 927.2 us)
Sparse Core Ops, SparseCore 0:
  9.6 15.0 all-gather.11
  26.2 13.4 all-gather.13
  41.2 13.4 all-gather.15
  56.2 13.4 all-gather.17
  189.5 16.2 all-gather.25
  274.1 16.3 all-gather.27
  312.5 25.6 reduce-scatter.20
  340.5 25.7 reduce-scatter.18
  367.9 12.1 all-gather.21
  440.1 12.0 all-gather.19
  453.8 12.0 all-gather.23
  548.3 19.0 reduce-scatter.38
  570.2 9.1 reduce-scatter.36
  582.1 11.1 reduce-scatter.32
  595.9 11.3 reduce-scatter.30
  610.0 11.3 reduce-scatter.34
  623.4 9.0 reduce-scatter.40
  635.2 12.4 reduce-scatter.28
  650.5 12.6 reduce-scatter.26
  665.8 12.6 reduce-scatter.24
  681.3 12.6 reduce-scatter.22
where the time goes:
time: 1530 us; the launch traced here: 1520 us
  blocking collectives  1010 us (66%)
  waiting for transfers between devices  203 us (13%)
  matrix products  131 us (9%)
  local copies, waits for them, and re-layouts  85.3 us (6%)
  other arithmetic  51.6 us (3%)
  starting transfers between devices  27.1 us (2%)
  between operations  16.2 us (1%)
    psum x1, blocking collectives, per_device(): lax.psum((halves[0], halves[1], halves[2], halves[3], halves[4], halves[5...  823 us
    all_to_all x1, blocking collectives, per_device(): lax.all_to_all(fill_slots(normed_two, pair_index // TOPK), 'wide', split_...  88.4 us
    all_to_all x1, blocking collectives, per_device(): lax.all_to_all(fill_slots(grad_pairs, pair_index), 'wide', split_axis=0,...  84.5 us
    all_to_all x1, waiting for transfers between devices, per_device(): lax.all_to_all(grad_slot_rows.astype(jnp.bfloat16).reshape(wide_size, cap...  48.6 us
    dot_general x11, matrix products, matmul(): return jnp.dot(left, right, preferred_element_type=jnp.float32)  45 us
    dot_general x11, matrix products, matmul_left(): lax.dot_general(left, right, (((0,), (0,)), ((), ())), preferred_element_...  40.7 us
    dot_general x11, matrix products, matmul_right(): lax.dot_general(left, right, (((1,), (1,)), ((), ())), preferred_element_...  39.1 us
  transfers between devices with their start and end apart: 23, of which 15 were waited for; matrix products, arithmetic and copies ran while one was open for 11% of the time, Pallas kernels for 0%

commit v1 on v0

--- a/solution.py
+++ b/solution.py
@@ -1,8 +1,11 @@
+import functools
 import math
 
 import jax
 import jax.numpy as jnp
 from jax import lax
+from jax.experimental import pallas as pl
+from jax.experimental.pallas import tpu as pltpu
 from jax.sharding import PartitionSpec as P
 
 HEAD_DIM = 128
@@ -128,7 +131,453 @@
     return (grad_queries, grad_keys, grad_values)
 
 
-def per_device(
+MESH_ID = pl.DeviceIdType.MESH
+BF16 = jnp.bfloat16
+F32 = jnp.float32
+
+
+class Place:
+    def __init__(self, levels):
+        self.levels = levels
+        wide = lax.axis_index("wide")
+        self.core = lax.axis_index("narrow")
+        self.level = wide // 4
+        self.spot = lax.rem(wide, 4)
+        self.across = self.spot + 1 - 2 * lax.rem(self.spot, 2)
+        self.along = lax.rem(self.spot + 2, 4)
+        self.corner = 3 - self.spot
+        self.has_up = self.level < levels - 1
+        self.has_down = self.level > 0
+
+    def device(self, level, spot, core=None):
+        return {"wide": level * 4 + spot, "narrow": self.core if core is None else core}
+
+    def enter(self, sibling):
+        barrier = pltpu.get_barrier_semaphore()
+
+        def greet(device):
+            pl.semaphore_signal(barrier, inc=1, device_id=device, device_id_type=MESH_ID)
+
+        greet(self.device(self.level, self.across))
+        greet(self.device(self.level, self.along))
+        if sibling:
+            greet(self.device(self.level, self.spot, 1 - self.core))
+
+        @pl.when(self.has_up)
+        def _():
+            greet(self.device(self.level + 1, self.spot))
+
+        @pl.when(self.has_down)
+        def _():
+            greet(self.device(self.level - 1, self.spot))
+
+        both = jnp.where(self.has_up, 1, 0) + jnp.where(self.has_down, 1, 0)
+        pl.semaphore_wait(barrier, both + (3 if sibling else 2))
+
+
+def remote(src, dst, send, recv, device):
+    return pltpu.make_async_remote_copy(
+        src_ref=src,
+        dst_ref=dst,
+        send_sem=send,
+        recv_sem=recv,
+        device_id=device,
+        device_id_type=MESH_ID,
+    )
+
+
+def gather_kernel(levels, sibling, x_ref, out_ref, own_sem, *sems):
+    send_up, send_dn, send_x, send_y, send_cx, send_cy, send_n = sems[:7]
+    recv_z, recv_x, recv_y, recv_cx, recv_cy, recv_n = sems[7:]
+    at = Place(levels)
+    level, spot, core = at.level, at.spot, at.core
+    across, along, corner = at.across, at.along, at.corner
+    half = x_ref.shape[0] // 2
+    first, second = pl.ds(0, half), pl.ds(half, half)
+    at.enter(sibling)
+
+    def block(lev, sp, co=None):
+        if sibling:
+            return out_ref.at[(lev * 4 + sp) * 2 + (core if co is None else co)]
+        return out_ref.at[lev * 4 + sp]
+
+    own = pltpu.make_async_copy(x_ref, block(level, spot), own_sem)
+    own.start()
+
+    def go_up(lev, src=None):
+        dst = block(lev, spot)
+        src = dst if src is None else src
+        return remote(src, dst, send_up.at[lev], recv_z.at[lev], at.device(level + 1, spot))
+
+    def go_down(lev, src=None):
+        dst = block(lev, spot)
+        src = dst if src is None else src
+        return remote(src, dst, send_dn.at[lev], recv_z.at[lev], at.device(level - 1, spot))
+
+    def go_x(lev, sp, src=None):
+        dst = block(lev, sp)
+        src = dst if src is None else src
+        return remote(src, dst, send_x.at[lev], recv_x.at[lev], at.device(level, across))
+
+    def go_y(lev, sp, src=None):
+        dst = block(lev, sp)
+        src = dst if src is None else src
+        return remote(src, dst, send_y.at[lev], recv_y.at[lev], at.device(level, along))
+
+    def corner_y(lev, sp):
+        ref = block(lev, sp).at[first]
+        return remote(ref, ref, send_cy.at[lev], recv_cy.at[lev], at.device(level, along))
+
+    def corner_x(lev, sp):
+        ref = block(lev, sp).at[second]
+        return remote(ref, ref, send_cx.at[lev], recv_cx.at[lev], at.device(level, across))
+
+    def to_sibling(lev, sp, src=None):
+        dst = block(lev, sp)
+        src = dst if src is None else src
+        sems = send_n.at[lev * 4 + sp], recv_n.at[lev * 4 + sp]
+        return remote(src, dst, *sems, at.device(level, spot, 1 - core))
+
+    def from_sibling(lev, sp):
+        ref = block(lev, sp, 1 - core)
+        sems = send_n.at[lev * 4 + sp], recv_n.at[lev * 4 + sp]
+        return remote(ref, ref, *sems, at.device(level, spot, 1 - core))
+
+    @pl.when(at.has_up)
+    def _():
+        go_up(level, x_ref).start()
+
+    @pl.when(at.has_down)
+    def _():
+        go_down(level, x_ref).start()
+
+    go_x(level, spot, x_ref).start()
+    go_y(level, spot, x_ref).start()
+    if sibling:
+        to_sibling(level, spot, x_ref).start()
+
+    def when(cond, run):
+        if cond is None:
+            run()
+        else:
+            pl.when(cond)(run)
+
+    def at_distance(s):
+        if s == 0:
+            return [(level, None)]
+        return [(level - s, level - s >= 0), (level + s, level + s < levels)]
+
+    def column(s):
+        for sign, (lev, cond) in zip((-1, 1), at_distance(s)):
+
+            def run(lev=lev, sign=sign):
+                go_up(lev).wait_recv()
+                if sign < 0:
+                    pl.when(at.has_up)(lambda: go_up(lev).start())
+                else:
+                    pl.when(at.has_down)(lambda: go_down(lev).start())
+                go_x(lev, spot).start()
+                go_y(lev, spot).start()
+                if sibling:
+                    to_sibling(lev, spot).start()
+
+            when(cond, run)
+
+    def square(s):
+        for lev, cond in at_distance(s):
+
+            def run(lev=lev):
+                go_x(lev, across).wait_recv()
+                corner_y(lev, across).start()
+                if sibling:
+                    to_sibling(lev, across).start()
+                go_y(lev, along).wait_recv()
+                corner_x(lev, along).start()
+                if sibling:
+                    to_sibling(lev, along).start()
+
+            when(cond, run)
+
+    def corners(s):
+        for lev, cond in at_distance(s):
+
+            def run(lev=lev):
+                corner_y(lev, corner).wait_recv()
+                corner_x(lev, corner).wait_recv()
+                if sibling:
+                    to_sibling(lev, corner).start()
+
+            when(cond, run)
+
+    for s in range(1, levels + 2):
+        if s < levels:
+            column(s)
+        if s - 1 < levels:
+            square(s - 1)
+        if s >= 2:
+            corners(s - 2)
+    own.wait()
+    for lev in range(levels):
+
+        @pl.when(at.has_up & (lev <= level))
+        def _():
+            go_up(lev).wait_send()
+
+        @pl.when(at.has_down & (lev >= level))
+        def _():
+            go_down(lev).wait_send()
+
+        go_x(lev, spot).wait_send()
+        go_y(lev, spot).wait_send()
+        corner_y(lev, across).wait_send()
+        corner_x(lev, along).wait_send()
+        if sibling:
+            for sp in range(4):
+                to_sibling(lev, sp).wait_send()
+                from_sibling(lev, sp).wait_recv()
+
+
+def gather_wide(x, levels, sibling, collective_id):
+    dma = pltpu.SemaphoreType.DMA
+    blocks = levels * 4
+    anywhere = pl.BlockSpec(memory_space=pl.ANY)
+    return pl.pallas_call(
+        functools.partial(gather_kernel, levels, sibling),
+        out_shape=jax.ShapeDtypeStruct((blocks * (2 if sibling else 1), *x.shape), x.dtype),
+        in_specs=[anywhere],
+        out_specs=anywhere,
+        scratch_shapes=[dma]
+        + [dma((levels,))] * 6
+        + [dma((blocks,))]
+        + [dma((levels,))] * 5
+        + [dma((blocks,))],
+        compiler_params=pltpu.CompilerParams(
+            collective_id=collective_id, has_side_effects=True
+        ),
+    )(x)
+
+
+def destinations(levels):
+    return [
+        sorted(range(levels), key=lambda to: (-abs(to - here), -to)) for here in range(levels)
+    ]
+
+
+def add_rows(write, sources, rows):
+    step = 16
+
+    def body(k, carry):
+        r = pl.ds(pl.multiple_of(k * step, step), step)
+        total = sources[0](r)
+        for source in sources[1:]:
+            total = total + source(r)
+        write(r, total)
+        return carry
+
+    lax.fori_loop(0, rows // step, body, 0)
+
+
+def reads(ref):
+    return lambda r: ref[r, :].astype(F32)
+
+
+def writes(ref):
+    def write(r, total):
+        ref[r, :] = total.astype(ref.dtype)
+
+    return write
+
+
+def scatter_kernel(levels, sibling, x_ref, out_ref, acc, near, hx, hy, fx, fy, out_buf, za, zb, *sems):
+    send_n, recv_n = sems[:2]
+    send_hx, send_hy, send_fx, send_fy, send_up, send_dn = sems[2:8]
+    recv_hx, recv_hy, recv_fx, recv_fy, recv_za, recv_zb = sems[8:]
+    at = Place(levels)
+    level, spot, core = at.level, at.spot, at.core
+    across, along, corner = at.across, at.along, at.corner
+    rows = out_ref.shape[0]
+    half = rows // 2
+    first, second = pl.ds(0, half), pl.ds(half, half)
+    at.enter(sibling)
+    table = destinations(levels)
+
+    def destination(s):
+        lev = jnp.int32(table[0][s])
+        for k in range(1, levels):
+            lev = jnp.where(level == k, table[k][s], lev)
+        return lev
+
+    order = [destination(s) for s in range(levels)]
+
+    def to_sibling(lev, sp):
+        b = lev * 4 + sp
+        src = x_ref.at[b * 2 + 1 - core]
+        return remote(
+            src, near.at[b], send_n.at[b], recv_n.at[b], at.device(level, spot, 1 - core)
+        )
+
+    def half_y(lev):
+        src = acc.at[lev * 4 + corner].at[first]
+        return remote(
+            src, hy.at[lev], send_hy.at[lev], recv_hy.at[lev], at.device(level, along)
+        )
+
+    def half_x(lev):
+        src = acc.at[lev * 4 + corner].at[second]
+        return remote(
+            src, hx.at[lev], send_hx.at[lev], recv_hx.at[lev], at.device(level, across)
+        )
+
+    def full_x(lev):
+        src = acc.at[lev * 4 + across]
+        return remote(
+            src, fx.at[lev], send_fx.at[lev], recv_fx.at[lev], at.device(level, across)
+        )
+
+    def full_y(lev):
+        src = acc.at[lev * 4 + along]
+        return remote(
+            src, fy.at[lev], send_fy.at[lev], recv_fy.at[lev], at.device(level, along)
+        )
+
+    def go_up(lev):
+        sems = send_up.at[lev], recv_zb.at[lev]
+        return remote(out_buf.at[lev], zb.at[lev], *sems, at.device(level + 1, spot))
+
+    def go_down(lev):
+        sems = send_dn.at[lev], recv_za.at[lev]
+        return remote(out_buf.at[lev], za.at[lev], *sems, at.device(level - 1, spot))
+
+    if sibling:
+        for lev in order:
+            for sp in (corner, across, along, spot):
+                to_sibling(lev, sp).start()
+
+    def local(lev):
+        for n, sp in enumerate((corner, across, along, spot)):
+            b = lev * 4 + sp
+            if sibling:
+                to_sibling(lev, sp).wait_recv()
+                add_rows(writes(acc.at[b]), [reads(x_ref.at[b * 2 + core]), reads(near.at[b])], rows)
+            else:
+                add_rows(writes(acc.at[b]), [reads(x_ref.at[b])], rows)
+            if n == 0:
+                half_y(lev).start()
+                half_x(lev).start()
+
+    def halves(lev):
+        half_y(lev).wait_recv()
+        ref = acc.at[lev * 4 + across].at[first]
+        add_rows(writes(ref), [reads(ref), reads(hy.at[lev])], half)
+        full_x(lev).start()
+        half_x(lev).wait_recv()
+        ref = acc.at[lev * 4 + along].at[second]
+        add_rows(writes(ref), [reads(ref), reads(hx.at[lev])], half)
+        full_y(lev).start()
+
+    def column(lev):
+        full_x(lev).wait_recv()
+        full_y(lev).wait_recv()
+        own = [reads(acc.at[lev * 4 + spot]), reads(fx.at[lev]), reads(fy.at[lev])]
+        above, below = reads(za.at[lev]), reads(zb.at[lev])
+
+        @pl.when(lev < level)
+        def _():
+            @pl.when(at.has_up)
+            def _():
+                go_down(lev).wait_recv()
+                add_rows(writes(out_buf.at[lev]), [*own, above], rows)
+
+            @pl.when(jnp.logical_not(at.has_up))
+            def _():
+                add_rows(writes(out_buf.at[lev]), own, rows)
+
+            go_down(lev).start()
+
+        @pl.when(lev > level)
+        def _():
+            @pl.when(at.has_down)
+            def _():
+                go_up(lev).wait_recv()
+                add_rows(writes(out_buf.at[lev]), [*own, below], rows)
+
+            @pl.when(jnp.logical_not(at.has_down))
+            def _():
+                add_rows(writes(out_buf.at[lev]), own, rows)
+
+            go_up(lev).start()
+
+        @pl.when(lev == level)
+        def _():
+            pl.when(at.has_up)(lambda: go_down(lev).wait_recv())
+            pl.when(at.has_down)(lambda: go_up(lev).wait_recv())
+
+            @pl.when(at.has_up & at.has_down)
+            def _():
+                add_rows(writes(out_ref), [*own, above, below], rows)
+
+            @pl.when(jnp.logical_not(at.has_down))
+            def _():
+                add_rows(writes(out_ref), [*own, above], rows)
+
+            @pl.when(jnp.logical_not(at.has_up))
+            def _():
+                add_rows(writes(out_ref), [*own, below], rows)
+
+    for s in range(levels + 2):
+        if s < levels:
+            local(order[s])
+        if 0 <= s - 1 < levels:
+            halves(order[s - 1])
+        if s >= 2:
+            column(order[s - 2])
+    for lev in range(levels):
+        if sibling:
+            for sp in range(4):
+                to_sibling(lev, sp).wait_send()
+        half_y(lev).wait_send()
+        half_x(lev).wait_send()
+        full_x(lev).wait_send()
+        full_y(lev).wait_send()
+
+        @pl.when(lev < level)
+        def _():
+            go_down(lev).wait_send()
+
+        @pl.when(lev > level)
+        def _():
+            go_up(lev).wait_send()
+
+
+def scatter_wide(x, levels, sibling, collective_id):
+    dma = pltpu.SemaphoreType.DMA
+    blocks = levels * 4
+    rows, width = x.shape[1:]
+    vmem = pltpu.VMEM
+    inside = pl.BlockSpec(memory_space=vmem)
+    return pl.pallas_call(
+        functools.partial(scatter_kernel, levels, sibling),
+        out_shape=jax.ShapeDtypeStruct((rows, width), BF16),
+        in_specs=[inside],
+        out_specs=inside,
+        scratch_shapes=[
+            vmem((blocks, rows, width), BF16),
+            vmem((blocks if sibling else 1, rows, width), BF16),
+            vmem((levels, rows // 2, width), BF16),
+            vmem((levels, rows // 2, width), BF16),
+        ]
+        + [vmem((levels, rows, width), BF16)] * 5
+        + [dma((blocks,))] * 2
+        + [dma((levels,))] * 12,
+        compiler_params=pltpu.CompilerParams(
+            collective_id=collective_id,
+            has_side_effects=True,
+            vmem_limit_bytes=60 * 1024 * 1024,
+        ),
+    )(x)
+
+
+def slots_path(
     tokens,
     cotangent,
     lengths,
@@ -463,6 +912,255 @@
     )
 
 
+def tokens_path(
+    tokens,
+    cotangent,
+    lengths,
+    routes,
+    keep,
+    attn_gain,
+    w_query,
+    w_key,
+    w_value,
+    w_out,
+    ffn_gain,
+    w_router,
+    shared_gate,
+    shared_up,
+    shared_down,
+    expert_gate,
+    expert_up,
+    expert_down,
+):
+    core = lax.axis_index("narrow")
+    place = lax.axis_index("wide")
+    wide_size = lax.axis_size("wide")
+    levels = wide_size // 4
+    local_rows, width = tokens.shape
+    row_length = 2 * local_rows
+    part = width // 2
+    heads = part // HEAD_DIM
+    hidden_part = expert_gate.shape[2]
+    slice_width = shared_gate.shape[1] // (2 * wide_size)
+    experts = w_router.shape[1]
+
+    def swap(value):
+        return lax.ppermute(value, "narrow", [(0, 1), (1, 0)])
+
+    def other_rows(value):
+        return jnp.concatenate([value[local_rows:], value[:local_rows]], axis=0)
+
+    def in_order(mine, theirs, axis):
+        return jnp.where(
+            core == 0,
+            jnp.concatenate([mine, theirs], axis=axis),
+            jnp.concatenate([theirs, mine], axis=axis),
+        )
+
+    def columns(value, which, size):
+        return lax.dynamic_slice_in_dim(value, which * size, size, axis=1)
+
+    picks = (routes[:, :, None] == jnp.arange(experts, dtype=jnp.int32)[None, None, :]).astype(
+        jnp.int32
+    )
+    marks = jnp.sum(picks * (1 + keep)[:, :, None], axis=1).astype(BF16)
+    all_marks = lax.all_gather(marks, ("wide", "narrow"), axis=0, tiled=True).astype(F32)
+    all_grads = gather_wide(cotangent, levels, True, 0).reshape(-1, width)
+
+    first_unit = place * slice_width
+    stored = shared_gate.shape[1] // 2
+    gate_mine = lax.dynamic_slice_in_dim(shared_gate, core * stored + first_unit, slice_width, 1)
+    up_mine = lax.dynamic_slice_in_dim(shared_up, core * stored + first_unit, slice_width, 1)
+    gate_send = lax.dynamic_slice_in_dim(
+        shared_gate, (1 - core) * stored + first_unit, slice_width, 1
+    )
+    up_send = lax.dynamic_slice_in_dim(shared_up, (1 - core) * stored + first_unit, slice_width, 1)
+    down_slice = lax.dynamic_slice_in_dim(shared_down, first_unit, slice_width, 0)
+    gains = jnp.stack([attn_gain, ffn_gain])
+    sent = swap(jnp.concatenate([gate_send, up_send, w_router], axis=1))
+    gains = in_order(gains, swap(gains), 1).astype(F32)
+    attn_scale, ffn_scale = gains[0], gains[1]
+    dense = in_order(jnp.concatenate([gate_mine, up_mine, w_router], axis=1), sent, 0)
+    gate_slice = dense[:, :slice_width]
+    up_slice = dense[:, slice_width : 2 * slice_width]
+    router = dense[:, 2 * slice_width :]
+
+    row_tokens = jnp.concatenate([tokens, swap(tokens)], axis=0).astype(F32)
+    normed, unit_one, scale_one = norm_forward(row_tokens, attn_scale)
+    normed_one = columns(normed.astype(BF16), core, part)
+    projections = [w_query, w_key, w_value]
+    keep_side = jnp.concatenate([columns(w, core, part) for w in projections], axis=1)
+    send_side = jnp.concatenate([columns(w, 1 - core, part) for w in projections], axis=1)
+    arrived = swap(matmul(normed_one, send_side).astype(BF16))
+    qkv = matmul(normed_one, keep_side) + other_rows(arrived).astype(F32)
+    index = jnp.arange(local_rows, dtype=jnp.int32)
+    index = jnp.concatenate([core * local_rows + index, (1 - core) * local_rows + index])
+    docs, positions = doc_layout(index, lengths[0])
+    allowed = (docs[:, None] == docs[None, :]) & (index[None, :] <= index[:, None])
+    cosine, sine_table = rotary_angles(positions)
+    head_shape = (row_length, heads, HEAD_DIM)
+    query_rows = rotate(qkv[:, :part].reshape(head_shape), cosine, sine_table)
+    query_rows = (query_rows * HEAD_DIM ** (-0.5)).astype(BF16)
+    key_rows = rotate(qkv[:, part : 2 * part].reshape(head_shape), cosine, sine_table).astype(BF16)
+    value_rows = qkv[:, 2 * part :].astype(BF16).reshape(head_shape)
+    attended, logsum = attend_block(query_rows, key_rows, value_rows, allowed)
+    attended = attended.reshape(row_length, part)
+    branch = matmul(attended, w_out)
+    arrived = swap(branch[local_rows:].astype(BF16))
+    inputs = row_tokens[:local_rows]
+    hidden = inputs + branch[:local_rows] + arrived.astype(F32)
+    normed, unit_two, scale_two = norm_forward(hidden, ffn_scale)
+    normed_two = normed.astype(BF16)
+    all_rows = gather_wide(normed_two, levels, True, 1).reshape(-1, width)
+
+    used = hidden_part + slice_width
+    full = -(-(used + experts) // 128) * 128
+
+    def pad(value, size, axis):
+        extra = list(value.shape)
+        extra[axis] = size - value.shape[axis]
+        return jnp.concatenate([value, jnp.zeros(extra, value.dtype)], axis=axis)
+
+    gate_all = pad(jnp.concatenate([expert_gate[0], gate_slice, router], axis=1), full, 1)
+    up_all = pad(jnp.concatenate([expert_up[0], up_slice], axis=1), full, 1)
+    down_all = pad(jnp.concatenate([expert_down[0], down_slice], axis=0), full, 0)
+    gate_vals = matmul(all_rows, gate_all)
+    upper = matmul(all_rows, up_all)
+    back = matmul_right(all_grads, down_all)
+    logits = gate_vals[:, used : used + experts]
+    routed = all_marks > 0.0
+    masked = jnp.where(routed, logits, MASKED)
+    weights = jnp.where(routed, jnp.exp(masked - jnp.max(masked, axis=1, keepdims=True)), 0.0)
+    gates = weights / jnp.sum(weights, axis=1, keepdims=True)
+    mix_all = gates * (all_marks > 1.5)
+    mix = jnp.sum(
+        jnp.where(jnp.arange(experts)[None, :] == place, mix_all, 0.0), axis=1, keepdims=True
+    )
+    unit = jnp.arange(full)[None, :]
+    scale = jnp.where(unit < hidden_part, mix, jnp.where(unit < used, 1.0, 0.0))
+    act_vals, slope_vals = silu_parts(gate_vals)
+    active = act_vals * upper
+    grad_act = scale * back
+    grad_gate = (grad_act * upper * slope_vals).astype(BF16)
+    grad_upper = (grad_act * act_vals).astype(BF16)
+    mixed = (scale * active).astype(BF16)
+    grad_mix = jnp.sum(jnp.where(unit < hidden_part, active * back, 0.0), axis=1)
+    grad_mix = lax.all_to_all(
+        grad_mix.reshape(wide_size, 2, local_rows), "wide", split_axis=0, concat_axis=0, tiled=True
+    )
+    pick_core = jnp.where(core == 0, grad_mix[:, 0], grad_mix[:, 1])
+    send_core = jnp.where(core == 0, grad_mix[:, 1], grad_mix[:, 0])
+    grad_mix = (pick_core + swap(send_core)).T
+    block_shape = (2 * wide_size, local_rows, width)
+    grad_rows = matmul_right(grad_gate, gate_all) + matmul_right(grad_upper, up_all)
+    grad_rows = scatter_wide(grad_rows.astype(BF16).reshape(block_shape), levels, True, 2)
+    expert_out = scatter_wide(matmul(mixed, down_all).astype(BF16).reshape(block_shape), levels, True, 3)
+    output = (hidden + expert_out.astype(F32)).astype(BF16)
+    grad_gate_all = matmul_left(all_rows, grad_gate)
+    grad_up_all = matmul_left(all_rows, grad_upper)
+    grad_down_all = matmul_left(mixed, all_grads)
+
+    marks = marks.astype(F32)
+    routed = marks > 0.0
+    logits = matmul(normed_two, router)
+    masked = jnp.where(routed, logits, MASKED)
+    weights = jnp.where(routed, jnp.exp(masked - jnp.max(masked, axis=1, keepdims=True)), 0.0)
+    gates = weights / jnp.sum(weights, axis=1, keepdims=True)
+    grad_gates = jnp.where(marks > 1.5, grad_mix, 0.0)
+    grad_logits = gates * (grad_gates - jnp.sum(gates * grad_gates, axis=1, keepdims=True))
+    grad_logits = grad_logits.astype(BF16)
+    grad_router = matmul_left(normed_two, grad_logits)
+    grad_normed = grad_rows.astype(F32) + matmul_right(grad_logits, router)
+    grad_hidden_norm, grad_ffn = norm_backward(grad_normed, unit_two, scale_two, ffn_scale)
+    grad_hidden = cotangent.astype(F32) + grad_hidden_norm
+    grad_branch = grad_hidden.astype(BF16)
+    row_branch = jnp.concatenate([grad_branch, swap(grad_branch)], axis=0)
+
+    grad_w_out = matmul_left(attended, row_branch)
+    grad_attended = matmul_right(row_branch, w_out).astype(BF16).reshape(head_shape)
+    grad_queries, grad_keys, grad_values = attend_back(
+        query_rows, key_rows, value_rows, allowed, logsum, grad_attended
+    )
+    grad_queries = rotate(grad_queries * HEAD_DIM ** (-0.5), cosine, -sine_table)
+    grad_keys = rotate(grad_keys, cosine, -sine_table)
+    mine = jnp.stack([grad_queries, grad_keys, grad_values]).reshape(3, row_length, part)
+    mine = mine.astype(BF16)
+    theirs = swap(mine)
+    theirs = jnp.concatenate([theirs[:, local_rows:], theirs[:, :local_rows]], axis=1)
+    grad_qkv = in_order(mine, theirs, 2)
+    grad_dense = jnp.stack(
+        [matmul_left(normed_one, grad_qkv[k]) for k in range(3)] + [grad_w_out]
+    ).astype(BF16)
+    grad_part = sum(matmul_right(grad_qkv[k], projections[k]) for k in range(3))
+    grad_normed_one = in_order(
+        grad_part[:local_rows], swap(grad_part[local_rows:].astype(BF16)).astype(F32), 1
+    )
+    grad_input_norm, grad_attn = norm_backward(
+        grad_normed_one, unit_one[:local_rows], scale_one[:local_rows], attn_scale
+    )
+    grad_tokens = grad_hidden + grad_input_norm
+
+    small = jnp.concatenate([grad_attn[:, None], grad_ffn[:, None], grad_router], axis=1)
+    small_mine = lax.dynamic_slice_in_dim(small, core * part, part, 0)
+    small_send = lax.dynamic_slice_in_dim(small, (1 - core) * part, part, 0)
+    small = (small_mine + swap(small_send)).astype(BF16)
+    shared_t = jnp.concatenate(
+        [
+            grad_gate_all[:, hidden_part:used].astype(BF16),
+            grad_up_all[:, hidden_part:used].astype(BF16),
+        ],
+        axis=1,
+    )
+    shared_mine = lax.dynamic_slice_in_dim(shared_t, core * part, part, 0)
+    shared_send = lax.dynamic_slice_in_dim(shared_t, (1 - core) * part, part, 0)
+    shared_pair = in_order(shared_mine[None], swap(shared_send)[None], 0)
+    shared_down_grad = grad_down_all[hidden_part:used].astype(BF16)
+    flat = jnp.concatenate(
+        [shared_pair.reshape(-1), shared_down_grad.reshape(-1), small.reshape(-1)]
+    )
+    unit_rows = 32
+    extra_rows = -(-flat.shape[0] // (width * unit_rows)) * unit_rows
+    flat = jnp.concatenate([flat, jnp.zeros((extra_rows * width - flat.shape[0],), BF16)])
+    sum_rows = 4 * part // wide_size
+    summed = scatter_wide(grad_dense.reshape(wide_size, sum_rows, width), levels, False, 4)
+    everything = gather_wide(
+        jnp.concatenate([summed, flat.reshape(extra_rows, width)], axis=0), levels, False, 5
+    ).astype(F32)
+    owned = everything[:, :sum_rows].reshape(4, part, width)
+    flat = everything[:, sum_rows:].reshape(wide_size, -1)
+    size = 2 * part * 2 * slice_width
+    pair = flat[:, :size].reshape(wide_size, 2, part, 2, slice_width)
+    pair = pair.transpose(3, 2, 1, 0, 4).reshape(2, part, 2 * wide_size * slice_width)
+    down_size = slice_width * width
+    own_down = flat[:, size : size + down_size].reshape(wide_size * slice_width, width)
+    small = jnp.sum(flat[:, size + down_size : size + down_size + small.size], axis=0)
+    small = small.reshape(part, 2 + experts)
+    return (
+        output,
+        grad_tokens,
+        small[:, 0],
+        owned[0],
+        owned[1],
+        owned[2],
+        owned[3],
+        small[:, 1],
+        small[:, 2:],
+        pair[0],
+        pair[1],
+        own_down,
+        grad_gate_all[None, :, :hidden_part],
+        grad_up_all[None, :, :hidden_part],
+        grad_down_all[None, :hidden_part],
+    )
+
+
+def per_device(*arrays):
+    tokens = arrays[0]
+    gathered = lax.axis_size("wide") * lax.axis_size("narrow") * tokens.size * 2
+    fits = gathered <= 12 * 1024 * 1024
+    return (tokens_path if fits else slots_path)(*arrays)
+
+
 def solution(mesh):
     in_specs = (
         P(("wide", "narrow"), None),

time: 1530 us -> 791 us (0.52)
  blocking collectives: 1010 us -> 40.6 us
  Pallas kernels: 0 us -> 364 us
  waiting for transfers between devices: 203 us -> 0.47 us
  local copies, waits for them, and re-layouts: 85.3 us -> 210 us
  starting transfers between devices: 27.1 us -> 7.76 us
  other arithmetic: 51.6 us -> 35.8 us
    psum x1 -> x0, blocking collectives: 823 us -> none  [per_device(): lax.psum((halves[0], halves[1], halves[2], halves[3], halves[4], halves[5...]
    pallas_call x0 -> x6, Pallas kernels: none -> 364 us  [the longest x3 188 us: gather_wide(): pl.pallas_call(functools.partial(gather_kernel, levels, sibling), out_sha...]
    all_to_all x2 -> x0, blocking collectives: 173 us -> none  [the longest x1 88.4 us: per_device(): lax.all_to_all(fill_slots(normed_two, pair_index // TOPK), 'wide', split_...]
    slice x1 -> x28, local copies, waits for them, and re-layouts: 0.29 us -> 94.1 us  [the longest x2 44.1 us: tokens_path(): pair[1]]
    reduce_scatter x9 -> x0, waiting for transfers between devices: 86.8 us -> none  [the longest x1 15.5 us: per_device(): lax.psum_scatter(grad_query_proj.astype(jnp.bfloat16), 'narrow', scatter_...]
    all_to_all x2 -> x1, waiting for transfers between devices: 75.1 us -> 0.01 us  [tokens_path(): lax.all_to_all(grad_mix.reshape(wide_size, 2, local_rows), 'wide', split_...]
    reshape x2 -> x6, local copies, waits for them, and re-layouts: 10.8 us -> 51.1 us  [the longest x1 46.2 us: tokens_path(): pair = flat[:, :size].reshape(wide_size, 2, part, 2, slice_width)]
    gather x4 -> x0, local copies, waits for them, and re-layouts: 34.7 us -> none  [the longest x2 17 us: fill_slots(): taken = jnp.take(in_rows, row_index, axis=0)]
  transfers between devices with their start and end apart: 23 -> 12, of which waited for: 15 -> 2; matrix products, arithmetic and copies ran while one was open for 11% -> 13% of each run, Pallas kernels for 0% -> 29%
where the time goes in v1:
time: 791 us; the launch traced here: 784 us
  Pallas kernels  364 us (46%)
  local copies, waits for them, and re-layouts  210 us (27%)
  matrix products  123 us (16%)
  blocking collectives  40.6 us (5%)
  other arithmetic  35.8 us (5%)
    pallas_call x3, Pallas kernels, gather_wide(): pl.pallas_call(functools.partial(gather_kernel, levels, sibling), out_sha...  188 us
    pallas_call x3, Pallas kernels, scatter_wide(): pl.pallas_call(functools.partial(scatter_kernel, levels, sibling), out_sh...  175 us
    reshape x1, local copies, waits for them, and re-layouts, tokens_path(): pair = flat[:, :size].reshape(wide_size, 2, part, 2, slice_width)  46.2 us
    dot_general x7, matrix products, matmul(): return jnp.dot(left, right, preferred_element_type=jnp.float32)  44.3 us
    slice x2, local copies, waits for them, and re-layouts, tokens_path(): pair[1]  44.1 us
    dot_general x8, matrix products, matmul_right(): lax.dot_general(left, right, (((1,), (1,)), ((), ())), preferred_element_...  43.1 us
    all_gather x1, blocking collectives, tokens_path(): lax.all_gather(marks, ('wide', 'narrow'), axis=0, tiled=True).astype(F32)  40.6 us
    unnamed x200, local copies, waits for them, and re-layouts  32.4 us
  transfers between devices with their start and end apart: 12, of which 2 were waited for; matrix products, arithmetic and copies ran while one was open for 13% of the time, Pallas kernels for 29%

profile of v1, /device:TPU:0, one launch (start us, length us, event | category | flops | bytes accessed | tf_op | source)
XLA Modules:
  0.0 784.2 jit_solution(6864924242102857502)
XLA Ops:
  12.9 52.4 %shard_map.291 = bf16[32,128,1280]{2,1,0:T(8,128)(2,1)} custom-call(bf16[128,1280]{1,0:T(8,128)(2,1)} %x_ref.1), custom_call_target="tpu_custom_call" | custom-call | tf_op jit(solution)/shard_map/pallas_call | solution.py:344
  70.9 12.4 %fusion.22 = f32[512,4096]{1,0:T(8,128)} fusion(bf16[4096,1280]{1,0:T(8,128)(2,1)} %bitcast.133, bf16[28,1280]{1,0:T(8,128)(2,1)S(1)} %constant_dynamic-slice_fusion.1, bf16[448,1280]{1,0:T(8,128)(2,1)S(1)} %bitcast.168, bf16[512]{0:T(512)(128)(2,1)S(1)} %pad.47.clone), kind=kOutput, calls=%fused_computation.62 | convolution fusion | flops 5372641280 | bytes 20093952 | tf_op jit(solution)/shard_map/dot_general | solution.py:30
  83.4 40.6 %all_gather.3 = bf16[4096,16]{0,1:T(8,128)(2,1)S(1)} all-gather(bf16[128,16]{0,1:T(8,128)(2,1)S(1)} %get-tuple-element.88), channel_id=1, replica_groups=mesh['wide'=16,'narrow'=2] {'wide','narrow'}, dimensions={0}, use_global_device_ids=true | all-gather | bytes 135168 | tf_op jit(solution)/shard_map/all_gather | solution.py:967
  159.6 48.0 %shard_map.289 = bf16[32,128,1280]{2,1,0:T(8,128)(2,1)} custom-call(bf16[128,1280]{1,0:T(8,128)(2,1)} %multiply_convert_fusion.3.x_ref), custom_call_target="tpu_custom_call" | custom-call | tf_op jit(solution)/shard_map/pallas_call | solution.py:344
  207.7 9.0 %fusion.61 = f32[4096,512]{0,1:T(8,128)S(1)} fusion(bf16[4096,1280]{1,0:T(8,128)(2,1)} %bitcast.136, bf16[1280,16]{0,1:T(8,128)(2,1)S(1)} %copy-done.60, bf16[1280,28]{0,1:T(8,128)(2,1)S(1)} %copy-done.55, bf16[1280,448]{0,1:T(8,128)(2,1)} %bitcast.170, bf16[512]{0:T(512)(128)(2,1)S(1)} %copy-done.80), kind=kOutput, calls=%fused_computation.197 | convolution fusion | flops 5373952000 | bytes 20134912 | tf_op jit(solution)/shard_map/dot_general | solution.py:20
  220.0 23.1 %multiply_convert_fusion.1 = (bf16[4096,512]{0,1:T(8,128)(2,1)}, f32[4096]{0:T(1024)}, bf16[4096,512]{0,1:T(8,128)(2,1)}, bf16[4096,512]{0,1:T(8,128)(2,1)}) fusion(f32[4096,512]{0,1:T(8,128)} %copy-done.58, f32[512,4096]{1,0:T(8,128)} %fusion.22, f32[512]{0:T(512)S(1)} %copy-done.76, f32[4096]{0:T(1024)S(1)} %select_reduce_fusion, ...), kind=kOutput, calls=%fused_computation.9 | convolution fusion | flops 5416677376 | bytes 41100800 | tf_op jit(solution)/shard_map/dot_general | solution.py:20
  243.2 11.6 %fusion.76 = f32[512,1280]{1,0:T(8,128)} fusion(bf16[4096,512]{0,1:T(8,128)(2,1)} %get-tuple-element.96, bf16[4096,1280]{1,0:T(8,128)(2,1)} %bitcast.134), kind=kOutput, calls=%fused_computation.211 | convolution fusion | flops 5368709120 | bytes 17301504 | tf_op jit(solution)/shard_map/dot_general | solution.py:24
  254.8 8.5 %convolution_convert_fusion = bf16[4096,1280]{1,0:T(8,128)(2,1)} fusion(bf16[4096,512]{0,1:T(8,128)(2,1)S(1)} %copy-done.90, bf16[28,1280]{1,0:T(8,128)(2,1)S(1)} %copy-done.57, bf16[448,1280]{1,0:T(8,128)(2,1)S(1)} %bitcast.169, bf16[512]{0:T(512)(128)(2,1)S(1)} %copy-done.78), kind=kOutput, calls=%fused_computation.1 | convolution fusion | flops 5377884160 | bytes 15899648 | tf_op jit(solution)/shard_map/dot_general | solution.py:20
  263.4 7.1 fusion.77
  270.4 10.0 %fusion.60 = f32[4096,1280]{1,0:T(8,128)} fusion(bf16[4096,512]{0,1:T(8,128)(2,1)S(1)} %copy-done.88, bf16[1280,16]{0,1:T(8,128)(2,1)S(1)} %copy-done.60, bf16[1280,28]{0,1:T(8,128)(2,1)S(1)} %copy-done.55, bf16[1280,448]{0,1:T(8,128)(2,1)S(1)} %bitcast.171, bf16[512]{0:T(512)(128)(2,1)S(1)} %copy-done.80), kind=kOutput, calls=%fused_computation.196 | convolution fusion | flops 5373952000 | bytes 26426368 | tf_op jit(solution)/shard_map/dot_general | solution.py:30
  280.4 4.7 all-to-all-start
  288.5 8.4 %fusion.78 = f32[1280,512]{0,1:T(8,128)S(1)} fusion(bf16[4096,512]{0,1:T(8,128)(2,1)S(1)} %copy-done.89, bf16[4096,1280]{1,0:T(8,128)(2,1)} %bitcast.138), kind=kOutput, calls=%fused_computation.213 | convolution fusion | flops 5368709120 | bytes 17301504 | tf_op jit(solution)/shard_map/dot_general | solution.py:24
  299.0 14.8 %add_convert_fusion = bf16[4096,1280]{1,0:T(8,128)(2,1)} fusion(f32[4096,1280]{1,0:T(8,128)} %fusion.60, bf16[4096,512]{0,1:T(8,128)(2,1)} %get-tuple-element.95, bf16[1280,28]{0,1:T(8,128)(2,1)S(1)} %copy-done.54, bf16[1280,448]{0,1:T(8,128)(2,1)S(1)} %bitcast.173, bf16[512]{0:T(512)(128)(2,1)S(1)} %copy-done.79), kind=kOutput, calls=%fused_computation | convolution fusion | flops 5383127040 | bytes 36871168 | tf_op jit(solution)/shard_map/dot_general | solution.py:30
  317.6 56.0 %shard_map.290 = bf16[128,1280]{1,0:T(8,128)(2,1)} custom-call(bf16[32,128,1280]{2,1,0:T(8,128)(2,1)} %bitcast.135), custom_call_target="tpu_custom_call" | custom-call | tf_op jit(solution)/shard_map/pallas_call | solution.py:558
  373.6 55.8 %shard_map.292 = bf16[128,1280]{1,0:T(8,128)(2,1)} custom-call(bf16[32,128,1280]{2,1,0:T(8,128)(2,1)} %bitcast.142), custom_call_target="tpu_custom_call" | custom-call | tf_op jit(solution)/shard_map/pallas_call | solution.py:558
  472.3 63.4 %shard_map.293 = bf16[160,1280]{1,0:T(8,128)(2,1)} custom-call(bf16[16,160,1280]{2,1,0:T(8,128)(2,1)} %bitcast.132), custom_call_target="tpu_custom_call" | custom-call | tf_op jit(solution)/shard_map/pallas_call | solution.py:558
  540.2 88.1 %shard_map.294 = bf16[16,256,1280]{2,1,0:T(8,128)(2,1)} custom-call(bf16[256,1280]{1,0:T(8,128)(2,1)} %pad_maximum_fusion.3.x_ref), custom_call_target="tpu_custom_call" | custom-call | tf_op jit(solution)/shard_map/pallas_call | solution.py:344
  631.2 4.6 copy.212
  643.6 4.8 slice.275
  648.3 8.1 %fusion.65 = (f32[4,160,1280]{2,1,0:T(8,128)}, f32[4,160,1280]{2,1,0:T(8,128)}, f32[4,160,1280]{2,1,0:T(8,128)}, f32[4,160,1280]{2,1,0:T(8,128)}) fusion(bf16[16,256,1280]{2,1,0:T(8,128)(2,1)} %shard_map.294), kind=kLoop, calls=%fused_computation.200 | loop fusion | bytes 26214400 | tf_op jit(solution)/shard_map/slice | solution.py:1145
  660.4 46.2 %reshape.378 = f32[16,2,640,2,28]{4,3,2,1,0:T(2,128)} reshape(f32[16,71680]{1,0:T(8,128)} %slice.275) | data formatting | bytes 9175040 | tf_op jit(solution)/shard_map/reshape | solution.py:1132
  706.6 23.8 %fusion.64 = (f32[1,640,2,16,28]{4,0,1,2,3:T(1,128)}, f32[1,640,2,16,28]{4,0,1,2,3:T(1,128)}) fusion(f32[2,640,2,16,28]{4,0,1,2,3:T(2,128)} %bitcast.127), kind=kLoop, calls=%fused_computation.199 | loop fusion | bytes 9175040 | tf_op jit(solution)/shard_map/slice | solution.py:1149
  730.4 20.3 %copy.188 = f32[1,640,2,16,28]{1,4,3,2,0:T(8,128)} copy(f32[1,640,2,16,28]{4,0,1,2,3:T(1,128)} %get-tuple-element.93) | data formatting | bytes 4587520 | tf_op jit(solution)/shard_map/slice | solution.py:1149
  757.2 20.3 %copy.187 = f32[1,640,2,16,28]{1,4,3,2,0:T(8,128)} copy(f32[1,640,2,16,28]{4,0,1,2,3:T(1,128)} %get-tuple-element.94) | data formatting | bytes 4587520 | tf_op jit(solution)/shard_map/slice | solution.py:1148
  (356 shorter events, 140.0 us)
Async XLA Ops:
  0.6 154.6 %copy-start = (bf16[640,1280]{1,0:T(8,128)(2,1)S(1)}, bf16[640,1280]{1,0:T(8,128)(2,1)}, u32[]{:S(2)}) copy-start(bf16[640,1280]{1,0:T(8,128)(2,1)} %param.27) | copy-start | bytes 4915204
  2.7 122.2 %collective-permute-start.1 = (bf16[2,640]{1,0:T(2,128)(2,1)}, bf16[2,640]{1,0:T(2,128)(2,1)}, u32[]{:S(2)}, u32[]{:S(2)}) collective-permute-start(bf16[2,640]{1,0:T(2,128)(2,1)} %pad_maximum_fusion.14), channel_id=1, source_target_pairs={{0,1},{1,0},{2,3},{3,2},{4,5},{5,4},{6,7},{7,6},{8,9},{9,8},{10,11... | collective-permute-start | bytes 7688 | tf_op jit(solution)/shard_map/ppermute | solution.py:948
  3.2 122.7 %collective-permute-start = (bf16[128,1280]{1,0:T(8,128)(2,1)}, bf16[128,1280]{1,0:T(8,128)(2,1)}, u32[]{:S(2)}, u32[]{:S(2)}) collective-permute-start(bf16[128,1280]{1,0:T(8,128)(2,1)} %param.18), channel_id=1, source_target_pairs={{0,1},{1,0},{2,3},{3,2},{4,5},{5,4},{6,7},{7,6},{8,9},{9,8},{10,11... | collective-permute-start | bytes 983048 | tf_op jit(solution)/shard_map/ppermute | solution.py:948
  7.2 125.0 %collective-permute-start.4 = (bf16[640,72]{0,1:T(8,128)(2,1)}, bf16[640,72]{0,1:T(8,128)(2,1)}, u32[]{:S(2)}, u32[]{:S(2)}) collective-permute-start(bf16[640,72]{0,1:T(8,128)(2,1)} %pad_maximum_fusion.11), channel_id=1, source_target_pairs={{0,1},{1,0},{2,3},{3,2},{4,5},{5,4},{6,7},{7,6},{8,9},{9,8},{10,11... | collective-permute-start | bytes 276488 | tf_op jit(solution)/shard_map/ppermute | solution.py:948
  12.9 70.4 %copy-start.63 = (bf16[128,16]{0,1:T(8,128)(2,1)}, bf16[128,16]{0,1:T(8,128)(2,1)S(1)}, u32[]{:S(2)}) copy-start(bf16[128,16]{0,1:T(8,128)(2,1)S(1)} %get-tuple-element.88) | copy-start | bytes 12292
  130.5 4.2 collective-permute-start.2
  156.0 1.7 collective-permute-start.3
  280.4 34.4 %all-to-all-start = ((f32[16,2,128]{2,1,0:T(2,128)}), f32[16,2,128]{2,1,0:T(2,128)S(1)}, u32[]{:S(2)}, u32[]{:S(2)}) async-start(f32[16,2,128]{2,1,0:T(2,128)} %bitcast.16), calls=%async_computation | async-start | bytes 32768 | tf_op jit(solution)/shard_map/all_to_all | solution.py:1048
  298.8 156.8 %collective-permute-start.9 = (bf16[640,56]{0,1:T(8,128)(2,1)}, bf16[640,56]{0,1:T(8,128)(2,1)}, u32[]{:S(2)}, u32[]{:S(2)}) collective-permute-start(bf16[640,56]{0,1:T(8,128)(2,1)} %get-tuple-element.138), channel_id=1, source_target_pairs={{0,1},{1,0},{2,3},{3,2},{4,5},{5,4},{6,7},{7,6},{8,9},{9,8},{10,11... | collective-permute-start | bytes 215048 | tf_op jit(solution)/shard_map/ppermute | solution.py:948
  314.8 58.7 %copy-start.70 = (f32[128]{0:T(128)}, f32[128]{0:T(128)S(1)}, u32[]{:S(2)}) copy-start(f32[128]{0:T(128)S(1)} %get-tuple-element.146) | copy-start | bytes 1540
  314.9 114.5 %collective-permute-start.5 = (f32[16,128]{1,0:T(8,128)S(1)}, f32[16,128]{1,0:T(8,128)}, u32[]{:S(2)}, u32[]{:S(2)}) collective-permute-start(f32[16,128]{1,0:T(8,128)S(1)} %select_bitcast_fusion), channel_id=1, source_target_pairs={{0,1},{1,0},{2,3},{3,2},{4,5},{5,4},{6,7},{7,6},{8,9},{9,8},{10,11... | collective-permute-start | bytes 24584 | tf_op jit(solution)/shard_map/ppermute | solution.py:948
  373.6 55.9 %copy-start.64 = (bf16[128,16]{0,1:T(8,128)(2,1)S(1)}, bf16[128,16]{0,1:T(8,128)(2,1)}, u32[]{:S(2)}) copy-start(bf16[128,16]{0,1:T(8,128)(2,1)} %copy-done.63) | copy-start | bytes 12292
  373.6 55.9 %copy-start.71 = (f32[128]{0:T(128)S(1)}, f32[128]{0:T(128)}, u32[]{:S(2)}) copy-start(f32[128]{0:T(128)} %copy-done.70) | copy-start | bytes 1540
  373.6 56.8 %copy-start.68 = (f32[128]{0:T(128)S(1)}, f32[128]{0:T(128)}, u32[]{:S(2)}) copy-start(f32[128]{0:T(128)} %copy-done.67) | copy-start | bytes 1540
  373.6 59.8 %copy-start.25 = (bf16[128,1280]{1,0:T(8,128)(2,1)S(1)}, bf16[128,1280]{1,0:T(8,128)(2,1)}, u32[]{:S(2)}) copy-start(bf16[128,1280]{1,0:T(8,128)(2,1)} %x_ref.1) | copy-start | bytes 983044
  434.8 1.7 collective-permute-start.6
  451.8 7.3 collective-permute-start.7
  468.8 67.0 %collective-permute-start.8 = (bf16[128,640]{1,0:T(8,128)(2,1)S(1)}, bf16[128,640]{1,0:T(8,128)(2,1)S(1)}, u32[]{:S(2)}, u32[]{:S(2)}) collective-permute-start(bf16[128,640]{1,0:T(8,128)(2,1)S(1)} %slice.335), channel_id=1, source_target_pairs={{0,1},{1,0},{2,3},{3,2},{4,5},{5,4},{6,7},{7,6},{8,9},{9,8},{10,11... | collective-permute-start | bytes 491528 | tf_op jit(solution)/shard_map/ppermute | solution.py:948
  472.2 63.6 %copy-start.5 = (f32[256,1280]{1,0:T(8,128)S(1)}, f32[256,1280]{1,0:T(8,128)}, u32[]{:S(2)}) copy-start(f32[256,1280]{1,0:T(8,128)} %copy-done.4) | copy-start | bytes 3932164
  472.2 63.6 %copy-start.51 = (f32[1280]{0:T(1024)S(1)}, f32[1280]{0:T(1024)}, u32[]{:S(2)}) copy-start(f32[1280]{0:T(1024)} %copy-done.50) | copy-start | bytes 15364
  472.3 64.0 %copy-start.69 = (f32[128]{0:T(128)S(1)}, f32[128]{0:T(128)}, u32[]{:S(2)}) copy-start(f32[128]{0:T(128)} %copy-done.67) | copy-start | bytes 1540
  472.3 64.0 %slice-start.3 = ((f32[256]{0:T(256)}), f32[128]{0:T(128)S(1)}, s32[]{:S(2)}) async-start(f32[256]{0:T(256)} %copy-done.73), calls=%async_computation.4 | async-start | bytes 1024 | tf_op jit(solution)/shard_map/slice | solution.py:1099
  472.3 64.0 %copy-start.75 = (f32[128]{0:T(128)S(1)}, f32[128]{0:T(128)}, u32[]{:S(2)}) copy-start(f32[128]{0:T(128)} %copy-done.74) | copy-start | bytes 1540
  536.2 2.3 collective-permute-start.10
  (83 other events, 893.7 us)

commit v2 on v1

--- a/solution.py
+++ b/solution.py
@@ -149,6 +149,12 @@
         self.has_up = self.level < levels - 1
         self.has_down = self.level > 0
 
+    def choose(self, values):
+        result = jnp.int32(values[0])
+        for k in range(1, self.levels):
+            result = jnp.where(self.level == k, values[k], result)
+        return result
+
     def device(self, level, spot, core=None):
         return {"wide": level * 4 + spot, "narrow": self.core if core is None else core}
 
@@ -186,175 +192,423 @@
     )
 
 
-def gather_kernel(levels, sibling, x_ref, out_ref, own_sem, *sems):
-    send_up, send_dn, send_x, send_y, send_cx, send_cy, send_n = sems[:7]
-    recv_z, recv_x, recv_y, recv_cx, recv_cy, recv_n = sems[7:]
+class Gather:
+    NAMES = ("up", "dn", "x", "y", "cx", "cy", "rz", "rx", "ry", "rcx", "rcy")
+
+    def __init__(self, at, sibling, pairs, sems):
+        self.at, self.sibling, self.pairs = at, sibling, pairs
+        self.own_sem = sems[0]
+        self.sems = dict(zip(self.NAMES, sems[1:12]))
+        self.send_n, self.recv_n = sems[12:]
+        self.order = self.visits()
+
+    @staticmethod
+    def scratch(levels, arrays):
+        dma = pltpu.SemaphoreType.DMA
+        return (
+            [dma((arrays,))]
+            + [dma((arrays, levels))] * 11
+            + [dma((arrays, levels * 4))] * 2
+        )
+
+    def visits(self):
+        at = self.at
+        table = [
+            sorted(range(at.levels), key=lambda lev: (abs(lev - here), lev))
+            for here in range(at.levels)
+        ]
+        return [at.choose([row[k] for row in table]) for k in range(at.levels)]
+
+    def block(self, n, lev, sp, core=None):
+        ref = self.pairs[n][1]
+        if self.sibling:
+            return ref.at[(lev * 4 + sp) * 2 + (self.at.core if core is None else core)]
+        return ref.at[lev * 4 + sp]
+
+    def each(self, send, recv, lev, sp, device, part=None, own=False):
+        copies = []
+        for n, (x_ref, _) in enumerate(self.pairs):
+            dst = self.block(n, lev, sp)
+            src = x_ref if own else dst
+            if part is not None:
+                half = x_ref.shape[0] // 2
+                src = src.at[pl.ds(part * half, half)]
+                dst = dst.at[pl.ds(part * half, half)]
+            copies.append(
+                remote(src, dst, self.sems[send].at[n, lev], self.sems[recv].at[n, lev], device)
+            )
+        return copies
+
+    def up(self, lev, own=False):
+        at = self.at
+        return self.each("up", "rz", lev, at.spot, at.device(at.level + 1, at.spot), own=own)
+
+    def down(self, lev, own=False):
+        at = self.at
+        return self.each("dn", "rz", lev, at.spot, at.device(at.level - 1, at.spot), own=own)
+
+    def over_x(self, lev, sp, own=False):
+        at = self.at
+        return self.each("x", "rx", lev, sp, at.device(at.level, at.across), own=own)
+
+    def over_y(self, lev, sp, own=False):
+        at = self.at
+        return self.each("y", "ry", lev, sp, at.device(at.level, at.along), own=own)
+
+    def corner_y(self, lev, sp):
+        at = self.at
+        return self.each("cy", "rcy", lev, sp, at.device(at.level, at.along), part=0)
+
+    def corner_x(self, lev, sp):
+        at = self.at
+        return self.each("cx", "rcx", lev, sp, at.device(at.level, at.across), part=1)
+
+    def near(self, lev, sp, core=None, own=False):
+        at = self.at
+        copies = []
+        for n, (x_ref, _) in enumerate(self.pairs):
+            dst = self.block(n, lev, sp, core)
+            sems = self.send_n.at[n, lev * 4 + sp], self.recv_n.at[n, lev * 4 + sp]
+            device = at.device(at.level, at.spot, 1 - at.core)
+            copies.append(remote(x_ref if own else dst, dst, *sems, device))
+        return copies
+
+    def own_copies(self):
+        at = self.at
+        return [
+            pltpu.make_async_copy(x_ref, self.block(n, at.level, at.spot), self.own_sem.at[n])
+            for n, (x_ref, _) in enumerate(self.pairs)
+        ]
+
+    def take_own(self):
+        for copy in self.own_copies():
+            copy.wait()
+
+    def begin(self):
+        at = self.at
+        pl.when(at.has_up)(lambda: start(self.up(at.level, own=True)))
+        pl.when(at.has_down)(lambda: start(self.down(at.level, own=True)))
+        start(self.over_x(at.level, at.spot, own=True))
+        start(self.over_y(at.level, at.spot, own=True))
+        if self.sibling:
+            start(self.near(at.level, at.spot, own=True))
+        start(self.own_copies())
+
+    def take_column(self, lev):
+        at = self.at
+        arrived(self.up(lev))
+        pl.when((lev < at.level) & at.has_up)(lambda: start(self.up(lev)))
+        pl.when((lev > at.level) & at.has_down)(lambda: start(self.down(lev)))
+        start(self.over_x(lev, at.spot))
+        start(self.over_y(lev, at.spot))
+        if self.sibling:
+            start(self.near(lev, at.spot))
+
+    def take_x(self, lev):
+        at = self.at
+        arrived(self.over_x(lev, at.across))
+        start(self.corner_y(lev, at.across))
+        if self.sibling:
+            start(self.near(lev, at.across))
+
+    def take_y(self, lev):
+        at = self.at
+        arrived(self.over_y(lev, at.along))
+        start(self.corner_x(lev, at.along))
+        if self.sibling:
+            start(self.near(lev, at.along))
+
+    def take_corner(self, lev):
+        at = self.at
+        arrived(self.corner_y(lev, at.corner))
+        arrived(self.corner_x(lev, at.corner))
+        if self.sibling:
+            start(self.near(lev, at.corner))
+
+    def take_near(self, lev, sp):
+        arrived(self.near(lev, sp, 1 - self.at.core))
+
+    def steps(self):
+        levels, steps = self.at.levels, []
+        for s in range(1, levels + 2):
+            if s < levels:
+                steps.append(lambda lev=self.order[s]: self.take_column(lev))
+            if s - 1 < levels:
+                steps.append(lambda lev=self.order[s - 1]: self.take_x(lev))
+                steps.append(lambda lev=self.order[s - 1]: self.take_y(lev))
+            if s >= 2:
+                steps.append(lambda lev=self.order[s - 2]: self.take_corner(lev))
+        return steps
+
+    def finish(self, near=True):
+        at = self.at
+        if near:
+            self.take_own()
+        for lev in range(at.levels):
+            pl.when(at.has_up & (lev <= at.level))(lambda lev=lev: sent(self.up(lev)))
+            pl.when(at.has_down & (lev >= at.level))(lambda lev=lev: sent(self.down(lev)))
+            sent(self.over_x(lev, at.spot))
+            sent(self.over_y(lev, at.spot))
+            sent(self.corner_y(lev, at.across))
+            sent(self.corner_x(lev, at.along))
+            if self.sibling:
+                for sp in range(4):
+                    sent(self.near(lev, sp))
+                    if near:
+                        self.take_near(lev, sp)
+
+
+def start(copies):
+    for copy in copies:
+        copy.start()
+
+
+def arrived(copies):
+    for copy in copies:
+        copy.wait_recv()
+
+
+def sent(copies):
+    for copy in copies:
+        copy.wait_send()
+
+
+def gather_kernel(levels, sibling, arrays, *refs):
+    x_refs, out_refs, sems = refs[:arrays], refs[arrays : 2 * arrays], refs[2 * arrays :]
     at = Place(levels)
-    level, spot, core = at.level, at.spot, at.core
-    across, along, corner = at.across, at.along, at.corner
-    half = x_ref.shape[0] // 2
-    first, second = pl.ds(0, half), pl.ds(half, half)
     at.enter(sibling)
-
-    def block(lev, sp, co=None):
-        if sibling:
-            return out_ref.at[(lev * 4 + sp) * 2 + (core if co is None else co)]
-        return out_ref.at[lev * 4 + sp]
-
-    own = pltpu.make_async_copy(x_ref, block(level, spot), own_sem)
-    own.start()
-
-    def go_up(lev, src=None):
-        dst = block(lev, spot)
-        src = dst if src is None else src
-        return remote(src, dst, send_up.at[lev], recv_z.at[lev], at.device(level + 1, spot))
-
-    def go_down(lev, src=None):
-        dst = block(lev, spot)
-        src = dst if src is None else src
-        return remote(src, dst, send_dn.at[lev], recv_z.at[lev], at.device(level - 1, spot))
-
-    def go_x(lev, sp, src=None):
-        dst = block(lev, sp)
-        src = dst if src is None else src
-        return remote(src, dst, send_x.at[lev], recv_x.at[lev], at.device(level, across))
-
-    def go_y(lev, sp, src=None):
-        dst = block(lev, sp)
-        src = dst if src is None else src
-        return remote(src, dst, send_y.at[lev], recv_y.at[lev], at.device(level, along))
-
-    def corner_y(lev, sp):
-        ref = block(lev, sp).at[first]
-        return remote(ref, ref, send_cy.at[lev], recv_cy.at[lev], at.device(level, along))
-
-    def corner_x(lev, sp):
-        ref = block(lev, sp).at[second]
-        return remote(ref, ref, send_cx.at[lev], recv_cx.at[lev], at.device(level, across))
-
-    def to_sibling(lev, sp, src=None):
-        dst = block(lev, sp)
-        src = dst if src is None else src
-        sems = send_n.at[lev * 4 + sp], recv_n.at[lev * 4 + sp]
-        return remote(src, dst, *sems, at.device(level, spot, 1 - core))
-
-    def from_sibling(lev, sp):
-        ref = block(lev, sp, 1 - core)
-        sems = send_n.at[lev * 4 + sp], recv_n.at[lev * 4 + sp]
-        return remote(ref, ref, *sems, at.device(level, spot, 1 - core))
-
-    @pl.when(at.has_up)
-    def _():
-        go_up(level, x_ref).start()
-
-    @pl.when(at.has_down)
-    def _():
-        go_down(level, x_ref).start()
-
-    go_x(level, spot, x_ref).start()
-    go_y(level, spot, x_ref).start()
-    if sibling:
-        to_sibling(level, spot, x_ref).start()
-
-    def when(cond, run):
-        if cond is None:
-            run()
-        else:
-            pl.when(cond)(run)
-
-    def at_distance(s):
-        if s == 0:
-            return [(level, None)]
-        return [(level - s, level - s >= 0), (level + s, level + s < levels)]
-
-    def column(s):
-        for sign, (lev, cond) in zip((-1, 1), at_distance(s)):
-
-            def run(lev=lev, sign=sign):
-                go_up(lev).wait_recv()
-                if sign < 0:
-                    pl.when(at.has_up)(lambda: go_up(lev).start())
-                else:
-                    pl.when(at.has_down)(lambda: go_down(lev).start())
-                go_x(lev, spot).start()
-                go_y(lev, spot).start()
-                if sibling:
-                    to_sibling(lev, spot).start()
-
-            when(cond, run)
-
-    def square(s):
-        for lev, cond in at_distance(s):
-
-            def run(lev=lev):
-                go_x(lev, across).wait_recv()
-                corner_y(lev, across).start()
-                if sibling:
-                    to_sibling(lev, across).start()
-                go_y(lev, along).wait_recv()
-                corner_x(lev, along).start()
-                if sibling:
-                    to_sibling(lev, along).start()
-
-            when(cond, run)
-
-    def corners(s):
-        for lev, cond in at_distance(s):
-
-            def run(lev=lev):
-                corner_y(lev, corner).wait_recv()
-                corner_x(lev, corner).wait_recv()
-                if sibling:
-                    to_sibling(lev, corner).start()
-
-            when(cond, run)
-
-    for s in range(1, levels + 2):
-        if s < levels:
-            column(s)
-        if s - 1 < levels:
-            square(s - 1)
-        if s >= 2:
-            corners(s - 2)
-    own.wait()
-    for lev in range(levels):
-
-        @pl.when(at.has_up & (lev <= level))
-        def _():
-            go_up(lev).wait_send()
-
-        @pl.when(at.has_down & (lev >= level))
-        def _():
-            go_down(lev).wait_send()
-
-        go_x(lev, spot).wait_send()
-        go_y(lev, spot).wait_send()
-        corner_y(lev, across).wait_send()
-        corner_x(lev, along).wait_send()
-        if sibling:
-            for sp in range(4):
-                to_sibling(lev, sp).wait_send()
-                from_sibling(lev, sp).wait_recv()
-
-
-def gather_wide(x, levels, sibling, collective_id):
-    dma = pltpu.SemaphoreType.DMA
-    blocks = levels * 4
+    gather = Gather(at, sibling, list(zip(x_refs, out_refs)), sems)
+    gather.begin()
+    for step in gather.steps():
+        step()
+    gather.finish()
+
+
+def gather_wide(arrays, levels, sibling, collective_id):
+    blocks = levels * 4 * (2 if sibling else 1)
     anywhere = pl.BlockSpec(memory_space=pl.ANY)
     return pl.pallas_call(
-        functools.partial(gather_kernel, levels, sibling),
-        out_shape=jax.ShapeDtypeStruct((blocks * (2 if sibling else 1), *x.shape), x.dtype),
-        in_specs=[anywhere],
-        out_specs=anywhere,
-        scratch_shapes=[dma]
-        + [dma((levels,))] * 6
-        + [dma((blocks,))]
-        + [dma((levels,))] * 5
-        + [dma((blocks,))],
+        functools.partial(gather_kernel, levels, sibling, len(arrays)),
+        out_shape=[jax.ShapeDtypeStruct((blocks, *x.shape), x.dtype) for x in arrays],
+        in_specs=[anywhere] * len(arrays),
+        out_specs=[anywhere] * len(arrays),
+        scratch_shapes=Gather.scratch(levels, len(arrays)),
         compiler_params=pltpu.CompilerParams(
             collective_id=collective_id, has_side_effects=True
         ),
-    )(x)
+    )(*arrays)
+
+
+def dot_nn(left, right):
+    return lax.dot_general(left, right, (((1,), (0,)), ((), ())), preferred_element_type=F32)
+
+
+def dot_nt(left, right):
+    return lax.dot_general(left, right, (((1,), (1,)), ((), ())), preferred_element_type=F32)
+
+
+def experts_kernel(
+    levels, sizes, x_ref, grads_ref, marks_ref, gate_ref, down_ref,
+    rows_ref, mixed_ref, act_ref, back_ref, out_ref, gm_ref,
+    x_buf, g_buf, mark_buf, cu_buf, g_val, mixed_buf, act_buf, back_buf, out_buf, gm_buf, mark_t,
+    in_sem, out_sem, gm_val, *sems,
+):
+    hidden, used, full = sizes
+    at = Place(levels)
+    at.enter(True)
+    gather = Gather(at, True, [(x_ref, rows_ref)], sems)
+    gather.begin()
+    place = at.level * 4 + at.spot
+    units = 4 * levels
+    plan = [(0, 0)]
+    for s in range(1, levels + 2):
+        if s < levels:
+            plan.append((s, 0))
+        if s - 1 < levels:
+            plan += [(s - 1, 1), (s - 1, 2)]
+        if s >= 2:
+            plan.append((s - 2, 3))
+    rows = x_ref.shape[0]
+    batch = 2 * rows
+
+    def pick(k, values):
+        result = jnp.int32(0) + values[0]
+        for j in range(1, len(values)):
+            result = jnp.where(k == j, values[j], result)
+        return result
+
+    def unit(k):
+        visit = pick(k, [v for v, _ in plan])
+        kind = pick(k, [t for _, t in plan])
+        lev = pick(visit, gather.order)
+        sp = pick(kind, [at.spot, at.across, at.along, at.corner])
+        return lev, sp, kind
+
+    def loads(k, first):
+        slot = lax.rem(k, 2)
+        blocks = pl.ds(first, 2)
+        return [
+            pltpu.make_async_copy(rows_ref.at[blocks], x_buf.at[slot], in_sem.at[slot, 0]),
+            pltpu.make_async_copy(grads_ref.at[blocks], g_buf.at[slot], in_sem.at[slot, 1]),
+            pltpu.make_async_copy(marks_ref.at[blocks], mark_buf.at[slot], in_sem.at[slot, 2]),
+        ]
+
+    def stores(k, first):
+        slot = lax.rem(k, 2)
+        rng = pl.ds(pl.multiple_of(first * rows, batch), batch)
+        pairs = [(mixed_buf, mixed_ref), (act_buf, act_ref), (back_buf, back_ref), (out_buf, out_ref)]
+        return [
+            pltpu.make_async_copy(buf.at[slot], ref.at[rng], out_sem.at[slot, n])
+            for n, (buf, ref) in enumerate(pairs)
+        ]
+
+    def serve(k):
+        lev, sp, kind = unit(k)
+        pl.when(kind == 0)(lambda: gather.take_column(lev))
+        pl.when(kind == 1)(lambda: gather.take_x(lev))
+        pl.when(kind == 2)(lambda: gather.take_y(lev))
+        pl.when(kind == 3)(lambda: gather.take_corner(lev))
+
+    def fetch(k):
+        lev, sp, _ = unit(k)
+        gather.take_near(lev, sp)
+        start(loads(k, (lev * 4 + sp) * 2))
+
+    def lanes(n):
+        return lax.broadcasted_iota(jnp.int32, (batch, 128), 1) + n * 128
+
+    def mixing():
+        tail = full // 128 - 1
+        mark = mark_t[...]
+        masked = jnp.where(mark > 0.5, cu_buf[:, full - 128 : full], MASKED)
+        top = jnp.max(masked, axis=1, keepdims=True)
+        weight = jnp.where(mark > 0.5, jnp.exp(masked - top), 0.0)
+        mine = jnp.where((lanes(tail) == used + place) & (mark > 1.5), weight, 0.0)
+        return jnp.sum(mine, axis=1, keepdims=True) / jnp.sum(weight, axis=1, keepdims=True)
+
+    def elementwise(slot):
+        mix = jnp.broadcast_to(mixing(), (batch, 128))
+        total = jnp.zeros((batch, 128), F32)
+        for n in range(full // 128):
+            cols = slice(n * 128, (n + 1) * 128)
+            up_cols = slice(full + n * 128, full + (n + 1) * 128)
+            gate, upper, back = cu_buf[:, cols], cu_buf[:, up_cols], g_val[:, cols]
+            whole = (n + 1) * 128 <= hidden
+            scale = mix
+            if not whole:
+                scale = jnp.where(lanes(n) < hidden, mix, jnp.where(lanes(n) < used, 1.0, 0.0))
+            sig = jax.nn.sigmoid(gate)
+            act = gate * sig
+            active = act * upper
+            grad_act = scale * back
+            slope = sig * (1.0 + gate * (1.0 - sig))
+            mixed_buf[slot, :, cols] = (scale * active).astype(BF16)
+            act_buf[slot, :, cols] = (grad_act * upper * slope).astype(BF16)
+            act_buf[slot, :, up_cols] = (grad_act * act).astype(BF16)
+            term = active * back
+            total = total + (term if whole else jnp.where(lanes(n) < hidden, term, 0.0))
+        gm_buf[...] = total
+
+    def compute(k):
+        lev, sp, _ = unit(k)
+        first = (lev * 4 + sp) * 2
+        slot = lax.rem(k, 2)
+        for copy in loads(k, first):
+            copy.wait()
+        x = x_buf[slot].reshape(batch, -1)
+        cu_buf[...] = dot_nn(x, gate_ref[...])
+        g_val[...] = dot_nt(g_buf[slot].reshape(batch, -1), down_ref[...])
+        for n in range(2):
+            marks = mark_buf[slot, n]
+            above = jnp.zeros((used - (full - 128), 128), F32)
+            below = jnp.zeros((full - used - marks.shape[0], 128), F32)
+            mark_t[pl.ds(n * rows, rows), :] = jnp.transpose(jnp.concatenate([above, marks, below], axis=0))
+
+        @pl.when(k >= 2)
+        def _():
+            for copy in stores(k, 0):
+                copy.wait()
+
+        elementwise(slot)
+        back_buf[slot] = dot_nt(act_buf[slot], gate_ref[...]).astype(BF16)
+        out_buf[slot] = dot_nn(mixed_buf[slot], down_ref[...]).astype(BF16)
+        for n in range(2):
+            gm = jnp.transpose(gm_buf[pl.ds(n * rows, rows), :])
+            gm_val[pl.ds(first + n, 1), :] = jnp.sum(gm, axis=0, keepdims=True)
+        start(stores(k, first))
+
+    gather.take_own()
+    fetch(0)
+
+    def loop(k, carry):
+        @pl.when((k > 0) & (k + 1 < units))
+        def _():
+            serve(k + 1)
+            fetch(k + 1)
+
+        compute(k)
+
+        @pl.when(k == 0)
+        def _():
+            serve(1)
+            fetch(1)
+
+        return carry
+
+    lax.fori_loop(0, units, loop, 0)
+    gm_ref[...] = gm_val[...]
+    for k in (0, 1):
+        for copy in stores(k, 0):
+            copy.wait()
+    gather.finish(near=False)
+
+
+def experts_rows(x, grads, marks, gate_up, down, hidden, used, levels, collective_id):
+    rows, width = x.shape
+    full = down.shape[0]
+    blocks = 8 * levels
+    total = blocks * rows
+    dma = pltpu.SemaphoreType.DMA
+    vmem = pltpu.VMEM
+    anywhere = pl.BlockSpec(memory_space=pl.ANY)
+    inside = pl.BlockSpec(memory_space=vmem)
+    shape = jax.ShapeDtypeStruct
+    batch = 2 * rows
+    return pl.pallas_call(
+        functools.partial(experts_kernel, levels, (hidden, used, full)),
+        out_shape=[
+            shape((blocks, rows, width), BF16),
+            shape((total, full), BF16),
+            shape((total, 2 * full), BF16),
+            shape((total, width), BF16),
+            shape((total, width), BF16),
+            shape((blocks, rows), F32),
+        ],
+        in_specs=[anywhere, anywhere, anywhere, inside, inside],
+        out_specs=[anywhere] * 5 + [inside],
+        scratch_shapes=[
+            vmem((2, 2, rows, width), BF16),
+            vmem((2, 2, rows, width), BF16),
+            vmem((2, 2, *marks.shape[1:]), F32),
+            vmem((batch, 2 * full), F32),
+            vmem((batch, full), F32),
+            vmem((2, batch, full), BF16),
+            vmem((2, batch, 2 * full), BF16),
+            vmem((2, batch, width), BF16),
+            vmem((2, batch, width), BF16),
+            vmem((batch, 128), F32),
+            vmem((batch, 128), F32),
+            dma((2, 3)),
+            dma((2, 4)),
+            vmem((blocks, rows), F32),
+        ]
+        + Gather.scratch(levels, 1),
+        compiler_params=pltpu.CompilerParams(
+            collective_id=collective_id,
+            has_side_effects=True,
+            vmem_limit_bytes=56 * 1024 * 1024,
+        ),
+    )(x, grads, marks, gate_up, down)
 
 
 def destinations(levels):
@@ -401,13 +655,7 @@
     at.enter(sibling)
     table = destinations(levels)
 
-    def destination(s):
-        lev = jnp.int32(table[0][s])
-        for k in range(1, levels):
-            lev = jnp.where(level == k, table[k][s], lev)
-        return lev
-
-    order = [destination(s) for s in range(levels)]
+    order = [at.choose([row[s] for row in table]) for s in range(levels)]
 
     def to_sibling(lev, sp):
         b = lev * 4 + sp
@@ -941,7 +1189,9 @@
     part = width // 2
     heads = part // HEAD_DIM
     hidden_part = expert_gate.shape[2]
-    slice_width = shared_gate.shape[1] // (2 * wide_size)
+    stored = shared_gate.shape[1] // 2
+    slice_width = -(-stored // (16 * wide_size)) * 16
+    slices = stored // slice_width
     experts = w_router.shape[1]
 
     def swap(value):
@@ -963,19 +1213,20 @@
     picks = (routes[:, :, None] == jnp.arange(experts, dtype=jnp.int32)[None, None, :]).astype(
         jnp.int32
     )
-    marks = jnp.sum(picks * (1 + keep)[:, :, None], axis=1).astype(BF16)
-    all_marks = lax.all_gather(marks, ("wide", "narrow"), axis=0, tiled=True).astype(F32)
-    all_grads = gather_wide(cotangent, levels, True, 0).reshape(-1, width)
+    marks = jnp.sum(picks * (1 + keep)[:, :, None], axis=1).astype(F32)
+    all_grads, all_marks = gather_wide([cotangent, marks.T], levels, True, 0)
 
     first_unit = place * slice_width
-    stored = shared_gate.shape[1] // 2
-    gate_mine = lax.dynamic_slice_in_dim(shared_gate, core * stored + first_unit, slice_width, 1)
-    up_mine = lax.dynamic_slice_in_dim(shared_up, core * stored + first_unit, slice_width, 1)
-    gate_send = lax.dynamic_slice_in_dim(
-        shared_gate, (1 - core) * stored + first_unit, slice_width, 1
-    )
-    up_send = lax.dynamic_slice_in_dim(shared_up, (1 - core) * stored + first_unit, slice_width, 1)
-    down_slice = lax.dynamic_slice_in_dim(shared_down, first_unit, slice_width, 0)
+    holds = place < slices
+
+    def shared_slice(value, which, axis):
+        begin = which * stored + first_unit
+        taken = lax.dynamic_slice_in_dim(value, begin, slice_width, axis)
+        return jnp.where(holds, taken, jnp.zeros((), value.dtype))
+
+    gate_mine, up_mine = shared_slice(shared_gate, core, 1), shared_slice(shared_up, core, 1)
+    gate_send, up_send = shared_slice(shared_gate, 1 - core, 1), shared_slice(shared_up, 1 - core, 1)
+    down_slice = shared_slice(shared_down, 0, 0)
     gains = jnp.stack([attn_gain, ffn_gain])
     sent = swap(jnp.concatenate([gate_send, up_send, w_router], axis=1))
     gains = in_order(gains, swap(gains), 1).astype(F32)
@@ -1011,7 +1262,6 @@
     hidden = inputs + branch[:local_rows] + arrived.astype(F32)
     normed, unit_two, scale_two = norm_forward(hidden, ffn_scale)
     normed_two = normed.astype(BF16)
-    all_rows = gather_wide(normed_two, levels, True, 1).reshape(-1, width)
 
     used = hidden_part + slice_width
     full = -(-(used + experts) // 128) * 128
@@ -1024,27 +1274,19 @@
     gate_all = pad(jnp.concatenate([expert_gate[0], gate_slice, router], axis=1), full, 1)
     up_all = pad(jnp.concatenate([expert_up[0], up_slice], axis=1), full, 1)
     down_all = pad(jnp.concatenate([expert_down[0], down_slice], axis=0), full, 0)
-    gate_vals = matmul(all_rows, gate_all)
-    upper = matmul(all_rows, up_all)
-    back = matmul_right(all_grads, down_all)
-    logits = gate_vals[:, used : used + experts]
-    routed = all_marks > 0.0
-    masked = jnp.where(routed, logits, MASKED)
-    weights = jnp.where(routed, jnp.exp(masked - jnp.max(masked, axis=1, keepdims=True)), 0.0)
-    gates = weights / jnp.sum(weights, axis=1, keepdims=True)
-    mix_all = gates * (all_marks > 1.5)
-    mix = jnp.sum(
-        jnp.where(jnp.arange(experts)[None, :] == place, mix_all, 0.0), axis=1, keepdims=True
-    )
-    unit = jnp.arange(full)[None, :]
-    scale = jnp.where(unit < hidden_part, mix, jnp.where(unit < used, 1.0, 0.0))
-    act_vals, slope_vals = silu_parts(gate_vals)
-    active = act_vals * upper
-    grad_act = scale * back
-    grad_gate = (grad_act * upper * slope_vals).astype(BF16)
-    grad_upper = (grad_act * act_vals).astype(BF16)
-    mixed = (scale * active).astype(BF16)
-    grad_mix = jnp.sum(jnp.where(unit < hidden_part, active * back, 0.0), axis=1)
+    all_rows, mixed, act, grad_rows, expert_out, grad_mix = experts_rows(
+        normed_two,
+        all_grads,
+        all_marks,
+        jnp.concatenate([gate_all, up_all], axis=1),
+        down_all,
+        hidden_part,
+        used,
+        levels,
+        1,
+    )
+    all_rows = all_rows.reshape(-1, width)
+    all_grads = all_grads.reshape(-1, width)
     grad_mix = lax.all_to_all(
         grad_mix.reshape(wide_size, 2, local_rows), "wide", split_axis=0, concat_axis=0, tiled=True
     )
@@ -1052,13 +1294,30 @@
     send_core = jnp.where(core == 0, grad_mix[:, 1], grad_mix[:, 0])
     grad_mix = (pick_core + swap(send_core)).T
     block_shape = (2 * wide_size, local_rows, width)
-    grad_rows = matmul_right(grad_gate, gate_all) + matmul_right(grad_upper, up_all)
-    grad_rows = scatter_wide(grad_rows.astype(BF16).reshape(block_shape), levels, True, 2)
-    expert_out = scatter_wide(matmul(mixed, down_all).astype(BF16).reshape(block_shape), levels, True, 3)
+    grad_rows = scatter_wide(grad_rows.reshape(block_shape), levels, True, 2)
+    expert_out = scatter_wide(expert_out.reshape(block_shape), levels, True, 3)
     output = (hidden + expert_out.astype(F32)).astype(BF16)
-    grad_gate_all = matmul_left(all_rows, grad_gate)
-    grad_up_all = matmul_left(all_rows, grad_upper)
-    grad_down_all = matmul_left(mixed, all_grads)
+    grad_expert_gate = matmul_left(all_rows, act[:, :hidden_part])
+    grad_expert_up = matmul_left(all_rows, act[:, full : full + hidden_part])
+    grad_expert_down = matmul_left(mixed[:, :hidden_part], all_grads)
+    shared_act = jnp.concatenate([act[:, hidden_part:used], act[:, full + hidden_part : full + used]], 1)
+    shared_t = matmul_left(shared_act, all_rows).astype(BF16)
+    shared_down_grad = matmul_left(mixed[:, hidden_part:used], all_grads).astype(BF16)
+    theirs = swap(columns(shared_t, 1 - core, part))
+    shared_t = columns(shared_t, core, part)
+
+    def side_by_side(value):
+        return jnp.concatenate([value[:slice_width], value[slice_width:]], axis=1)
+
+    shared_block = jnp.concatenate(
+        [in_order(side_by_side(shared_t), side_by_side(theirs), 0), shared_down_grad], axis=0
+    )
+    (shared_all,) = gather_wide([shared_block], levels, False, 4)
+    shared_all = shared_all[:slices].astype(F32)
+    pair = shared_all[:, : 2 * slice_width].reshape(slices, 2, slice_width, 2, part)
+    grad_shared_gate = pair[:, :, :, 0].transpose(3, 1, 0, 2).reshape(part, 2 * stored)
+    grad_shared_up = pair[:, :, :, 1].transpose(3, 1, 0, 2).reshape(part, 2 * stored)
+    grad_shared_down = shared_all[:, 2 * slice_width :].reshape(stored, width)
 
     marks = marks.astype(F32)
     routed = marks > 0.0
@@ -1104,53 +1363,33 @@
     small_mine = lax.dynamic_slice_in_dim(small, core * part, part, 0)
     small_send = lax.dynamic_slice_in_dim(small, (1 - core) * part, part, 0)
     small = (small_mine + swap(small_send)).astype(BF16)
-    shared_t = jnp.concatenate(
-        [
-            grad_gate_all[:, hidden_part:used].astype(BF16),
-            grad_up_all[:, hidden_part:used].astype(BF16),
-        ],
-        axis=1,
-    )
-    shared_mine = lax.dynamic_slice_in_dim(shared_t, core * part, part, 0)
-    shared_send = lax.dynamic_slice_in_dim(shared_t, (1 - core) * part, part, 0)
-    shared_pair = in_order(shared_mine[None], swap(shared_send)[None], 0)
-    shared_down_grad = grad_down_all[hidden_part:used].astype(BF16)
-    flat = jnp.concatenate(
-        [shared_pair.reshape(-1), shared_down_grad.reshape(-1), small.reshape(-1)]
-    )
-    unit_rows = 32
-    extra_rows = -(-flat.shape[0] // (width * unit_rows)) * unit_rows
-    flat = jnp.concatenate([flat, jnp.zeros((extra_rows * width - flat.shape[0],), BF16)])
+    size = small.size
+    extra_rows = -(-size // (width * 16)) * 16
+    flat = jnp.concatenate([small.reshape(-1), jnp.zeros((extra_rows * width - size,), BF16)])
     sum_rows = 4 * part // wide_size
-    summed = scatter_wide(grad_dense.reshape(wide_size, sum_rows, width), levels, False, 4)
-    everything = gather_wide(
-        jnp.concatenate([summed, flat.reshape(extra_rows, width)], axis=0), levels, False, 5
-    ).astype(F32)
+    summed = scatter_wide(grad_dense.reshape(wide_size, sum_rows, width), levels, False, 5)
+    (everything,) = gather_wide(
+        [jnp.concatenate([summed, flat.reshape(extra_rows, width)], axis=0)], levels, False, 6
+    )
     owned = everything[:, :sum_rows].reshape(4, part, width)
-    flat = everything[:, sum_rows:].reshape(wide_size, -1)
-    size = 2 * part * 2 * slice_width
-    pair = flat[:, :size].reshape(wide_size, 2, part, 2, slice_width)
-    pair = pair.transpose(3, 2, 1, 0, 4).reshape(2, part, 2 * wide_size * slice_width)
-    down_size = slice_width * width
-    own_down = flat[:, size : size + down_size].reshape(wide_size * slice_width, width)
-    small = jnp.sum(flat[:, size + down_size : size + down_size + small.size], axis=0)
-    small = small.reshape(part, 2 + experts)
+    flat = everything[:, sum_rows:].astype(F32).reshape(wide_size, -1)
+    small = jnp.sum(flat[:, :size], axis=0).reshape(part, 2 + experts)
     return (
         output,
         grad_tokens,
         small[:, 0],
-        owned[0],
-        owned[1],
-        owned[2],
-        owned[3],
+        owned[0].astype(F32),
+        owned[1].astype(F32),
+        owned[2].astype(F32),
+        owned[3].astype(F32),
         small[:, 1],
         small[:, 2:],
-        pair[0],
-        pair[1],
-        own_down,
-        grad_gate_all[None, :, :hidden_part],
-        grad_up_all[None, :, :hidden_part],
-        grad_down_all[None, :hidden_part],
+        grad_shared_gate,
+        grad_shared_up,
+        grad_shared_down,
+        grad_expert_gate[None],
+        grad_expert_up[None],
+        grad_expert_down[None],
     )
 
 

time: 791 us -> 652 us (0.82)
  local copies, waits for them, and re-layouts: 210 us -> 96.2 us
  Pallas kernels: 364 us -> 428 us
  matrix products: 123 us -> 62.9 us
  blocking collectives: 40.6 us -> 0 us
    pallas_call x3 -> x4, Pallas kernels: 188 us -> 255 us  [the longest x3 154 us: gather_wide(): pl.pallas_call(functools.partial(gather_kernel, levels, sibling, len(arra...]
    slice x10 -> x9, local copies, waits for them, and re-layouts: 85.3 us -> 23.9 us  [the longest x1 9.81 us: tokens_path(): pair[:, :, :, 1].transpose(3, 1, 0, 2).reshape(part, 2 * stored)]
    reshape x4 -> x2, local copies, waits for them, and re-layouts: 50.5 us -> 7.46 us  [the longest x1 6.43 us: tokens_path(): shared_all[:, :2 * slice_width].reshape(slices, 2, slice_width, 2, part)]
    all_gather x1 -> x0, blocking collectives: 40.6 us -> none  [tokens_path(): lax.all_gather(marks, ('wide', 'narrow'), axis=0, tiled=True).astype(F32)]
    dot_general x7 -> x4, matrix products: 44.3 us -> 6.39 us  [matmul(): return jnp.dot(left, right, preferred_element_type=jnp.float32)]
    dot_general x8 -> x5, matrix products: 43.1 us -> 6.25 us  [matmul_right(): lax.dot_general(left, right, (((1,), (1,)), ((), ())), preferred_element_...]
    dot_general x8 -> x10, matrix products: 30.8 us -> 46.8 us  [matmul_left(): lax.dot_general(left, right, (((0,), (0,)), ((), ())), preferred_element_...]
    convert_element_type x0 -> x6, other arithmetic: none -> 12.9 us  [the longest x1 3.5 us: tokens_path(): owned[3].astype(F32)]
  transfers between devices with their start and end apart: 12 -> 12, of which waited for: 2 -> 2; matrix products, arithmetic and copies ran while one was open for 13% -> 13% of each run, Pallas kernels for 29% -> 41%
where the time goes in v2:
time: 652 us; the launch traced here: 642 us
  Pallas kernels  428 us (66%)
  local copies, waits for them, and re-layouts  96.2 us (15%)
  matrix products  62.9 us (10%)
  other arithmetic  43.4 us (7%)
  starting transfers between devices  7.88 us (1%)
    pallas_call x3, Pallas kernels, scatter_wide(): pl.pallas_call(functools.partial(scatter_kernel, levels, sibling), out_sh...  173 us
    pallas_call x3, Pallas kernels, gather_wide(): pl.pallas_call(functools.partial(gather_kernel, levels, sibling, len(arra...  154 us
    pallas_call x1, Pallas kernels, experts_rows(): pl.pallas_call(functools.partial(experts_kernel, levels, (hidden, used, f...  101 us
    dot_general x10, matrix products, matmul_left(): lax.dot_general(left, right, (((0,), (0,)), ((), ())), preferred_element_...  46.8 us
    unnamed x167, local copies, waits for them, and re-layouts  31 us
  transfers between devices with their start and end apart: 12, of which 2 were waited for; matrix products, arithmetic and copies ran while one was open for 13% of the time, Pallas kernels for 41%

profile of v2, /device:TPU:0, one launch (start us, length us, event | category | flops | bytes accessed | tf_op | source)
XLA Modules:
  0.0 641.7 jit_solution(13396261976930650848)
XLA Ops:
  27.2 53.5 %shard_map.289 = (bf16[32,128,1280]{2,1,0:T(8,128)(2,1)}, f32[32,16,128]{2,1,0:T(8,128)}) custom-call(bf16[128,1280]{1,0:T(8,128)(2,1)} %refs_0_.1, f32[16,128]{1,0:T(8,128)} %convert_bitcast_fusion.refs_1_), custom_call_target="tpu_custom_call" | custom-call | tf_op jit(solution)/shard_map/pallas_call | solution.py:390
  84.7 6.3 concatenate.118.gate_ref
  118.8 100.8 %shard_map.290 = (bf16[32,128,1280]{2,1,0:T(8,128)(2,1)}, bf16[4096,512]{1,0:T(8,128)(2,1)}, bf16[4096,1024]{1,0:T(8,128)(2,1)}, bf16[4096,1280]{1,0:T(8,128)(2,...) custom-call(bf16[128,1280]{1,0:T(8,128)(2,1)} %copy-done.20, bf16[32,128,1280]{2,1,0:T(8,128)(2,1)} %get-tuple-element.23.grads_ref, ...), custom_call_target="tpu_custom_call" | custom-call | tf_op jit(solution)/shard_map/pallas_call | solution.py:577
  219.7 6.7 %convolution_convert_fusion.6 = bf16[32,1280]{1,0:T(8,128)(2,1)} fusion(bf16[4096,1280]{1,0:T(8,128)(2,1)} %bitcast.122, bf16[4096,512]{1,0:T(8,128)(2,1)} %get-tuple-element.30), kind=kOutput, calls=%fused_computation.33 | convolution fusion | flops 335585280 | bytes 11616256 | tf_op jit(solution)/shard_map/dot_general | solution.py:24
  226.4 6.4 fusion.6
  232.8 3.3 fusion.62
  236.1 9.0 %fusion.12 = f32[1,1280,448]{1,2,0:T(8,128)} fusion(bf16[4096,1280]{1,0:T(8,128)(2,1)S(1)} %bitcast.129, bf16[4096,1024]{1,0:T(8,128)(2,1)} %get-tuple-element.28), kind=kOutput, calls=%fused_computation.14 | convolution fusion | flops 4697620480 | bytes 16973824 | tf_op jit(solution)/shard_map/dot_general | solution.py:24
  245.1 15.2 %fusion.9 = f32[1,1280,448]{1,2,0:T(8,128)} fusion(bf16[4096,1280]{1,0:T(8,128)(2,1)S(1)} %bitcast.130, bf16[4096,1024]{1,0:T(8,128)(2,1)S(1)} %bitcast.157), kind=kOutput, calls=%fused_computation.13 | convolution fusion | flops 4697620480 | bytes 16973824 | tf_op jit(solution)/shard_map/dot_general | solution.py:24
  260.2 4.7 all-to-all-start
  265.0 6.0 convolution_convert_fusion.5
  272.2 56.1 %shard_map.291 = bf16[128,1280]{1,0:T(8,128)(2,1)} custom-call(bf16[32,128,1280]{2,1,0:T(8,128)(2,1)} %bitcast.134), custom_call_target="tpu_custom_call" | custom-call | tf_op jit(solution)/shard_map/pallas_call | solution.py:806
  328.4 55.3 %shard_map.292 = bf16[128,1280]{1,0:T(8,128)(2,1)} custom-call(bf16[32,128,1280]{2,1,0:T(8,128)(2,1)} %bitcast.133), custom_call_target="tpu_custom_call" | custom-call | tf_op jit(solution)/shard_map/pallas_call | solution.py:806
  390.9 38.5 %shard_map.295 = bf16[16,96,1280]{2,1,0:T(8,128)(2,1)} custom-call(bf16[96,1280]{1,0:T(8,128)(2,1)} %pad_maximum_fusion.10.refs_0_), custom_call_target="tpu_custom_call" | custom-call | tf_op jit(solution)/shard_map/pallas_call | solution.py:390
  436.1 6.4 %reshape.359 = f32[14,2,32,2,640]{4,3,2,1,0:T(2,128)} reshape(f32[14,64,1280]{2,1,0:T(8,128)} %slice.283) | data formatting | bytes 9175040 | tf_op jit(solution)/shard_map/reshape | solution.py:1317
  454.8 9.8 %fusion.64 = (f32[14,2,32,1,640]{4,3,2,1,0:T(1,128)S(1)}, f32[14,2,32,1,640]{4,3,2,1,0:T(1,128)}) fusion(f32[14,2,32,2,640]{4,3,2,1,0:T(2,128)} %reshape.359), kind=kLoop, calls=%fused_computation.175 | loop fusion | bytes 9175040 | tf_op jit(solution)/shard_map/slice | solution.py:1319
  466.2 3.1 copy.189
  469.3 3.2 copy.206
  472.5 3.2 copy.188
  478.5 3.2 maximum_select_fusion
  488.2 3.3 pad_maximum_fusion
  491.5 61.5 %shard_map.293 = bf16[160,1280]{1,0:T(8,128)(2,1)} custom-call(bf16[16,160,1280]{2,1,0:T(8,128)(2,1)} %bitcast.132), custom_call_target="tpu_custom_call" | custom-call | tf_op jit(solution)/shard_map/pallas_call | solution.py:806
  557.1 62.1 %shard_map.294 = bf16[16,176,1280]{2,1,0:T(8,128)(2,1)} custom-call(bf16[176,1280]{1,0:T(8,128)(2,1)} %pad_maximum_fusion.4.refs_0_), custom_call_target="tpu_custom_call" | custom-call | tf_op jit(solution)/shard_map/pallas_call | solution.py:390
  619.2 5.3 fusion.63
  631.6 3.5 bitcast_convert_fusion
  (311 shorter events, 113.2 us)
Async XLA Ops:
  0.6 113.7 %copy-start = (bf16[640,1280]{1,0:T(8,128)(2,1)S(1)}, bf16[640,1280]{1,0:T(8,128)(2,1)}, u32[]{:S(2)}) copy-start(bf16[640,1280]{1,0:T(8,128)(2,1)} %param.27) | copy-start | bytes 4915204
  2.2 14.5 %collective-permute-start.1 = (bf16[2,640]{1,0:T(2,128)(2,1)S(1)}, bf16[2,640]{1,0:T(2,128)(2,1)S(1)}, u32[]{:S(2)}, u32[]{:S(2)}) collective-permute-start(bf16[2,640]{1,0:T(2,128)(2,1)S(1)} %pad_maximum_fusion.15), channel_id=1, source_target_pairs={{0,1},{1,0},{2,3},{3,2},{4,5},{5,4},{6,7},{7,6},{8,9},{9,8},{10,11... | collective-permute-start | bytes 7688 | tf_op jit(solution)/shard_map/ppermute | solution.py:1198
  2.7 14.1 %collective-permute-start = (bf16[128,1280]{1,0:T(8,128)(2,1)}, bf16[128,1280]{1,0:T(8,128)(2,1)}, u32[]{:S(2)}, u32[]{:S(2)}) collective-permute-start(bf16[128,1280]{1,0:T(8,128)(2,1)} %param.18), channel_id=1, source_target_pairs={{0,1},{1,0},{2,3},{3,2},{4,5},{5,4},{6,7},{7,6},{8,9},{9,8},{10,11... | collective-permute-start | bytes 983048 | tf_op jit(solution)/shard_map/ppermute | solution.py:1198
  6.8 74.0 %collective-permute-start.4 = (bf16[640,80]{1,0:T(8,128)(2,1)}, bf16[640,80]{1,0:T(8,128)(2,1)}, u32[]{:S(2)}, u32[]{:S(2)}) collective-permute-start(bf16[640,80]{1,0:T(8,128)(2,1)} %pad_maximum_fusion.11), channel_id=1, source_target_pairs={{0,1},{1,0},{2,3},{3,2},{4,5},{5,4},{6,7},{7,6},{8,9},{9,8},{10,11... | collective-permute-start | bytes 307208 | tf_op jit(solution)/shard_map/ppermute | solution.py:1198
  18.2 98.4 %copy-start.63 = (f32[256]{0:T(256)}, f32[256]{0:T(256)S(1)}, u32[]{:S(2)}) copy-start(f32[256]{0:T(256)S(1)} %add_rsqrt_fusion) | copy-start | bytes 3076
  20.5 71.9 %copy-start.18 = (bf16[256,640]{1,0:T(8,128)(2,1)}, bf16[256,640]{1,0:T(8,128)(2,1)S(1)}, u32[]{:S(2)}) copy-start(bf16[256,640]{1,0:T(8,128)(2,1)S(1)} %fusion.39) | copy-start | bytes 983044
  22.5 68.5 %collective-permute-start.2 = (bf16[256,1920]{1,0:T(8,128)(2,1)}, bf16[256,1920]{1,0:T(8,128)(2,1)}, u32[]{:S(2)}, u32[]{:S(2)}) collective-permute-start(bf16[256,1920]{1,0:T(8,128)(2,1)} %convolution_convert_fusion.4), channel_id=1, source_target_pairs={{0,1},{1,0},{2,3},{3,2},{4,5},{5,4},{6,7},{7,6},{8,9},{9,8},{10,11... | collective-permute-start | bytes 2949128 | tf_op jit(solution)/shard_map/ppermute | solution.py:1198
  115.1 1.7 collective-permute-start.3
  117.0 102.6 %copy-start.59 = (f32[128]{0:T(128)}, f32[128]{0:T(128)S(1)}, u32[]{:S(2)}) copy-start(f32[128]{0:T(128)S(1)} %add_rsqrt_fusion.1) | copy-start | bytes 1540
  118.8 107.6 %slice-start = ((s8[10485760]{0:T(1024)(128)(4,1)}), s8[4194304]{0:T(1024)(128)(4,1)S(1)}, s32[]{:S(2)}) async-start(s8[10485760]{0:T(1024)(128)(4,1)} %bitcast.123), calls=%async_computation.1 | async-start | bytes 8388608
  118.8 107.6 %slice-start.1 = ((s8[10485760]{0:T(1024)(128)(4,1)}), s8[2097152]{0:T(1024)(128)(4,1)S(1)}, s32[]{:S(2)}) async-start(s8[10485760]{0:T(1024)(128)(4,1)} %bitcast.123), calls=%async_computation.2 | async-start | bytes 4194304
  260.2 123.5 %all-to-all-start = ((f32[16,2,128]{2,1,0:T(2,128)}), f32[16,2,128]{2,1,0:T(2,128)S(1)}, u32[]{:S(2)}, u32[]{:S(2)}) async-start(f32[16,2,128]{2,1,0:T(2,128)} %bitcast.14), calls=%async_computation | async-start | bytes 32768 | tf_op jit(solution)/shard_map/all_to_all | solution.py:1290
  328.3 56.0 %copy-start.56 = (f32[128,16]{0,1:T(8,128)S(1)}, f32[128,16]{0,1:T(8,128)}, u32[]{:S(2)}) copy-start(f32[128,16]{0,1:T(8,128)} %get-tuple-element.161) | copy-start | bytes 24580
  328.3 56.0 %copy-start.62 = (f32[128]{0:T(128)S(1)}, f32[128]{0:T(128)}, u32[]{:S(2)}) copy-start(f32[128]{0:T(128)} %get-tuple-element.160) | copy-start | bytes 1540
  328.4 57.1 %copy-start.4 = (f32[128,1280]{1,0:T(8,128)S(1)}, f32[128,1280]{1,0:T(8,128)}, u32[]{:S(2)}) copy-start(f32[128,1280]{1,0:T(8,128)} %copy-done.3) | copy-start | bytes 1966084
  328.4 57.1 %copy-start.60 = (f32[128]{0:T(128)S(1)}, f32[128]{0:T(128)}, u32[]{:S(2)}) copy-start(f32[128]{0:T(128)} %copy-done.59) | copy-start | bytes 1540
  383.7 5.6 collective-permute-start.10
  383.8 1.6 collective-permute-start.5
  389.1 53.4 %collective-permute-start.6 = (bf16[128,1280]{1,0:T(8,128)(2,1)S(1)}, bf16[128,1280]{1,0:T(8,128)(2,1)}, u32[]{:S(2)}, u32[]{:S(2)}) collective-permute-start(bf16[128,1280]{1,0:T(8,128)(2,1)S(1)} %fusion.60), channel_id=1, source_target_pairs={{0,1},{1,0},{2,3},{3,2},{4,5},{5,4},{6,7},{7,6},{8,9},{9,8},{10,11... | collective-permute-start | bytes 983048 | tf_op jit(solution)/shard_map/ppermute | solution.py:1198
  454.8 22.4 %collective-permute-start.7 = (bf16[3,256,640]{1,2,0:T(8,128)(2,1)}, bf16[3,256,640]{1,2,0:T(8,128)(2,1)}, u32[]{:S(2)}, u32[]{:S(2)}) collective-permute-start(bf16[3,256,640]{1,2,0:T(8,128)(2,1)} %pad_maximum_fusion.2), channel_id=1, source_target_pairs={{0,1},{1,0},{2,3},{3,2},{4,5},{5,4},{6,7},{7,6},{8,9},{9,8},{10,11... | collective-permute-start | bytes 2949128 | tf_op jit(solution)/shard_map/ppermute | solution.py:1198
  487.6 65.4 %collective-permute-start.8 = (bf16[128,640]{1,0:T(8,128)(2,1)S(1)}, bf16[128,640]{1,0:T(8,128)(2,1)S(1)}, u32[]{:S(2)}, u32[]{:S(2)}) collective-permute-start(bf16[128,640]{1,0:T(8,128)(2,1)S(1)} %slice.341), channel_id=1, source_target_pairs={{0,1},{1,0},{2,3},{3,2},{4,5},{5,4},{6,7},{7,6},{8,9},{9,8},{10,11... | collective-permute-start | bytes 491528 | tf_op jit(solution)/shard_map/ppermute | solution.py:1198
  491.5 61.6 %copy-start.7 = (f32[256,1280]{1,0:T(8,128)S(1)}, f32[256,1280]{1,0:T(8,128)}, u32[]{:S(2)}) copy-start(f32[256,1280]{1,0:T(8,128)} %copy-done.6) | copy-start | bytes 3932164
  491.5 61.6 %copy-start.58 = (f32[1280]{0:T(1024)S(1)}, f32[1280]{0:T(1024)}, u32[]{:S(2)}) copy-start(f32[1280]{0:T(1024)} %copy-done.57) | copy-start | bytes 15364
  553.4 2.3 collective-permute-start.9
  (67 other events, 494.0 us)

commit v3 on v2

--- a/solution.py
+++ b/solution.py
@@ -195,8 +195,8 @@
 class Gather:
     NAMES = ("up", "dn", "x", "y", "cx", "cy", "rz", "rx", "ry", "rcx", "rcy")
 
-    def __init__(self, at, sibling, pairs, sems):
-        self.at, self.sibling, self.pairs = at, sibling, pairs
+    def __init__(self, at, sibling, pairs, sems, keeps_own=True):
+        self.at, self.sibling, self.pairs, self.keeps_own = at, sibling, pairs, keeps_own
         self.own_sem = sems[0]
         self.sems = dict(zip(self.NAMES, sems[1:12]))
         self.send_n, self.recv_n = sems[12:]
@@ -292,7 +292,8 @@
         start(self.over_y(at.level, at.spot, own=True))
         if self.sibling:
             start(self.near(at.level, at.spot, own=True))
-        start(self.own_copies())
+        if self.keeps_own:
+            start(self.own_copies())
 
     def take_column(self, lev):
         at = self.at
@@ -403,20 +404,24 @@
     return lax.dot_general(left, right, (((1,), (0,)), ((), ())), preferred_element_type=F32)
 
 
+def dot_tn(left, right):
+    return lax.dot_general(left, right, (((0,), (0,)), ((), ())), preferred_element_type=F32)
+
+
 def dot_nt(left, right):
     return lax.dot_general(left, right, (((1,), (1,)), ((), ())), preferred_element_type=F32)
 
 
 def experts_kernel(
-    levels, sizes, x_ref, grads_ref, marks_ref, gate_ref, down_ref,
-    rows_ref, mixed_ref, act_ref, back_ref, out_ref, gm_ref,
+    levels, sizes, x_ref, g_ref, m_ref, gate_ref, down_ref,
+    rows_ref, grads_ref, marks_ref, back_ref, out_ref, gm_ref, dgate_ref, dup_ref, ddown_ref, shared_ref,
     x_buf, g_buf, mark_buf, cu_buf, g_val, mixed_buf, act_buf, back_buf, out_buf, gm_buf, mark_t,
-    in_sem, out_sem, gm_val, *sems,
+    in_sem, out_sem, gm_val, gw_ref, gd_ref, *sems,
 ):
     hidden, used, full = sizes
     at = Place(levels)
     at.enter(True)
-    gather = Gather(at, True, [(x_ref, rows_ref)], sems)
+    gather = Gather(at, True, [(x_ref, rows_ref), (g_ref, grads_ref), (m_ref, marks_ref)], sems, False)
     gather.begin()
     place = at.level * 4 + at.spot
     units = 4 * levels
@@ -456,7 +461,7 @@
     def stores(k, first):
         slot = lax.rem(k, 2)
         rng = pl.ds(pl.multiple_of(first * rows, batch), batch)
-        pairs = [(mixed_buf, mixed_ref), (act_buf, act_ref), (back_buf, back_ref), (out_buf, out_ref)]
+        pairs = [(back_buf, back_ref), (out_buf, out_ref)]
         return [
             pltpu.make_async_copy(buf.at[slot], ref.at[rng], out_sem.at[slot, n])
             for n, (buf, ref) in enumerate(pairs)
@@ -473,6 +478,16 @@
         lev, sp, _ = unit(k)
         gather.take_near(lev, sp)
         start(loads(k, (lev * 4 + sp) * 2))
+
+    def fetch_own():
+        gather.take_near(at.level, at.spot)
+        theirs = 1 - at.core
+        triples = [(x_ref, rows_ref, x_buf), (g_ref, grads_ref, g_buf), (m_ref, marks_ref, mark_buf)]
+        for n, (own, gathered, buf) in enumerate(triples):
+            sem = in_sem.at[0, n]
+            other = gathered.at[place * 2 + theirs]
+            pltpu.make_async_copy(own, buf.at[0, at.core], sem).start()
+            pltpu.make_async_copy(other, buf.at[0, theirs], sem).start()
 
     def lanes(n):
         return lax.broadcasted_iota(jnp.int32, (batch, 128), 1) + n * 128
@@ -486,7 +501,7 @@
         mine = jnp.where((lanes(tail) == used + place) & (mark > 1.5), weight, 0.0)
         return jnp.sum(mine, axis=1, keepdims=True) / jnp.sum(weight, axis=1, keepdims=True)
 
-    def elementwise(slot):
+    def elementwise():
         mix = jnp.broadcast_to(mixing(), (batch, 128))
         total = jnp.zeros((batch, 128), F32)
         for n in range(full // 128):
@@ -502,14 +517,14 @@
             active = act * upper
             grad_act = scale * back
             slope = sig * (1.0 + gate * (1.0 - sig))
-            mixed_buf[slot, :, cols] = (scale * active).astype(BF16)
-            act_buf[slot, :, cols] = (grad_act * upper * slope).astype(BF16)
-            act_buf[slot, :, up_cols] = (grad_act * act).astype(BF16)
+            mixed_buf[:, cols] = (scale * active).astype(BF16)
+            act_buf[:, cols] = (grad_act * upper * slope).astype(BF16)
+            act_buf[:, up_cols] = (grad_act * act).astype(BF16)
             term = active * back
             total = total + (term if whole else jnp.where(lanes(n) < hidden, term, 0.0))
         gm_buf[...] = total
 
-    def compute(k):
+    def forward(k):
         lev, sp, _ = unit(k)
         first = (lev * 4 + sp) * 2
         slot = lax.rem(k, 2)
@@ -523,40 +538,61 @@
             above = jnp.zeros((used - (full - 128), 128), F32)
             below = jnp.zeros((full - used - marks.shape[0], 128), F32)
             mark_t[pl.ds(n * rows, rows), :] = jnp.transpose(jnp.concatenate([above, marks, below], axis=0))
+        elementwise()
+
+    def backward(k):
+        lev, sp, _ = unit(k)
+        first = (lev * 4 + sp) * 2
+        slot = lax.rem(k, 2)
 
         @pl.when(k >= 2)
         def _():
             for copy in stores(k, 0):
                 copy.wait()
 
-        elementwise(slot)
-        back_buf[slot] = dot_nt(act_buf[slot], gate_ref[...]).astype(BF16)
-        out_buf[slot] = dot_nn(mixed_buf[slot], down_ref[...]).astype(BF16)
+        back_buf[slot] = dot_nt(act_buf[...], gate_ref[...]).astype(BF16)
+        out_buf[slot] = dot_nn(mixed_buf[...], down_ref[...]).astype(BF16)
         for n in range(2):
             gm = jnp.transpose(gm_buf[pl.ds(n * rows, rows), :])
             gm_val[pl.ds(first + n, 1), :] = jnp.sum(gm, axis=0, keepdims=True)
         start(stores(k, first))
 
-    gather.take_own()
-    fetch(0)
+        def gate_grad(m, carry):
+            part = pl.ds(pl.multiple_of(m * 256, 256), 256)
+            x = x_buf[slot, :, :, part].reshape(batch, 256)
+            gw_ref[part, :] += dot_tn(x, act_buf[...])
+            return carry
+
+        def down_grad(m, carry):
+            part = pl.ds(pl.multiple_of(m * 256, 256), 256)
+            gd_ref[part, :] += dot_tn(mixed_buf[:, part], g_buf[slot].reshape(batch, -1))
+            return carry
+
+        lax.fori_loop(0, gw_ref.shape[0] // 256, gate_grad, 0)
+        lax.fori_loop(0, full // 256, down_grad, 0)
+
+    gw_ref[...] = jnp.zeros_like(gw_ref)
+    gd_ref[...] = jnp.zeros_like(gd_ref)
+    fetch_own()
 
     def loop(k, carry):
-        @pl.when((k > 0) & (k + 1 < units))
-        def _():
-            serve(k + 1)
-            fetch(k + 1)
-
-        compute(k)
-
-        @pl.when(k == 0)
-        def _():
-            serve(1)
-            fetch(1)
-
+        pl.when((k > 0) & (k + 1 < units))(lambda: serve(k + 1))
+        forward(k)
+        pl.when(k == 0)(lambda: serve(1))
+        pl.when(k + 1 < units)(lambda: fetch(k + 1))
+        backward(k)
         return carry
 
     lax.fori_loop(0, units, loop, 0)
     gm_ref[...] = gm_val[...]
+    dgate_ref[...] = gw_ref[:, :hidden]
+    dup_ref[...] = gw_ref[:, full : full + hidden]
+    ddown_ref[...] = gd_ref[:hidden, :]
+    size, skip = used - hidden, hidden - (full - 128)
+    for n in range(2):
+        turned = jnp.transpose(gw_ref[:, (n + 1) * full - 128 : (n + 1) * full])
+        shared_ref[n * size : (n + 1) * size, :] = turned[skip : skip + size, :].astype(BF16)
+    shared_ref[2 * size :, :] = gd_ref[hidden:used, :].astype(BF16)
     for k in (0, 1):
         for copy in stores(k, 0):
             copy.wait()
@@ -578,37 +614,90 @@
         functools.partial(experts_kernel, levels, (hidden, used, full)),
         out_shape=[
             shape((blocks, rows, width), BF16),
-            shape((total, full), BF16),
-            shape((total, 2 * full), BF16),
+            shape((blocks, rows, width), BF16),
+            shape((blocks, *marks.shape), F32),
             shape((total, width), BF16),
             shape((total, width), BF16),
             shape((blocks, rows), F32),
+            shape((width, hidden), F32),
+            shape((width, hidden), F32),
+            shape((hidden, width), F32),
+            shape((3 * (used - hidden), width), BF16),
         ],
         in_specs=[anywhere, anywhere, anywhere, inside, inside],
-        out_specs=[anywhere] * 5 + [inside],
+        out_specs=[anywhere] * 5 + [inside] * 5,
         scratch_shapes=[
             vmem((2, 2, rows, width), BF16),
             vmem((2, 2, rows, width), BF16),
-            vmem((2, 2, *marks.shape[1:]), F32),
+            vmem((2, 2, *marks.shape), F32),
             vmem((batch, 2 * full), F32),
             vmem((batch, full), F32),
-            vmem((2, batch, full), BF16),
-            vmem((2, batch, 2 * full), BF16),
+            vmem((batch, full), BF16),
+            vmem((batch, 2 * full), BF16),
             vmem((2, batch, width), BF16),
             vmem((2, batch, width), BF16),
             vmem((batch, 128), F32),
             vmem((batch, 128), F32),
             dma((2, 3)),
-            dma((2, 4)),
+            dma((2, 2)),
             vmem((blocks, rows), F32),
+            vmem((width, 2 * full), F32),
+            vmem((full, width), F32),
         ]
-        + Gather.scratch(levels, 1),
+        + Gather.scratch(levels, 3),
         compiler_params=pltpu.CompilerParams(
             collective_id=collective_id,
             has_side_effects=True,
             vmem_limit_bytes=56 * 1024 * 1024,
         ),
     )(x, grads, marks, gate_up, down)
+
+
+def shared_kernel(slices, x_ref, gate_ref, up_ref, down_ref, gate_buf, up_buf, down_buf, sem):
+    part, units = gate_ref.shape
+    stored = units // 2
+    size = stored // slices
+    copies = []
+    for n in range(slices):
+        for c in range(2):
+            rows = pl.ds(c * stored + n * size, size)
+            src = x_ref.at[n, pl.ds(c * size, size)]
+            for buf, lanes in ((gate_buf, pl.ds(0, part)), (up_buf, pl.ds(part, part))):
+                copies.append(pltpu.make_async_copy(src.at[:, lanes], buf.at[rows], sem.at[len(copies)]))
+        src, dst = x_ref.at[n, pl.ds(2 * size, size)], down_buf.at[pl.ds(n * size, size)]
+        copies.append(pltpu.make_async_copy(src, dst, sem.at[len(copies)]))
+    start(copies)
+    for copy in copies:
+        copy.wait()
+    down_ref[...] = down_buf[...].astype(F32)
+    for buf, ref in ((gate_buf, gate_ref), (up_buf, up_ref)):
+        for n in range(units // 128):
+            rows = pl.ds(n * 128, 128)
+            ref[:, rows] = jnp.transpose(buf[rows, :].astype(F32))
+
+
+def shared_grads(gathered, slices, part, stored):
+    width = gathered.shape[2]
+    vmem = pltpu.VMEM
+    inside = pl.BlockSpec(memory_space=vmem)
+    shape = jax.ShapeDtypeStruct
+    return pl.pallas_call(
+        functools.partial(shared_kernel, slices),
+        out_shape=[
+            shape((part, 2 * stored), F32),
+            shape((part, 2 * stored), F32),
+            shape((stored, width), F32),
+        ],
+        in_specs=[pl.BlockSpec(memory_space=pl.ANY)],
+        out_specs=[inside] * 3,
+        scratch_shapes=[
+            vmem((2 * stored, part), BF16),
+            vmem((2 * stored, part), BF16),
+            vmem((stored, width), BF16),
+            pltpu.SemaphoreType.DMA((5 * slices,)),
+        ],
+        compiler_params=pltpu.CompilerParams(vmem_limit_bytes=32 * 1024 * 1024),
+    )(gathered)
 
 
 def destinations(levels):
@@ -642,187 +731,195 @@
     return write
 
 
-def scatter_kernel(levels, sibling, x_ref, out_ref, acc, near, hx, hy, fx, fy, out_buf, za, zb, *sems):
-    send_n, recv_n = sems[:2]
-    send_hx, send_hy, send_fx, send_fy, send_up, send_dn = sems[2:8]
-    recv_hx, recv_hy, recv_fx, recv_fy, recv_za, recv_zb = sems[8:]
-    at = Place(levels)
-    level, spot, core = at.level, at.spot, at.core
-    across, along, corner = at.across, at.along, at.corner
-    rows = out_ref.shape[0]
-    half = rows // 2
-    first, second = pl.ds(0, half), pl.ds(half, half)
-    at.enter(sibling)
-    table = destinations(levels)
-
-    order = [at.choose([row[s] for row in table]) for s in range(levels)]
-
-    def to_sibling(lev, sp):
+class Scatter:
+    def __init__(self, at, sibling, x_ref, out_ref, refs):
+        self.at, self.sibling, self.x_ref, self.out_ref = at, sibling, x_ref, out_ref
+        self.acc, self.near, self.hx, self.hy, self.fx, self.fy = refs[:6]
+        self.out_buf, self.za, self.zb = refs[6:9]
+        self.own_sem, self.send_n, self.recv_n = refs[9:12]
+        self.send = dict(zip(("hx", "hy", "fx", "fy", "up", "dn"), refs[12:18]))
+        self.recv = dict(zip(("hx", "hy", "fx", "fy", "za", "zb"), refs[18:24]))
+        self.rows = out_ref.shape[0]
+        table = destinations(at.levels)
+        self.order = [at.choose([row[s] for row in table]) for s in range(at.levels)]
+
+    SCRATCH = 24
+
+    @staticmethod
+    def scratch(levels, sibling, rows, width):
+        dma, vmem = pltpu.SemaphoreType.DMA, pltpu.VMEM
+        blocks = levels * 4
+        return (
+            [
+                vmem((blocks, rows, width), BF16),
+                vmem((blocks if sibling else 1, rows, width), BF16),
+                vmem((levels, rows // 2, width), BF16),
+                vmem((levels, rows // 2, width), BF16),
+            ]
+            + [vmem((levels, rows, width), BF16)] * 5
+            + [dma((blocks,))] * 3
+            + [dma((levels,))] * 12
+        )
+
+    def own(self, lev, sp):
         b = lev * 4 + sp
-        src = x_ref.at[b * 2 + 1 - core]
-        return remote(
-            src, near.at[b], send_n.at[b], recv_n.at[b], at.device(level, spot, 1 - core)
-        )
-
-    def half_y(lev):
-        src = acc.at[lev * 4 + corner].at[first]
-        return remote(
-            src, hy.at[lev], send_hy.at[lev], recv_hy.at[lev], at.device(level, along)
-        )
-
-    def half_x(lev):
-        src = acc.at[lev * 4 + corner].at[second]
-        return remote(
-            src, hx.at[lev], send_hx.at[lev], recv_hx.at[lev], at.device(level, across)
-        )
-
-    def full_x(lev):
-        src = acc.at[lev * 4 + across]
-        return remote(
-            src, fx.at[lev], send_fx.at[lev], recv_fx.at[lev], at.device(level, across)
-        )
-
-    def full_y(lev):
-        src = acc.at[lev * 4 + along]
-        return remote(
-            src, fy.at[lev], send_fy.at[lev], recv_fy.at[lev], at.device(level, along)
-        )
-
-    def go_up(lev):
-        sems = send_up.at[lev], recv_zb.at[lev]
-        return remote(out_buf.at[lev], zb.at[lev], *sems, at.device(level + 1, spot))
-
-    def go_down(lev):
-        sems = send_dn.at[lev], recv_za.at[lev]
-        return remote(out_buf.at[lev], za.at[lev], *sems, at.device(level - 1, spot))
-
-    if sibling:
-        for lev in order:
-            for sp in (corner, across, along, spot):
-                to_sibling(lev, sp).start()
-
-    def local(lev):
-        for n, sp in enumerate((corner, across, along, spot)):
-            b = lev * 4 + sp
-            if sibling:
-                to_sibling(lev, sp).wait_recv()
-                add_rows(writes(acc.at[b]), [reads(x_ref.at[b * 2 + core]), reads(near.at[b])], rows)
-            else:
-                add_rows(writes(acc.at[b]), [reads(x_ref.at[b])], rows)
+        src = self.x_ref.at[b * 2 + self.at.core if self.sibling else b]
+        return pltpu.make_async_copy(src, self.acc.at[b], self.own_sem.at[b])
+
+    def to_sibling(self, lev, sp):
+        at, b = self.at, lev * 4 + sp
+        sems = self.send_n.at[b], self.recv_n.at[b]
+        src = self.x_ref.at[b * 2 + 1 - at.core]
+        return remote(src, self.near.at[b], *sems, at.device(at.level, at.spot, 1 - at.core))
+
+    def side(self, name, src, dst, lev, spot):
+        sems = self.send[name].at[lev], self.recv[name].at[lev]
+        return remote(src, dst, *sems, self.at.device(self.at.level, spot))
+
+    def half_y(self, lev):
+        src = self.acc.at[lev * 4 + self.at.corner].at[pl.ds(0, self.rows // 2)]
+        return self.side("hy", src, self.hy.at[lev], lev, self.at.along)
+
+    def half_x(self, lev):
+        src = self.acc.at[lev * 4 + self.at.corner].at[pl.ds(self.rows // 2, self.rows // 2)]
+        return self.side("hx", src, self.hx.at[lev], lev, self.at.across)
+
+    def full_x(self, lev):
+        return self.side("fx", self.acc.at[lev * 4 + self.at.across], self.fx.at[lev], lev, self.at.across)
+
+    def full_y(self, lev):
+        return self.side("fy", self.acc.at[lev * 4 + self.at.along], self.fy.at[lev], lev, self.at.along)
+
+    def go_up(self, lev):
+        sems = self.send["up"].at[lev], self.recv["zb"].at[lev]
+        device = self.at.device(self.at.level + 1, self.at.spot)
+        return remote(self.out_buf.at[lev], self.zb.at[lev], *sems, device)
+
+    def go_down(self, lev):
+        sems = self.send["dn"].at[lev], self.recv["za"].at[lev]
+        device = self.at.device(self.at.level - 1, self.at.spot)
+        return remote(self.out_buf.at[lev], self.za.at[lev], *sems, device)
+
+    def spots(self):
+        return self.at.corner, self.at.across, self.at.along, self.at.spot
+
+    def begin(self):
+        for lev in self.order:
+            for sp in self.spots():
+                if self.sibling:
+                    self.to_sibling(lev, sp).start()
+                self.own(lev, sp).start()
+
+    def local(self, lev):
+        for n, sp in enumerate(self.spots()):
+            ref = self.acc.at[lev * 4 + sp]
+            self.own(lev, sp).wait()
+            if self.sibling:
+                self.to_sibling(lev, sp).wait_recv()
+                add_rows(writes(ref), [reads(ref), reads(self.near.at[lev * 4 + sp])], self.rows)
             if n == 0:
-                half_y(lev).start()
-                half_x(lev).start()
-
-    def halves(lev):
-        half_y(lev).wait_recv()
-        ref = acc.at[lev * 4 + across].at[first]
-        add_rows(writes(ref), [reads(ref), reads(hy.at[lev])], half)
-        full_x(lev).start()
-        half_x(lev).wait_recv()
-        ref = acc.at[lev * 4 + along].at[second]
-        add_rows(writes(ref), [reads(ref), reads(hx.at[lev])], half)
-        full_y(lev).start()
-
-    def column(lev):
-        full_x(lev).wait_recv()
-        full_y(lev).wait_recv()
-        own = [reads(acc.at[lev * 4 + spot]), reads(fx.at[lev]), reads(fy.at[lev])]
-        above, below = reads(za.at[lev]), reads(zb.at[lev])
-
-        @pl.when(lev < level)
-        def _():
-            @pl.when(at.has_up)
+                self.half_y(lev).start()
+                self.half_x(lev).start()
+
+    def halves(self, lev):
+        half = self.rows // 2
+        self.half_y(lev).wait_recv()
+        ref = self.acc.at[lev * 4 + self.at.across].at[pl.ds(0, half)]
+        add_rows(writes(ref), [reads(ref), reads(self.hy.at[lev])], half)
+        self.full_x(lev).start()
+        self.half_x(lev).wait_recv()
+        ref = self.acc.at[lev * 4 + self.at.along].at[pl.ds(half, half)]
+        add_rows(writes(ref), [reads(ref), reads(self.hx.at[lev])], half)
+        self.full_y(lev).start()
+
+    def column(self, lev):
+        at, rows, level = self.at, self.rows, self.at.level
+        self.full_x(lev).wait_recv()
+        self.full_y(lev).wait_recv()
+        own = [reads(self.acc.at[lev * 4 + at.spot]), reads(self.fx.at[lev]), reads(self.fy.at[lev])]
+        above, below = reads(self.za.at[lev]), reads(self.zb.at[lev])
+        passed = writes(self.out_buf.at[lev])
+        final = writes(self.out_ref)
+
+        def send(has, arrival, term, departure):
+            @pl.when(has)
             def _():
-                go_down(lev).wait_recv()
-                add_rows(writes(out_buf.at[lev]), [*own, above], rows)
-
-            @pl.when(jnp.logical_not(at.has_up))
-            def _():
-                add_rows(writes(out_buf.at[lev]), own, rows)
-
-            go_down(lev).start()
-
-        @pl.when(lev > level)
-        def _():
-            @pl.when(at.has_down)
-            def _():
-                go_up(lev).wait_recv()
-                add_rows(writes(out_buf.at[lev]), [*own, below], rows)
-
-            @pl.when(jnp.logical_not(at.has_down))
-            def _():
-                add_rows(writes(out_buf.at[lev]), own, rows)
-
-            go_up(lev).start()
+                arrival(lev).wait_recv()
+                add_rows(passed, [*own, term], rows)
+
+            pl.when(jnp.logical_not(has))(lambda: add_rows(passed, own, rows))
+            departure(lev).start()
+
+        pl.when(lev < level)(lambda: send(at.has_up, self.go_down, above, self.go_down))
+        pl.when(lev > level)(lambda: send(at.has_down, self.go_up, below, self.go_up))
 
         @pl.when(lev == level)
         def _():
-            pl.when(at.has_up)(lambda: go_down(lev).wait_recv())
-            pl.when(at.has_down)(lambda: go_up(lev).wait_recv())
-
-            @pl.when(at.has_up & at.has_down)
-            def _():
-                add_rows(writes(out_ref), [*own, above, below], rows)
-
-            @pl.when(jnp.logical_not(at.has_down))
-            def _():
-                add_rows(writes(out_ref), [*own, above], rows)
-
-            @pl.when(jnp.logical_not(at.has_up))
-            def _():
-                add_rows(writes(out_ref), [*own, below], rows)
-
-    for s in range(levels + 2):
-        if s < levels:
-            local(order[s])
-        if 0 <= s - 1 < levels:
-            halves(order[s - 1])
-        if s >= 2:
-            column(order[s - 2])
-    for lev in range(levels):
-        if sibling:
-            for sp in range(4):
-                to_sibling(lev, sp).wait_send()
-        half_y(lev).wait_send()
-        half_x(lev).wait_send()
-        full_x(lev).wait_send()
-        full_y(lev).wait_send()
-
-        @pl.when(lev < level)
-        def _():
-            go_down(lev).wait_send()
-
-        @pl.when(lev > level)
-        def _():
-            go_up(lev).wait_send()
-
-
-def scatter_wide(x, levels, sibling, collective_id):
-    dma = pltpu.SemaphoreType.DMA
-    blocks = levels * 4
-    rows, width = x.shape[1:]
-    vmem = pltpu.VMEM
-    inside = pl.BlockSpec(memory_space=vmem)
+            pl.when(at.has_up)(lambda: self.go_down(lev).wait_recv())
+            pl.when(at.has_down)(lambda: self.go_up(lev).wait_recv())
+            both = at.has_up & at.has_down
+            pl.when(both)(lambda: add_rows(final, [*own, above, below], rows))
+            pl.when(jnp.logical_not(at.has_down))(lambda: add_rows(final, [*own, above], rows))
+            pl.when(jnp.logical_not(at.has_up))(lambda: add_rows(final, [*own, below], rows))
+
+    def steps(self):
+        levels, steps = self.at.levels, []
+        for s in range(levels + 2):
+            if s < levels:
+                steps.append(lambda lev=self.order[s]: self.local(lev))
+            if 0 <= s - 1 < levels:
+                steps.append(lambda lev=self.order[s - 1]: self.halves(lev))
+            if s >= 2:
+                steps.append(lambda lev=self.order[s - 2]: self.column(lev))
+        return steps
+
+    def finish(self):
+        for lev in range(self.at.levels):
+            if self.sibling:
+                for sp in range(4):
+                    self.to_sibling(lev, sp).wait_send()
+            sent([self.half_y(lev), self.half_x(lev), self.full_x(lev), self.full_y(lev)])
+            pl.when(lev < self.at.level)(lambda lev=lev: self.go_down(lev).wait_send())
+            pl.when(lev > self.at.level)(lambda lev=lev: self.go_up(lev).wait_send())
+
+
+def scatter_kernel(levels, sibling, lag, count, *refs):
+    x_refs, refs = refs[:count], refs[count:]
+    out_refs, refs = refs[:count], refs[count:]
+    at = Place(levels)
+    at.enter(sibling)
+    size = Scatter.SCRATCH
+    tasks = [
+        Scatter(at, sibling, x_refs[n], out_refs[n], refs[n * size : (n + 1) * size])
+        for n in range(count)
+    ]
+    for task in tasks:
+        task.begin()
+    order = [
+        (s + n * lag, n, step) for n, task in enumerate(tasks) for s, step in enumerate(task.steps())
+    ]
+    for _, _, step in sorted(order, key=lambda entry: entry[:2]):
+        step()
+    for task in tasks:
+        task.finish()
+
+
+def scatter_wide(arrays, levels, sibling, collective_id):
+    rows, width = arrays[0].shape[1:]
+    anywhere, inside = pl.BlockSpec(memory_space=pl.ANY), pl.BlockSpec(memory_space=pltpu.VMEM)
+    count = len(arrays)
     return pl.pallas_call(
-        functools.partial(scatter_kernel, levels, sibling),
-        out_shape=jax.ShapeDtypeStruct((rows, width), BF16),
-        in_specs=[inside],
-        out_specs=inside,
-        scratch_shapes=[
-            vmem((blocks, rows, width), BF16),
-            vmem((blocks if sibling else 1, rows, width), BF16),
-            vmem((levels, rows // 2, width), BF16),
-            vmem((levels, rows // 2, width), BF16),
-        ]
-        + [vmem((levels, rows, width), BF16)] * 5
-        + [dma((blocks,))] * 2
-        + [dma((levels,))] * 12,
+        functools.partial(scatter_kernel, levels, sibling, 7, count),
+        out_shape=[jax.ShapeDtypeStruct((rows, width), BF16)] * count,
+        in_specs=[anywhere] * count,
+        out_specs=[inside] * count,
+        scratch_shapes=Scatter.scratch(levels, sibling, rows, width) * count,
         compiler_params=pltpu.CompilerParams(
             collective_id=collective_id,
             has_side_effects=True,
             vmem_limit_bytes=60 * 1024 * 1024,
         ),
-    )(x)
+    )(*arrays)
 
 
 def slots_path(
@@ -1214,7 +1311,6 @@
         jnp.int32
     )
     marks = jnp.sum(picks * (1 + keep)[:, :, None], axis=1).astype(F32)
-    all_grads, all_marks = gather_wide([cotangent, marks.T], levels, True, 0)
 
     first_unit = place * slice_width
     holds = place < slices
@@ -1274,10 +1370,10 @@
     gate_all = pad(jnp.concatenate([expert_gate[0], gate_slice, router], axis=1), full, 1)
     up_all = pad(jnp.concatenate([expert_up[0], up_slice], axis=1), full, 1)
     down_all = pad(jnp.concatenate([expert_down[0], down_slice], axis=0), full, 0)
-    all_rows, mixed, act, grad_rows, expert_out, grad_mix = experts_rows(
+    (_, _, _, grad_rows, expert_out, grad_mix, *expert_grads, shared_part) = experts_rows(
         normed_two,
-        all_grads,
-        all_marks,
+        cotangent,
+        marks.T,
         jnp.concatenate([gate_all, up_all], axis=1),
         down_all,
         hidden_part,
@@ -1285,8 +1381,6 @@
         levels,
         1,
     )
-    all_rows = all_rows.reshape(-1, width)
-    all_grads = all_grads.reshape(-1, width)
     grad_mix = lax.all_to_all(
         grad_mix.reshape(wide_size, 2, local_rows), "wide", split_axis=0, concat_axis=0, tiled=True
     )
@@ -1294,15 +1388,12 @@
     send_core = jnp.where(core == 0, grad_mix[:, 1], grad_mix[:, 0])
     grad_mix = (pick_core + swap(send_core)).T
     block_shape = (2 * wide_size, local_rows, width)
-    grad_rows = scatter_wide(grad_rows.reshape(block_shape), levels, True, 2)
-    expert_out = scatter_wide(expert_out.reshape(block_shape), levels, True, 3)
+    grad_rows, expert_out = scatter_wide(
+        [grad_rows.reshape(block_shape), expert_out.reshape(block_shape)], levels, True, 2
+    )
     output = (hidden + expert_out.astype(F32)).astype(BF16)
-    grad_expert_gate = matmul_left(all_rows, act[:, :hidden_part])
-    grad_expert_up = matmul_left(all_rows, act[:, full : full + hidden_part])
-    grad_expert_down = matmul_left(mixed[:, :hidden_part], all_grads)
-    shared_act = jnp.concatenate([act[:, hidden_part:used], act[:, full + hidden_part : full + used]], 1)
-    shared_t = matmul_left(shared_act, all_rows).astype(BF16)
-    shared_down_grad = matmul_left(mixed[:, hidden_part:used], all_grads).astype(BF16)
+    grad_expert_gate, grad_expert_up, grad_expert_down = expert_grads
+    shared_t, shared_down_grad = shared_part[: 2 * slice_width], shared_part[2 * slice_width :]
     theirs = swap(columns(shared_t, 1 - core, part))
     shared_t = columns(shared_t, core, part)
 
@@ -1313,11 +1404,9 @@
         [in_order(side_by_side(shared_t), side_by_side(theirs), 0), shared_down_grad], axis=0
     )
     (shared_all,) = gather_wide([shared_block], levels, False, 4)
-    shared_all = shared_all[:slices].astype(F32)
-    pair = shared_all[:, : 2 * slice_width].reshape(slices, 2, slice_width, 2, part)
-    grad_shared_gate = pair[:, :, :, 0].transpose(3, 1, 0, 2).reshape(part, 2 * stored)
-    grad_shared_up = pair[:, :, :, 1].transpose(3, 1, 0, 2).reshape(part, 2 * stored)
-    grad_shared_down = shared_all[:, 2 * slice_width :].reshape(stored, width)
+    grad_shared_gate, grad_shared_up, grad_shared_down = shared_grads(
+        shared_all, slices, part, stored
+    )
 
     marks = marks.astype(F32)
     routed = marks > 0.0
@@ -1367,12 +1456,10 @@
     extra_rows = -(-size // (width * 16)) * 16
     flat = jnp.concatenate([small.reshape(-1), jnp.zeros((extra_rows * width - size,), BF16)])
     sum_rows = 4 * part // wide_size
-    summed = scatter_wide(grad_dense.reshape(wide_size, sum_rows, width), levels, False, 5)
-    (everything,) = gather_wide(
-        [jnp.concatenate([summed, flat.reshape(extra_rows, width)], axis=0)], levels, False, 6
-    )
-    owned = everything[:, :sum_rows].reshape(4, part, width)
-    flat = everything[:, sum_rows:].astype(F32).reshape(wide_size, -1)
+    (summed,) = scatter_wide([grad_dense.reshape(wide_size, sum_rows, width)], levels, False, 5)
+    everything, flat = gather_wide([summed, flat.reshape(extra_rows, width)], levels, False, 6)
+    owned = everything.reshape(4, part, width)
+    flat = flat.astype(F32).reshape(wide_size, -1)
     small = jnp.sum(flat[:, :size], axis=0).reshape(part, 2 + experts)
     return (
         output,

time: 652 us -> 558 us (0.86)
  matrix products: 62.9 us -> 19.1 us
  local copies, waits for them, and re-layouts: 96.2 us -> 73.1 us
  Pallas kernels: 428 us -> 407 us
    pallas_call x3 -> x2, Pallas kernels: 154 us -> 110 us  [gather_wide(): pl.pallas_call(functools.partial(gather_kernel, levels, sibling, len(arra...]
    dot_general x10 -> x5, matrix products: 46.8 us -> 3.65 us  [matmul_left(): lax.dot_general(left, right, (((0,), (0,)), ((), ())), preferred_element_...]
    pallas_call x1, Pallas kernels: 101 us -> 138 us  [experts_rows(): pl.pallas_call(functools.partial(experts_kernel, levels, (hidden, used, f...]
    slice x6 -> x2, local copies, waits for them, and re-layouts: 17.1 us -> 0.02 us  [the longest x1 0.01 us: tokens_path(): shared_part[:2 * slice_width]]
    pallas_call x3, Pallas kernels: 173 us -> 159 us  [the longest x2 153 us: scatter_wide(): pl.pallas_call(functools.partial(scatter_kernel, levels, sibling, 7, coun...]
    unnamed x167 -> x146, local copies, waits for them, and re-layouts: 31 us -> 38.5 us
  transfers between devices with their start and end apart: 12 -> 12, of which waited for: 2 -> 1; matrix products, arithmetic and copies ran while one was open for 13% -> 11% of each run, Pallas kernels for 41% -> 37%
where the time goes in v3:
time: 558 us; the launch traced here: 553 us
  Pallas kernels  407 us (73%)
  local copies, waits for them, and re-layouts  73.1 us (13%)
  other arithmetic  37.6 us (7%)
  matrix products  19.1 us (3%)
  starting transfers between devices  8.06 us (1%)
  waiting for transfers between devices  5.92 us (1%)
    pallas_call x2, Pallas kernels, scatter_wide(): pl.pallas_call(functools.partial(scatter_kernel, levels, sibling, 7, coun...  153 us
    pallas_call x1, Pallas kernels, experts_rows(): pl.pallas_call(functools.partial(experts_kernel, levels, (hidden, used, f...  138 us
    pallas_call x2, Pallas kernels, gather_wide(): pl.pallas_call(functools.partial(gather_kernel, levels, sibling, len(arra...  110 us
    unnamed x146, local copies, waits for them, and re-layouts  38.5 us
  transfers between devices with their start and end apart: 12, of which 1 were waited for; matrix products, arithmetic and copies ran while one was open for 11% of the time, Pallas kernels for 37%

profile of v3, /device:TPU:0, one launch (start us, length us, event | category | flops | bytes accessed | tf_op | source)
XLA Modules:
  0.0 553.2 jit_solution(14698379356663994663)
XLA Ops:
  3.8 2.1 dynamic-slice_select_fusion.2
  23.0 2.4 copy.162
  25.4 2.4 copy.159
  41.0 2.1 copy.193
  57.3 6.3 %concatenate.112.gate_ref = bf16[1280,1024]{1,0:T(8,128)(2,1)} concatenate(bf16[1280,448]{1,0:T(8,128)(2,1)} %bitcast.105, bf16[1280,32]{1,0:T(8,128)(2,1)} %get-tuple-element.167, bf16[1280,16]{1,0:T(8,128)(2,1)} %slice.216, bf16[1280,16]{1,0:T(8,128)(2,1)} %broadcast_in_dim.50, bf16[1280,448]{1,0:T(8,128)(2,1)} %bitcast.104, bf16[1280,32]{1,0:T(8,128)(2,1)} %get-tuple-element.166, ...), dimensions={1} | concatenate | bytes 5242880 | tf_op jit(solution)/shard_map/concatenate | solution.py:1377
  68.0 138.4 %shard_map.289 = (bf16[32,128,1280]{2,1,0:T(8,128)(2,1)}, bf16[32,128,1280]{2,1,0:T(8,128)(2,1)}, f32[32,16,128]{2,1,0:T(8,128)}, bf16[4096,1280]{1,0:T(8,128)(2...) custom-call(bf16[128,1280]{1,0:T(8,128)(2,1)} %multiply_convert_fusi, ...), custom_call_target="tpu_custom_call" | custom-call | tf_op jit(solution)/shard_map/pallas_call | solution.py:613
  206.4 5.8 %all-to-all-start = ((f32[16,2,128]{2,1,0:T(2,128)}), f32[16,2,128]{2,1,0:T(2,128)S(1)}, u32[]{:S(2)}, u32[]{:S(2)}) async-start(f32[16,2,128]{2,1,0:T(2,128)} %bitcast.130), calls=%async_computation | async-start | bytes 32768 | tf_op jit(solution)/shard_map/all_to_all | solution.py:1384
  213.6 5.9 %all-to-all-done = f32[16,2,128]{2,1,0:T(2,128)S(1)} async-done(((f32[16,2,128]{2,1,0:T(2,128)}), f32[16,2,128]{2,1,0:T(2,128)S(1)}, u32[]{:S(2)}, u32[]{:S(2)}) %all-to-all-start) | async-done | bytes 16416 | tf_op jit(solution)/shard_map/all_to_all | solution.py:1384
  219.7 92.7 %shard_map.290 = (bf16[128,1280]{1,0:T(8,128)(2,1)}, bf16[128,1280]{1,0:T(8,128)(2,1)}) custom-call(bf16[32,128,1280]{2,1,0:T(8,128)(2,1)} %bitcast.102, bf16[32,128,1280]{2,1,0:T(8,128)(2,1)} %bitcast.103), custom_call_target="tpu_custom_call" | custom-call | tf_op jit(solution)/shard_map/pallas_call | solution.py:911
  312.5 2.4 multiply_reduce_fusion.2
  317.6 3.1 copy.179
  320.7 3.1 copy.180
  325.2 2.4 convolution_convert_fusion.6
  337.4 46.0 %shard_map.293.x_ref = bf16[16,96,1280]{2,1,0:T(8,128)(2,1)} custom-call(bf16[96,1280]{1,0:T(8,128)(2,1)} %pad_maximum_fusion.9.refs_0_), custom_call_target="tpu_custom_call" | custom-call | tf_op jit(solution)/shard_map/pallas_call | solution.py:391
  383.4 2.1 copy-done.2
  385.5 6.1 %shard_map.294 = (f32[640,896]{1,0:T(8,128)}, f32[640,896]{1,0:T(8,128)}, f32[448,1280]{1,0:T(8,128)}) custom-call(bf16[16,96,1280]{2,1,0:T(8,128)(2,1)S(1)} %copy-done.2), custom_call_target="tpu_custom_call" | custom-call | tf_op jit(solution)/shard_map/pallas_call | solution.py:684
  394.2 2.9 maximum_select_fusion
  403.1 3.3 pad_maximum_fusion
  406.4 60.6 %shard_map.291.refs_0_ = bf16[160,1280]{1,0:T(8,128)(2,1)} custom-call(bf16[16,160,1280]{2,1,0:T(8,128)(2,1)} %bitcast.101), custom_call_target="tpu_custom_call" | custom-call | tf_op jit(solution)/shard_map/pallas_call | solution.py:911
  470.9 63.5 %shard_map.292 = (bf16[16,160,1280]{2,1,0:T(8,128)(2,1)}, bf16[16,16,1280]{2,1,0:T(8,128)(2,1)}) custom-call(bf16[160,1280]{1,0:T(8,128)(2,1)} %shard_map.291.refs_0_, bf16[16,1280]{1,0:T(8,128)(2,1)} %reshape.336.refs_1_), custom_call_target="tpu_custom_call" | custom-call | tf_op jit(solution)/shard_map/pallas_call | solution.py:391
  537.3 3.4 fusion.42
  540.7 2.1 bitcast_convert_fusion
  542.7 2.1 bitcast_convert_fusion.1
  549.6 3.3 copy.199
  (274 shorter events, 86.7 us)
Async XLA Ops:
  0.6 50.4 %copy-start = (bf16[640,1280]{1,0:T(8,128)(2,1)S(1)}, bf16[640,1280]{1,0:T(8,128)(2,1)}, u32[]{:S(2)}) copy-start(bf16[640,1280]{1,0:T(8,128)(2,1)} %param.27) | copy-start | bytes 4915204
  0.7 6.6 %copy-start.66 = (s32[1,3]{1,0:T(1,128)S(1)}, s32[1,3]{1,0:T(1,128)}, u32[]{:S(2)}) copy-start(s32[1,3]{1,0:T(1,128)} %param.20) | copy-start | bytes 40
  0.7 8.2 %copy-start.62 = (s32[128,7]{0,1:T(8,128)S(1)}, s32[128,7]{0,1:T(8,128)}, u32[]{:S(2)}) copy-start(s32[128,7]{0,1:T(8,128)} %param.22) | copy-start | bytes 10756
  0.7 8.2 %copy-start.8 = (bf16[640,1280]{1,0:T(8,128)(2,1)S(1)}, bf16[640,1280]{1,0:T(8,128)(2,1)}, u32[]{:S(2)}) copy-start(bf16[640,1280]{1,0:T(8,128)(2,1)} %param.24) | copy-start | bytes 4915204
  2.3 11.8 %collective-permute-start.1 = (bf16[2,640]{1,0:T(2,128)(2,1)S(1)}, bf16[2,640]{1,0:T(2,128)(2,1)S(1)}, u32[]{:S(2)}, u32[]{:S(2)}) collective-permute-start(bf16[2,640]{1,0:T(2,128)(2,1)S(1)} %pad_maximum_fusion.14), channel_id=1, source_target_pairs={{0,1},{1,0},{2,3},{3,2},{4,5},{5,4},{6,7},{7,6},{8,9},{9,8},{10,11... | collective-permute-start | bytes 7688 | tf_op jit(solution)/shard_map/ppermute | solution.py:1295
  2.8 11.4 %collective-permute-start = (bf16[128,1280]{1,0:T(8,128)(2,1)}, bf16[128,1280]{1,0:T(8,128)(2,1)}, u32[]{:S(2)}, u32[]{:S(2)}) collective-permute-start(bf16[128,1280]{1,0:T(8,128)(2,1)} %param.18), channel_id=1, source_target_pairs={{0,1},{1,0},{2,3},{3,2},{4,5},{5,4},{6,7},{7,6},{8,9},{9,8},{10,11... | collective-permute-start | bytes 983048 | tf_op jit(solution)/shard_map/ppermute | solution.py:1295
  6.8 21.0 %collective-permute-start.4 = (bf16[640,80]{1,0:T(8,128)(2,1)}, bf16[640,80]{1,0:T(8,128)(2,1)}, u32[]{:S(2)}, u32[]{:S(2)}) collective-permute-start(bf16[640,80]{1,0:T(8,128)(2,1)} %pad_maximum_fusion.10), channel_id=1, source_target_pairs={{0,1},{1,0},{2,3},{3,2},{4,5},{5,4},{6,7},{7,6},{8,9},{9,8},{10,11... | collective-permute-start | bytes 307208 | tf_op jit(solution)/shard_map/ppermute | solution.py:1295
  17.9 11.8 %copy-start.17 = (bf16[256,640]{1,0:T(8,128)(2,1)}, bf16[256,640]{1,0:T(8,128)(2,1)S(1)}, u32[]{:S(2)}) copy-start(bf16[256,640]{1,0:T(8,128)(2,1)S(1)} %fusion.20) | copy-start | bytes 983044
  19.9 9.7 %collective-permute-start.2 = (bf16[256,1920]{1,0:T(8,128)(2,1)}, bf16[256,1920]{1,0:T(8,128)(2,1)S(1)}, u32[]{:S(2)}, u32[]{:S(2)}) collective-permute-start(bf16[256,1920]{1,0:T(8,128)(2,1)} %convolution_convert_fusion.4), channel_id=1, source_target_pairs={{0,1},{1,0},{2,3},{3,2},{4,5},{5,4},{6,7},{7,6},{8,9},{9,8},{10,11... | collective-permute-start | bytes 2949128 | tf_op jit(solution)/shard_map/ppermute | solution.py:1295
  41.0 6.1 %copy-start.48 = (f32[256,64]{1,0:T(8,128)S(1)}, f32[256,64]{1,0:T(8,128)}, u32[]{:S(2)}) copy-start(f32[256,64]{1,0:T(8,128)} %get-tuple-element.179) | copy-start | bytes 196612
  53.6 11.4 %collective-permute-start.3 = (bf16[128,1280]{1,0:T(8,128)(2,1)}, bf16[128,1280]{1,0:T(8,128)(2,1)}, u32[]{:S(2)}, u32[]{:S(2)}) collective-permute-start(bf16[128,1280]{1,0:T(8,128)(2,1)} %slice.275), channel_id=1, source_target_pairs={{0,1},{1,0},{2,3},{3,2},{4,5},{5,4},{6,7},{7,6},{8,9},{9,8},{10,11... | collective-permute-start | bytes 983048 | tf_op jit(solution)/shard_map/ppermute | solution.py:1295
  66.3 248.6 %copy-start.58 = (f32[128]{0:T(128)}, f32[128]{0:T(128)S(1)}, u32[]{:S(2)}) copy-start(f32[128]{0:T(128)S(1)} %add_rsqrt_fusion.1) | copy-start | bytes 1540
  206.4 13.1 %all-to-all-start = ((f32[16,2,128]{2,1,0:T(2,128)}), f32[16,2,128]{2,1,0:T(2,128)S(1)}, u32[]{:S(2)}, u32[]{:S(2)}) async-start(f32[16,2,128]{2,1,0:T(2,128)} %bitcast.130), calls=%async_computation | async-start | bytes 32768 | tf_op jit(solution)/shard_map/all_to_all | solution.py:1384
  219.6 92.9 %collective-permute-start.5 = (f32[16,128]{1,0:T(8,128)S(1)}, f32[16,128]{1,0:T(8,128)S(1)}, u32[]{:S(2)}, u32[]{:S(2)}) collective-permute-start(f32[16,128]{1,0:T(8,128)S(1)} %select_bitcast_fusion), channel_id=1, source_target_pairs={{0,1},{1,0},{2,3},{3,2},{4,5},{5,4},{6,7},{7,6},{8,9},{9,8},{10,11... | collective-permute-start | bytes 24584 | tf_op jit(solution)/shard_map/ppermute | solution.py:1295
  315.7 9.5 %copy-start.35 = (bf16[128,1280]{1,0:T(8,128)(2,1)}, bf16[128,1280]{1,0:T(8,128)(2,1)S(1)}, u32[]{:S(2)}) copy-start(bf16[128,1280]{1,0:T(8,128)(2,1)S(1)} %fusion.40) | copy-start | bytes 983044
  315.7 9.5 %collective-permute-start.6 = (bf16[128,1280]{1,0:T(8,128)(2,1)S(1)}, bf16[128,1280]{1,0:T(8,128)(2,1)}, u32[]{:S(2)}, u32[]{:S(2)}) collective-permute-start(bf16[128,1280]{1,0:T(8,128)(2,1)S(1)} %fusion.40), channel_id=1, source_target_pairs={{0,1},{1,0},{2,3},{3,2},{4,5},{5,4},{6,7},{7,6},{8,9},{9,8},{10,11... | collective-permute-start | bytes 983048 | tf_op jit(solution)/shard_map/ppermute | solution.py:1295
  317.1 18.6 %collective-permute-start.10 = (bf16[64,640]{1,0:T(8,128)(2,1)}, bf16[64,640]{1,0:T(8,128)(2,1)}, u32[]{:S(2)}, u32[]{:S(2)}) collective-permute-start(bf16[64,640]{1,0:T(8,128)(2,1)} %constant_dynamic-slice_fusion), channel_id=1, source_target_pairs={{0,1},{1,0},{2,3},{3,2},{4,5},{5,4},{6,7},{7,6},{8,9},{9,8},{10,11... | collective-permute-start | bytes 245768 | tf_op jit(solution)/shard_map/ppermute | solution.py:1295
  335.5 57.7 %collective-permute-start.7 = (bf16[3,256,640]{1,2,0:T(8,128)(2,1)}, bf16[3,256,640]{1,2,0:T(8,128)(2,1)S(1)}, u32[]{:S(2)}, u32[]{:S(2)}) collective-permute-start(bf16[3,256,640]{1,2,0:T(8,128)(2,1)} %pad_maximum_fusion.2), channel_id=1, source_target_pairs={{0,1},{1,0},{2,3},{3,2},{4,5},{5,4},{6,7},{7,6},{8,9},{9,8},{10,11... | collective-permute-start | bytes 2949128 | tf_op jit(solution)/shard_map/ppermute | solution.py:1295
  385.5 6.1 %copy-start.34 = (bf16[5,128,256]{2,1,0:T(8,128)(2,1)S(1)}, bf16[5,128,256]{2,1,0:T(8,128)(2,1)}, u32[]{:S(2)}) copy-start(bf16[5,128,256]{2,1,0:T(8,128)(2,1)} %copy-done.33) | copy-start | bytes 983044
  385.5 6.1 %copy-start.36 = (bf16[128,1280]{1,0:T(8,128)(2,1)S(1)}, bf16[128,1280]{1,0:T(8,128)(2,1)}, u32[]{:S(2)}) copy-start(bf16[128,1280]{1,0:T(8,128)(2,1)} %copy-done.35) | copy-start | bytes 983044
  403.0 64.1 %collective-permute-start.8 = (bf16[128,640]{1,0:T(8,128)(2,1)S(1)}, bf16[128,640]{1,0:T(8,128)(2,1)S(1)}, u32[]{:S(2)}, u32[]{:S(2)}) collective-permute-start(bf16[128,640]{1,0:T(8,128)(2,1)S(1)} %slice.277), channel_id=1, source_target_pairs={{0,1},{1,0},{2,3},{3,2},{4,5},{5,4},{6,7},{7,6},{8,9},{9,8},{10,11... | collective-permute-start | bytes 491528 | tf_op jit(solution)/shard_map/ppermute | solution.py:1295
  406.4 60.7 %copy-start.7 = (f32[256,1280]{1,0:T(8,128)S(1)}, f32[256,1280]{1,0:T(8,128)}, u32[]{:S(2)}) copy-start(f32[256,1280]{1,0:T(8,128)} %copy-done.6) | copy-start | bytes 3932164
  406.4 60.7 %copy-start.54 = (f32[1280]{0:T(1024)S(1)}, f32[1280]{0:T(1024)}, u32[]{:S(2)}) copy-start(f32[1280]{0:T(1024)} %copy-done.53) | copy-start | bytes 15364
  467.4 2.3 collective-permute-start.9
  (56 other events, 108.4 us)

commit v4 on v3

--- a/solution.py
+++ b/solution.py
@@ -220,14 +220,16 @@
         return [at.choose([row[k] for row in table]) for k in range(at.levels)]
 
     def block(self, n, lev, sp, core=None):
-        ref = self.pairs[n][1]
+        x_ref, ref = self.pairs[n][:2]
         if self.sibling:
             return ref.at[(lev * 4 + sp) * 2 + (self.at.core if core is None else core)]
+        if len(self.pairs[n]) == 3:
+            return ref.at[lev * 4 + sp].at[pl.ds(self.pairs[n][2], x_ref.shape[0])]
         return ref.at[lev * 4 + sp]
 
     def each(self, send, recv, lev, sp, device, part=None, own=False):
         copies = []
-        for n, (x_ref, _) in enumerate(self.pairs):
+        for n, (x_ref, *_) in enumerate(self.pairs):
             dst = self.block(n, lev, sp)
             src = x_ref if own else dst
             if part is not None:
@@ -266,7 +268,7 @@
     def near(self, lev, sp, core=None, own=False):
         at = self.at
         copies = []
-        for n, (x_ref, _) in enumerate(self.pairs):
+        for n, (x_ref, *_) in enumerate(self.pairs):
             dst = self.block(n, lev, sp, core)
             sems = self.send_n.at[n, lev * 4 + sp], self.recv_n.at[n, lev * 4 + sp]
             device = at.device(at.level, at.spot, 1 - at.core)
@@ -277,7 +279,7 @@
         at = self.at
         return [
             pltpu.make_async_copy(x_ref, self.block(n, at.level, at.spot), self.own_sem.at[n])
-            for n, (x_ref, _) in enumerate(self.pairs)
+            for n, (x_ref, *_) in enumerate(self.pairs)
         ]
 
     def take_own(self):
@@ -374,32 +376,6 @@
         copy.wait_send()
 
 
-def gather_kernel(levels, sibling, arrays, *refs):
-    x_refs, out_refs, sems = refs[:arrays], refs[arrays : 2 * arrays], refs[2 * arrays :]
-    at = Place(levels)
-    at.enter(sibling)
-    gather = Gather(at, sibling, list(zip(x_refs, out_refs)), sems)
-    gather.begin()
-    for step in gather.steps():
-        step()
-    gather.finish()
-
-
-def gather_wide(arrays, levels, sibling, collective_id):
-    blocks = levels * 4 * (2 if sibling else 1)
-    anywhere = pl.BlockSpec(memory_space=pl.ANY)
-    return pl.pallas_call(
-        functools.partial(gather_kernel, levels, sibling, len(arrays)),
-        out_shape=[jax.ShapeDtypeStruct((blocks, *x.shape), x.dtype) for x in arrays],
-        in_specs=[anywhere] * len(arrays),
-        out_specs=[anywhere] * len(arrays),
-        scratch_shapes=Gather.scratch(levels, len(arrays)),
-        compiler_params=pltpu.CompilerParams(
-            collective_id=collective_id, has_side_effects=True
-        ),
-    )(*arrays)
-
-
 def dot_nn(left, right):
     return lax.dot_general(left, right, (((1,), (0,)), ((), ())), preferred_element_type=F32)
 
@@ -413,16 +389,34 @@
 
 
 def experts_kernel(
-    levels, sizes, x_ref, g_ref, m_ref, gate_ref, down_ref,
+    levels, sizes, x_ref, g_ref, m_ref, eg_ref, eu_ref, ed_ref, small_ref, sd_ref,
     rows_ref, grads_ref, marks_ref, back_ref, out_ref, gm_ref, dgate_ref, dup_ref, ddown_ref, shared_ref,
     x_buf, g_buf, mark_buf, cu_buf, g_val, mixed_buf, act_buf, back_buf, out_buf, gm_buf, mark_t,
-    in_sem, out_sem, gm_val, gw_ref, gd_ref, *sems,
+    in_sem, out_sem, gm_val, gw_ref, gd_ref, gate_ref, down_ref, w_sem, *sems,
 ):
     hidden, used, full = sizes
     at = Place(levels)
     at.enter(True)
     gather = Gather(at, True, [(x_ref, rows_ref), (g_ref, grads_ref), (m_ref, marks_ref)], sems, False)
     gather.begin()
+    size, experts = used - hidden, m_ref.shape[0]
+    pieces = [
+        (eg_ref, gate_ref, 0, hidden),
+        (eu_ref, gate_ref, full, hidden),
+        (small_ref.at[pl.ds(0, size)], gate_ref, hidden, size),
+        (small_ref.at[pl.ds(size, size)], gate_ref, full + hidden, size),
+        (small_ref.at[pl.ds(2 * size, experts)], gate_ref, used, experts),
+        (ed_ref, down_ref, 0, hidden),
+        (sd_ref, down_ref, hidden, size),
+    ]
+    weights = [
+        pltpu.make_async_copy(src, dst.at[pl.ds(row, count)], w_sem.at[n])
+        for n, (src, dst, row, count) in enumerate(pieces)
+    ]
+    start(weights)
+    for ref, row, end in ((gate_ref, used + experts, full), (gate_ref, full + used, 2 * full), (down_ref, used, full)):
+        if end > row:
+            ref[row:end, :] = jnp.zeros((end - row, ref.shape[1]), BF16)
     place = at.level * 4 + at.spot
     units = 4 * levels
     plan = [(0, 0)]
@@ -450,7 +444,7 @@
         return lev, sp, kind
 
     def loads(k, first):
-        slot = lax.rem(k, 2)
+        slot = lax.rem(k, 4)
         blocks = pl.ds(first, 2)
         return [
             pltpu.make_async_copy(rows_ref.at[blocks], x_buf.at[slot], in_sem.at[slot, 0]),
@@ -501,7 +495,7 @@
         mine = jnp.where((lanes(tail) == used + place) & (mark > 1.5), weight, 0.0)
         return jnp.sum(mine, axis=1, keepdims=True) / jnp.sum(weight, axis=1, keepdims=True)
 
-    def elementwise():
+    def elementwise(odd):
         mix = jnp.broadcast_to(mixing(), (batch, 128))
         total = jnp.zeros((batch, 128), F32)
         for n in range(full // 128):
@@ -517,9 +511,9 @@
             active = act * upper
             grad_act = scale * back
             slope = sig * (1.0 + gate * (1.0 - sig))
-            mixed_buf[:, cols] = (scale * active).astype(BF16)
-            act_buf[:, cols] = (grad_act * upper * slope).astype(BF16)
-            act_buf[:, up_cols] = (grad_act * act).astype(BF16)
+            mixed_buf[odd, :, cols] = (scale * active).astype(BF16)
+            act_buf[odd, :, cols] = (grad_act * upper * slope).astype(BF16)
+            act_buf[odd, :, up_cols] = (grad_act * act).astype(BF16)
             term = active * back
             total = total + (term if whole else jnp.where(lanes(n) < hidden, term, 0.0))
         gm_buf[...] = total
@@ -527,18 +521,18 @@
     def forward(k):
         lev, sp, _ = unit(k)
         first = (lev * 4 + sp) * 2
-        slot = lax.rem(k, 2)
+        slot = lax.rem(k, 4)
         for copy in loads(k, first):
             copy.wait()
         x = x_buf[slot].reshape(batch, -1)
-        cu_buf[...] = dot_nn(x, gate_ref[...])
+        cu_buf[...] = dot_nt(x, gate_ref[...])
         g_val[...] = dot_nt(g_buf[slot].reshape(batch, -1), down_ref[...])
         for n in range(2):
             marks = mark_buf[slot, n]
             above = jnp.zeros((used - (full - 128), 128), F32)
             below = jnp.zeros((full - used - marks.shape[0], 128), F32)
             mark_t[pl.ds(n * rows, rows), :] = jnp.transpose(jnp.concatenate([above, marks, below], axis=0))
-        elementwise()
+        elementwise(lax.rem(k, 2))
 
     def backward(k):
         lev, sp, _ = unit(k)
@@ -550,30 +544,37 @@
             for copy in stores(k, 0):
                 copy.wait()
 
-        back_buf[slot] = dot_nt(act_buf[...], gate_ref[...]).astype(BF16)
-        out_buf[slot] = dot_nn(mixed_buf[...], down_ref[...]).astype(BF16)
+        back_buf[slot] = dot_nn(act_buf[slot], gate_ref[...]).astype(BF16)
+        out_buf[slot] = dot_nn(mixed_buf[slot], down_ref[...]).astype(BF16)
         for n in range(2):
             gm = jnp.transpose(gm_buf[pl.ds(n * rows, rows), :])
             gm_val[pl.ds(first + n, 1), :] = jnp.sum(gm, axis=0, keepdims=True)
         start(stores(k, first))
 
+        both = pl.ds(lax.rem(k, 4) - 1, 2)
+
         def gate_grad(m, carry):
             part = pl.ds(pl.multiple_of(m * 256, 256), 256)
-            x = x_buf[slot, :, :, part].reshape(batch, 256)
-            gw_ref[part, :] += dot_tn(x, act_buf[...])
+            left = act_buf[:, :, part].reshape(2 * batch, 256)
+            gw_ref[part, :] += dot_tn(left, x_buf[both].reshape(2 * batch, -1))
             return carry
 
         def down_grad(m, carry):
             part = pl.ds(pl.multiple_of(m * 256, 256), 256)
-            gd_ref[part, :] += dot_tn(mixed_buf[:, part], g_buf[slot].reshape(batch, -1))
+            left = mixed_buf[:, :, part].reshape(2 * batch, 256)
+            gd_ref[part, :] += dot_tn(left, g_buf[both].reshape(2 * batch, -1))
             return carry
 
-        lax.fori_loop(0, gw_ref.shape[0] // 256, gate_grad, 0)
-        lax.fori_loop(0, full // 256, down_grad, 0)
+        @pl.when(slot == 1)
+        def _():
+            lax.fori_loop(0, gw_ref.shape[0] // 256, gate_grad, 0)
+            lax.fori_loop(0, full // 256, down_grad, 0)
 
     gw_ref[...] = jnp.zeros_like(gw_ref)
     gd_ref[...] = jnp.zeros_like(gd_ref)
     fetch_own()
+    for copy in weights:
+        copy.wait()
 
     def loop(k, carry):
         pl.when((k > 0) & (k + 1 < units))(lambda: serve(k + 1))
@@ -585,23 +586,25 @@
 
     lax.fori_loop(0, units, loop, 0)
     gm_ref[...] = gm_val[...]
-    dgate_ref[...] = gw_ref[:, :hidden]
-    dup_ref[...] = gw_ref[:, full : full + hidden]
-    ddown_ref[...] = gd_ref[:hidden, :]
-    size, skip = used - hidden, hidden - (full - 128)
-    for n in range(2):
-        turned = jnp.transpose(gw_ref[:, (n + 1) * full - 128 : (n + 1) * full])
-        shared_ref[n * size : (n + 1) * size, :] = turned[skip : skip + size, :].astype(BF16)
-    shared_ref[2 * size :, :] = gd_ref[hidden:used, :].astype(BF16)
+    finals = [
+        pltpu.make_async_copy(src.at[pl.ds(row, hidden)], dst, w_sem.at[n])
+        for n, (src, row, dst) in enumerate(
+            ((gw_ref, 0, dgate_ref), (gw_ref, full, dup_ref), (gd_ref, 0, ddown_ref))
+        )
+    ]
+    start(finals)
+    for n, (ref, row) in enumerate(((gw_ref, hidden), (gw_ref, full + hidden), (gd_ref, hidden))):
+        shared_ref[n * size : (n + 1) * size, :] = ref[row : row + size, :].astype(BF16)
+    for copy in finals:
+        copy.wait()
     for k in (0, 1):
         for copy in stores(k, 0):
             copy.wait()
     gather.finish(near=False)
 
 
-def experts_rows(x, grads, marks, gate_up, down, hidden, used, levels, collective_id):
+def experts_rows(x, grads, marks, weights, hidden, used, full, levels, collective_id):
     rows, width = x.shape
-    full = down.shape[0]
     blocks = 8 * levels
     total = blocks * rows
     dma = pltpu.SemaphoreType.DMA
@@ -619,30 +622,33 @@
             shape((total, width), BF16),
             shape((total, width), BF16),
             shape((blocks, rows), F32),
-            shape((width, hidden), F32),
-            shape((width, hidden), F32),
+            shape((hidden, width), F32),
+            shape((hidden, width), F32),
             shape((hidden, width), F32),
             shape((3 * (used - hidden), width), BF16),
         ],
-        in_specs=[anywhere, anywhere, anywhere, inside, inside],
-        out_specs=[anywhere] * 5 + [inside] * 5,
+        in_specs=[anywhere] * 8,
+        out_specs=[anywhere] * 5 + [inside] + [anywhere] * 3 + [inside],
         scratch_shapes=[
-            vmem((2, 2, rows, width), BF16),
-            vmem((2, 2, rows, width), BF16),
-            vmem((2, 2, *marks.shape), F32),
+            vmem((4, 2, rows, width), BF16),
+            vmem((4, 2, rows, width), BF16),
+            vmem((4, 2, *marks.shape), F32),
             vmem((batch, 2 * full), F32),
             vmem((batch, full), F32),
-            vmem((batch, full), BF16),
-            vmem((batch, 2 * full), BF16),
+            vmem((2, batch, full), BF16),
+            vmem((2, batch, 2 * full), BF16),
             vmem((2, batch, width), BF16),
             vmem((2, batch, width), BF16),
             vmem((batch, 128), F32),
             vmem((batch, 128), F32),
-            dma((2, 3)),
+            dma((4, 3)),
             dma((2, 2)),
             vmem((blocks, rows), F32),
-            vmem((width, 2 * full), F32),
+            vmem((2 * full, width), F32),
             vmem((full, width), F32),
+            vmem((2 * full, width), BF16),
+            vmem((full, width), BF16),
+            dma((7,)),
         ]
         + Gather.scratch(levels, 3),
         compiler_params=pltpu.CompilerParams(
@@ -650,7 +656,7 @@
             has_side_effects=True,
             vmem_limit_bytes=56 * 1024 * 1024,
         ),
-    )(x, grads, marks, gate_up, down)
+    )(x, grads, marks, *weights)
 
 
 def shared_kernel(slices, x_ref, gate_ref, up_ref, down_ref, gate_buf, up_buf, down_buf, sem):
@@ -732,8 +738,9 @@
 
 
 class Scatter:
-    def __init__(self, at, sibling, x_ref, out_ref, refs):
+    def __init__(self, at, sibling, x_ref, out_ref, refs, row=None):
         self.at, self.sibling, self.x_ref, self.out_ref = at, sibling, x_ref, out_ref
+        self.row = row
         self.acc, self.near, self.hx, self.hy, self.fx, self.fy = refs[:6]
         self.out_buf, self.za, self.zb = refs[6:9]
         self.own_sem, self.send_n, self.recv_n = refs[9:12]
@@ -764,6 +771,8 @@
     def own(self, lev, sp):
         b = lev * 4 + sp
         src = self.x_ref.at[b * 2 + self.at.core if self.sibling else b]
+        if self.row is not None:
+            src = src.at[pl.ds(self.row, self.rows)]
         return pltpu.make_async_copy(src, self.acc.at[b], self.own_sem.at[b])
 
     def to_sibling(self, lev, sp):
@@ -883,43 +892,127 @@
             pl.when(lev > self.at.level)(lambda lev=lev: self.go_up(lev).wait_send())
 
 
-def scatter_kernel(levels, sibling, lag, count, *refs):
-    x_refs, refs = refs[:count], refs[count:]
-    out_refs, refs = refs[:count], refs[count:]
+def dense_kernel(levels, spans, x_ref, flat_ref, all_ref, flat_all_ref, *refs):
     at = Place(levels)
-    at.enter(sibling)
+    at.enter(False)
+    sums, refs = refs[:2], refs[2:]
     size = Scatter.SCRATCH
-    tasks = [
-        Scatter(at, sibling, x_refs[n], out_refs[n], refs[n * size : (n + 1) * size])
-        for n in range(count)
+    scatters = [
+        Scatter(at, False, x_ref, sums[n], refs[n * size : (n + 1) * size], spans[n][0]) for n in range(2)
     ]
-    for task in tasks:
+    refs = refs[2 * size :]
+    pairs = [[(sums[n], all_ref, spans[n][0])] for n in range(2)]
+    pairs[1].append((flat_ref, flat_all_ref))
+    gathers = []
+    for n in range(2):
+        gathers.append(Gather(at, False, pairs[n], refs[n * 14 : (n + 1) * 14]))
+    for task in scatters:
         task.begin()
-    order = [
-        (s + n * lag, n, step) for n, task in enumerate(tasks) for s, step in enumerate(task.steps())
-    ]
-    for _, _, step in sorted(order, key=lambda entry: entry[:2]):
+    steps = []
+    for n, lag in enumerate((0, 7)):
+        begin = len(scatters[n].steps()) + lag
+        steps += [(s + lag, n, step) for s, step in enumerate(scatters[n].steps())]
+        steps.append((begin - 0.5, n, gathers[n].begin))
+        steps += [(begin + s, 2 + n, step) for s, step in enumerate(gathers[n].steps())]
+    for _, _, step in sorted(steps, key=lambda entry: entry[:2]):
         step()
-    for task in tasks:
+    for task in [*scatters, *gathers]:
         task.finish()
 
 
-def scatter_wide(arrays, levels, sibling, collective_id):
-    rows, width = arrays[0].shape[1:]
-    anywhere, inside = pl.BlockSpec(memory_space=pl.ANY), pl.BlockSpec(memory_space=pltpu.VMEM)
-    count = len(arrays)
+def sum_dense(x, flat, levels, collective_id):
+    blocks, rows, width = x.shape
+    first = -(-rows // 64) * 32
+    spans = [(0, first), (first, rows - first)]
+    vmem, anywhere = pltpu.VMEM, pl.BlockSpec(memory_space=pl.ANY)
+    shape = jax.ShapeDtypeStruct
     return pl.pallas_call(
-        functools.partial(scatter_kernel, levels, sibling, 7, count),
-        out_shape=[jax.ShapeDtypeStruct((rows, width), BF16)] * count,
-        in_specs=[anywhere] * count,
-        out_specs=[inside] * count,
-        scratch_shapes=Scatter.scratch(levels, sibling, rows, width) * count,
+        functools.partial(dense_kernel, levels, spans),
+        out_shape=[shape(x.shape, BF16), shape((blocks, *flat.shape), BF16)],
+        in_specs=[anywhere, anywhere],
+        out_specs=[anywhere, anywhere],
+        scratch_shapes=[vmem((n, width), BF16) for _, n in spans]
+        + Scatter.scratch(levels, False, spans[0][1], width)
+        + Scatter.scratch(levels, False, spans[1][1], width)
+        + Gather.scratch(levels, 1)
+        + Gather.scratch(levels, 2),
         compiler_params=pltpu.CompilerParams(
             collective_id=collective_id,
             has_side_effects=True,
             vmem_limit_bytes=60 * 1024 * 1024,
         ),
-    )(*arrays)
+    )(x, flat)
+
+
+def exchange_kernel(
+    levels, back_ref, out_ref, part_ref, rows_ref, sum_ref, all_ref, block, send_s, recv_s, own_s, *refs
+):
+    at = Place(levels)
+    at.enter(True)
+    size = Scatter.SCRATCH
+    first = Scatter(at, True, back_ref, rows_ref, refs[:size])
+    second = Scatter(at, True, out_ref, sum_ref, refs[size : 2 * size])
+    gather = Gather(at, False, [(block, all_ref)], refs[2 * size :])
+    units, half = part_ref.shape[0] // 3, part_ref.shape[1] // 2
+    mine = pl.ds(pl.multiple_of(at.core * units, units), units)
+    own, theirs, sends = [], [], []
+    for n in range(2):
+        rows, lanes = pl.ds(n * units, units), pl.ds(n * half, half)
+
+        def side(core):
+            return part_ref.at[rows, pl.ds(pl.multiple_of(core * half, 128), half)]
+
+        own.append(pltpu.make_async_copy(side(at.core), block.at[mine, lanes], own_s.at[n]))
+        device = at.device(at.level, at.spot, 1 - at.core)
+        sems = send_s.at[n], recv_s.at[n]
+        sends.append(remote(side(1 - at.core), block.at[mine, lanes], *sems, device))
+    down = pl.ds(2 * units, units)
+    own.append(pltpu.make_async_copy(part_ref.at[down], block.at[down], own_s.at[2]))
+    start(sends)
+    start(own)
+    first.begin()
+    second.begin()
+    for copy in own:
+        copy.wait()
+    arrived(sends)
+    gather.begin()
+    steps = [(s, 0, step) for s, step in enumerate(first.steps())]
+    steps += [(s + 7, 1, step) for s, step in enumerate(second.steps())]
+    steps += [(s + 2, 2, step) for s, step in enumerate(gather.steps())]
+    for _, _, step in sorted(steps, key=lambda entry: entry[:2]):
+        step()
+    sent(sends)
+    first.finish()
+    second.finish()
+    gather.finish()
+
+
+def exchange_wide(back, out, part, levels, collective_id):
+    rows, width = back.shape[1:]
+    dma = pltpu.SemaphoreType.DMA
+    anywhere, inside = pl.BlockSpec(memory_space=pl.ANY), pl.BlockSpec(memory_space=pltpu.VMEM)
+    shape = jax.ShapeDtypeStruct
+    return pl.pallas_call(
+        functools.partial(exchange_kernel, levels),
+        out_shape=[
+            shape((rows, width), BF16),
+            shape((rows, width), BF16),
+            shape((levels * 4, *part.shape), BF16),
+        ],
+        in_specs=[anywhere, anywhere, inside],
+        out_specs=[inside, inside, anywhere],
+        scratch_shapes=[pltpu.VMEM(part.shape, BF16), dma((2,)), dma((2,)), dma((3,))]
+        + Scatter.scratch(levels, True, rows, width) * 2
+        + Gather.scratch(levels, 1),
+        compiler_params=pltpu.CompilerParams(
+            collective_id=collective_id,
+            has_side_effects=True,
+            vmem_limit_bytes=60 * 1024 * 1024,
+        ),
+        cost_estimate=pl.CostEstimate(
+            flops=40 * 10**9, bytes_accessed=200 * 10**6, transcendentals=0
+        ),
+    )(back, out, part)
 
 
 def slots_path(
@@ -1324,13 +1417,11 @@
     gate_send, up_send = shared_slice(shared_gate, 1 - core, 1), shared_slice(shared_up, 1 - core, 1)
     down_slice = shared_slice(shared_down, 0, 0)
     gains = jnp.stack([attn_gain, ffn_gain])
-    sent = swap(jnp.concatenate([gate_send, up_send, w_router], axis=1))
+    sent = swap(jnp.concatenate([gate_send.T, up_send.T, w_router.T], axis=0))
     gains = in_order(gains, swap(gains), 1).astype(F32)
     attn_scale, ffn_scale = gains[0], gains[1]
-    dense = in_order(jnp.concatenate([gate_mine, up_mine, w_router], axis=1), sent, 0)
-    gate_slice = dense[:, :slice_width]
-    up_slice = dense[:, slice_width : 2 * slice_width]
-    router = dense[:, 2 * slice_width :]
+    dense = in_order(jnp.concatenate([gate_mine.T, up_mine.T, w_router.T], axis=0), sent, 1)
+    router = dense[2 * slice_width :]
 
     row_tokens = jnp.concatenate([tokens, swap(tokens)], axis=0).astype(F32)
     normed, unit_one, scale_one = norm_forward(row_tokens, attn_scale)
@@ -1362,22 +1453,14 @@
     used = hidden_part + slice_width
     full = -(-(used + experts) // 128) * 128
 
-    def pad(value, size, axis):
-        extra = list(value.shape)
-        extra[axis] = size - value.shape[axis]
-        return jnp.concatenate([value, jnp.zeros(extra, value.dtype)], axis=axis)
-
-    gate_all = pad(jnp.concatenate([expert_gate[0], gate_slice, router], axis=1), full, 1)
-    up_all = pad(jnp.concatenate([expert_up[0], up_slice], axis=1), full, 1)
-    down_all = pad(jnp.concatenate([expert_down[0], down_slice], axis=0), full, 0)
     (_, _, _, grad_rows, expert_out, grad_mix, *expert_grads, shared_part) = experts_rows(
         normed_two,
         cotangent,
         marks.T,
-        jnp.concatenate([gate_all, up_all], axis=1),
-        down_all,
+        [expert_gate[0].T, expert_up[0].T, expert_down[0], dense, down_slice],
         hidden_part,
         used,
+        full,
         levels,
         1,
     )
@@ -1388,29 +1471,18 @@
     send_core = jnp.where(core == 0, grad_mix[:, 1], grad_mix[:, 0])
     grad_mix = (pick_core + swap(send_core)).T
     block_shape = (2 * wide_size, local_rows, width)
-    grad_rows, expert_out = scatter_wide(
-        [grad_rows.reshape(block_shape), expert_out.reshape(block_shape)], levels, True, 2
+    grad_rows, expert_out, shared_all = exchange_wide(
+        grad_rows.reshape(block_shape), expert_out.reshape(block_shape), shared_part, levels, 2
     )
     output = (hidden + expert_out.astype(F32)).astype(BF16)
     grad_expert_gate, grad_expert_up, grad_expert_down = expert_grads
-    shared_t, shared_down_grad = shared_part[: 2 * slice_width], shared_part[2 * slice_width :]
-    theirs = swap(columns(shared_t, 1 - core, part))
-    shared_t = columns(shared_t, core, part)
-
-    def side_by_side(value):
-        return jnp.concatenate([value[:slice_width], value[slice_width:]], axis=1)
-
-    shared_block = jnp.concatenate(
-        [in_order(side_by_side(shared_t), side_by_side(theirs), 0), shared_down_grad], axis=0
-    )
-    (shared_all,) = gather_wide([shared_block], levels, False, 4)
     grad_shared_gate, grad_shared_up, grad_shared_down = shared_grads(
         shared_all, slices, part, stored
     )
 
     marks = marks.astype(F32)
     routed = marks > 0.0
-    logits = matmul(normed_two, router)
+    logits = matmul_right(normed_two, router)
     masked = jnp.where(routed, logits, MASKED)
     weights = jnp.where(routed, jnp.exp(masked - jnp.max(masked, axis=1, keepdims=True)), 0.0)
     gates = weights / jnp.sum(weights, axis=1, keepdims=True)
@@ -1418,7 +1490,7 @@
     grad_logits = gates * (grad_gates - jnp.sum(gates * grad_gates, axis=1, keepdims=True))
     grad_logits = grad_logits.astype(BF16)
     grad_router = matmul_left(normed_two, grad_logits)
-    grad_normed = grad_rows.astype(F32) + matmul_right(grad_logits, router)
+    grad_normed = grad_rows.astype(F32) + matmul(grad_logits, router)
     grad_hidden_norm, grad_ffn = norm_backward(grad_normed, unit_two, scale_two, ffn_scale)
     grad_hidden = cotangent.astype(F32) + grad_hidden_norm
     grad_branch = grad_hidden.astype(BF16)
@@ -1456,8 +1528,9 @@
     extra_rows = -(-size // (width * 16)) * 16
     flat = jnp.concatenate([small.reshape(-1), jnp.zeros((extra_rows * width - size,), BF16)])
     sum_rows = 4 * part // wide_size
-    (summed,) = scatter_wide([grad_dense.reshape(wide_size, sum_rows, width)], levels, False, 5)
-    everything, flat = gather_wide([summed, flat.reshape(extra_rows, width)], levels, False, 6)
+    everything, flat = sum_dense(
+        grad_dense.reshape(wide_size, sum_rows, width), flat.reshape(extra_rows, width), levels, 3
+    )
     owned = everything.reshape(4, part, width)
     flat = flat.astype(F32).reshape(wide_size, -1)
     small = jnp.sum(flat[:, :size], axis=0).reshape(part, 2 + experts)
@@ -1474,8 +1547,8 @@
         grad_shared_gate,
         grad_shared_up,
         grad_shared_down,
-        grad_expert_gate[None],
-        grad_expert_up[None],
+        grad_expert_gate.T[None],
+        grad_expert_up.T[None],
         grad_expert_down[None],
     )
 

time: 558 us -> 519 us (0.930)
  Pallas kernels: 407 us -> 384 us
  local copies, waits for them, and re-layouts: 73.1 us -> 57.5 us
    pallas_call x1, Pallas kernels: 138 us -> 124 us  [experts_rows(): pl.pallas_call(functools.partial(experts_kernel, levels, (hidden, used, f...]
    pallas_call x4 -> x2, Pallas kernels: 263 us -> 253 us  [the longest x1 129 us: exchange_wide(): pl.pallas_call(functools.partial(exchange_kernel, levels), out_shape=[sha...]
    unnamed x146 -> x147, local copies, waits for them, and re-layouts: 38.5 us -> 29.4 us
    concatenate x1 -> x0, local copies, waits for them, and re-layouts: 6.31 us -> none  [tokens_path(): jnp.concatenate([gate_all, up_all], axis=1)]
    all_to_all x1, waiting for transfers between devices: 5.89 us -> 0.01 us  [tokens_path(): lax.all_to_all(grad_mix.reshape(wide_size, 2, local_rows), 'wide', split_...]
  transfers between devices with their start and end apart: 12 -> 11, of which waited for: 1 -> 2; matrix products, arithmetic and copies ran while one was open for 11% -> 11% of each run, Pallas kernels for 37% -> 26%
where the time goes in v4:
time: 519 us; the launch traced here: 511 us
  Pallas kernels  384 us (74%)
  local copies, waits for them, and re-layouts  57.5 us (11%)
  other arithmetic  39.9 us (8%)
  matrix products  17.5 us (3%)
  starting transfers between devices  8.53 us (2%)
    pallas_call x1, Pallas kernels, exchange_wide(): pl.pallas_call(functools.partial(exchange_kernel, levels), out_shape=[sha...  129 us
    pallas_call x1, Pallas kernels, experts_rows(): pl.pallas_call(functools.partial(experts_kernel, levels, (hidden, used, f...  124 us
    pallas_call x1, Pallas kernels, sum_dense(): pl.pallas_call(functools.partial(dense_kernel, levels, spans), out_shape=...  124 us
    unnamed x147, local copies, waits for them, and re-layouts  29.4 us
  transfers between devices with their start and end apart: 11, of which 2 were waited for; matrix products, arithmetic and copies ran while one was open for 11% of the time, Pallas kernels for 26%

profile of v4, /device:TPU:0, one launch (start us, length us, event | category | flops | bytes accessed | tf_op | source)
XLA Modules:
  0.0 511.1 jit_solution(5014139380544851388)
XLA Ops:
  3.4 2.2 constant_dynamic-slice_fusion.3
  13.0 3.3 constant_dynamic-slice_fusion.8
  30.4 2.0 fusion.47
  33.6 2.1 copy.182
  36.7 2.0 fusion.46
  38.6 2.1 copy.183
  40.8 2.0 copy.184
  54.6 124.3 %shard_map.289 = (bf16[32,128,1280]{2,1,0:T(8,128)(2,1)}, bf16[32,128,1280]{2,1,0:T(8,128)(2,1)}, f32[32,16,128]{2,1,0:T(8,128)}, bf16[4096,1280]{1,0:T(8,128)(2...) custom-call(bf16[128,1280]{1,0:T(8,128)(2,1)} %multiply_convert_fusi, ...), custom_call_target="tpu_custom_call" | custom-call | tf_op jit(solution)/shard_map/pallas_call | solution.py:616
  179.0 5.8 %all-to-all-start = ((f32[16,2,128]{2,1,0:T(2,128)}), f32[16,2,128]{2,1,0:T(2,128)}, u32[]{:S(2)}, u32[]{:S(2)}) async-start(f32[16,2,128]{2,1,0:T(2,128)} %bitcast.147), calls=%async_computation | async-start | bytes 32768 | tf_op jit(solution)/shard_map/all_to_all | solution.py:1467
  184.8 128.7 %shard_map.290 = (bf16[128,1280]{1,0:T(8,128)(2,1)}, bf16[128,1280]{1,0:T(8,128)(2,1)}, bf16[16,96,1280]{2,1,0:T(8,128)(2,1)}) custom-call(bf16[32,128,1280]{2,1,0:T(8,128)(2,1)} %bitcast.151, bf16[32,128,1280]{2,1,0:T(8,128)(2,1)} %bitcast.152, bf16[96,1280]{1,0:T(8,128)(2,1)} %get-tuple-element.32.part_ref), custom_call_target="tpu_custom_call" | custom-call | flops 40000000000 | bytes 200000000 | tf_op jit(solution)/shard_map/pallas_call | solution.py:995
  313.5 2.1 fusion.50
  319.2 2.2 multiply_reduce_fusion.2
  326.0 1.9 copy.157
  338.1 2.1 copy-done.1
  340.2 6.3 %shard_map.292 = (f32[640,896]{1,0:T(8,128)}, f32[640,896]{1,0:T(8,128)}, f32[448,1280]{1,0:T(8,128)}) custom-call(bf16[16,96,1280]{2,1,0:T(8,128)(2,1)S(1)} %copy-done.1), custom_call_target="tpu_custom_call" | custom-call | tf_op jit(solution)/shard_map/pallas_call | solution.py:690
  347.6 2.9 maximum_select_fusion
  356.9 3.3 pad_maximum_fusion
  364.1 124.2 %shard_map.291 = (bf16[16,160,1280]{2,1,0:T(8,128)(2,1)}, bf16[16,16,1280]{2,1,0:T(8,128)(2,1)}) custom-call(bf16[16,160,1280]{2,1,0:T(8,128)(2,1)} %bitcast.118, bf16[16,1280]{1,0:T(8,128)(2,1)} %reshape.336.flat_ref), custom_call_target="tpu_custom_call" | custom-call | tf_op jit(solution)/shard_map/pallas_call | solution.py:929
  491.2 3.4 fusion.42
  494.5 2.1 bitcast_convert_fusion
  496.6 2.1 bitcast_convert_fusion.1
  498.6 2.1 bitcast_convert_fusion.2
  500.7 2.1 bitcast_convert_fusion.3
  503.5 3.3 copy.195
  (261 shorter events, 74.5 us)
Async XLA Ops:
  0.6 48.0 %copy-start = (bf16[640,1280]{1,0:T(8,128)(2,1)S(1)}, bf16[640,1280]{1,0:T(8,128)(2,1)}, u32[]{:S(2)}) copy-start(bf16[640,1280]{1,0:T(8,128)(2,1)} %param.27) | copy-start | bytes 4915204
  0.7 7.0 %copy-start.50 = (bf16[640,16]{0,1:T(8,128)(2,1)S(1)}, bf16[640,16]{0,1:T(8,128)(2,1)}, u32[]{:S(2)}) copy-start(bf16[640,16]{0,1:T(8,128)(2,1)} %param.29) | copy-start | bytes 61444
  0.7 11.1 %copy-start.64 = (s32[128,7]{0,1:T(8,128)S(1)}, s32[128,7]{0,1:T(8,128)}, u32[]{:S(2)}) copy-start(s32[128,7]{0,1:T(8,128)} %param.22) | copy-start | bytes 10756
  0.7 12.4 %copy-start.9 = (bf16[640,1280]{1,0:T(8,128)(2,1)S(1)}, bf16[640,1280]{1,0:T(8,128)(2,1)}, u32[]{:S(2)}) copy-start(bf16[640,1280]{1,0:T(8,128)(2,1)} %param.26) | copy-start | bytes 4915204
  2.9 14.8 %collective-permute-start.1 = (bf16[2,640]{1,0:T(2,128)(2,1)}, bf16[2,640]{1,0:T(2,128)(2,1)}, u32[]{:S(2)}, u32[]{:S(2)}) collective-permute-start(bf16[2,640]{1,0:T(2,128)(2,1)} %pad_maximum_fusion.12), channel_id=1, source_target_pairs={{0,1},{1,0},{2,3},{3,2},{4,5},{5,4},{6,7},{7,6},{8,9},{9,8},{10,11... | collective-permute-start | bytes 7688 | tf_op jit(solution)/shard_map/ppermute | solution.py:1388
  3.4 15.2 %collective-permute-start = (bf16[128,1280]{1,0:T(8,128)(2,1)}, bf16[128,1280]{1,0:T(8,128)(2,1)}, u32[]{:S(2)}, u32[]{:S(2)}) collective-permute-start(bf16[128,1280]{1,0:T(8,128)(2,1)} %param.18), channel_id=1, source_target_pairs={{0,1},{1,0},{2,3},{3,2},{4,5},{5,4},{6,7},{7,6},{8,9},{9,8},{10,11... | collective-permute-start | bytes 983048 | tf_op jit(solution)/shard_map/ppermute | solution.py:1388
  8.3 41.6 %collective-permute-start.4 = (bf16[80,640]{1,0:T(8,128)(2,1)}, bf16[80,640]{1,0:T(8,128)(2,1)}, u32[]{:S(2)}, u32[]{:S(2)}) collective-permute-start(bf16[80,640]{1,0:T(8,128)(2,1)} %pad_maximum_fusion.9), channel_id=1, source_target_pairs={{0,1},{1,0},{2,3},{3,2},{4,5},{5,4},{6,7},{7,6},{8,9},{9,8},{10,11... | collective-permute-start | bytes 307208 | tf_op jit(solution)/shard_map/ppermute | solution.py:1388
  23.2 4.2 collective-permute-start.2
  38.6 6.0 %copy-start.28 = (f32[256,5,64]{2,0,1:T(8,128)S(1)}, f32[256,5,64]{2,0,1:T(8,128)}, u32[]{:S(2)}) copy-start(f32[256,5,64]{2,0,1:T(8,128)} %copy.182) | copy-start | bytes 983044
  49.5 3.3 collective-permute-start.3
  179.0 136.6 %all-to-all-start = ((f32[16,2,128]{2,1,0:T(2,128)}), f32[16,2,128]{2,1,0:T(2,128)}, u32[]{:S(2)}, u32[]{:S(2)}) async-start(f32[16,2,128]{2,1,0:T(2,128)} %bitcast.147), calls=%async_computation | async-start | bytes 32768 | tf_op jit(solution)/shard_map/all_to_all | solution.py:1467
  184.8 128.7 %copy-start.14 = (bf16[128,1280]{1,0:T(8,128)(2,1)S(1)}, bf16[128,1280]{1,0:T(8,128)(2,1)}, u32[]{:S(2)}) copy-start(bf16[128,1280]{1,0:T(8,128)(2,1)} %multiply_convert_fusion.1.x_ref) | copy-start | bytes 983044
  315.6 5.8 %copy-start.17 = (bf16[128,1280]{1,0:T(8,128)(2,1)S(1)}, bf16[128,1280]{1,0:T(8,128)(2,1)}, u32[]{:S(2)}) copy-start(bf16[128,1280]{1,0:T(8,128)(2,1)} %g_ref.1) | copy-start | bytes 983044
  315.6 5.8 %copy-start.60 = (f32[128]{0:T(128)S(1)}, f32[128]{0:T(128)}, u32[]{:S(2)}) copy-start(f32[128]{0:T(128)} %copy-done.59) | copy-start | bytes 1540
  316.5 1.2 collective-permute-start.5
  322.3 1.6 collective-permute-start.6
  337.9 9.5 %collective-permute-start.7 = (bf16[3,256,640]{1,2,0:T(8,128)(2,1)S(1)}, bf16[3,256,640]{1,2,0:T(8,128)(2,1)S(1)}, u32[]{:S(2)}, u32[]{:S(2)}) collective-permute-start(bf16[3,256,640]{1,2,0:T(8,128)(2,1)S(1)} %pad_maximum_fusion.1), channel_id=1, source_target_pairs={{0,1},{1,0},{2,3},{3,2},{4,5},{5,4},{6,7},{7,6},{8,9},{9,8},{10,11... | collective-permute-start | bytes 2949128 | tf_op jit(solution)/shard_map/ppermute | solution.py:1388
  340.2 6.3 %copy-start.56 = (f32[1280]{0:T(1024)S(1)}, f32[1280]{0:T(1024)}, u32[]{:S(2)}) copy-start(f32[1280]{0:T(1024)} %get-tuple-element.107) | copy-start | bytes 15364
  340.2 6.4 %copy-start.55 = (bf16[128,16]{0,1:T(8,128)(2,1)S(1)}, bf16[128,16]{0,1:T(8,128)(2,1)}, u32[]{:S(2)}) copy-start(bf16[128,16]{0,1:T(8,128)(2,1)} %copy-done.54) | copy-start | bytes 12292
  340.2 6.5 %copy-start.32 = (bf16[5,128,256]{2,1,0:T(8,128)(2,1)S(1)}, bf16[5,128,256]{2,1,0:T(8,128)(2,1)}, u32[]{:S(2)}) copy-start(bf16[5,128,256]{2,1,0:T(8,128)(2,1)} %copy-done.31) | copy-start | bytes 983044
  340.2 6.5 %copy-start.34 = (bf16[128,1280]{1,0:T(8,128)(2,1)S(1)}, bf16[128,1280]{1,0:T(8,128)(2,1)}, u32[]{:S(2)}) copy-start(bf16[128,1280]{1,0:T(8,128)(2,1)} %copy-done.33) | copy-start | bytes 983044
  340.2 6.5 %copy-start.44 = (bf16[128,1280]{1,0:T(8,128)(2,1)S(1)}, bf16[128,1280]{1,0:T(8,128)(2,1)}, u32[]{:S(2)}) copy-start(bf16[128,1280]{1,0:T(8,128)(2,1)} %copy-done.43) | copy-start | bytes 983044
  356.4 3.8 collective-permute-start.8
  360.6 2.3 collective-permute-start.9
  (55 other events, 115.9 us)

commit v5 on v4

--- a/solution.py
+++ b/solution.py
@@ -1015,6 +1015,120 @@
     )(back, out, part)
 
 
+def local_call(kernel, outs, scratch, *args):
+    inside = pl.BlockSpec(memory_space=pltpu.VMEM)
+    return pl.pallas_call(
+        kernel,
+        out_shape=[jax.ShapeDtypeStruct(s, d) for s, d in outs],
+        in_specs=[inside] * len(args),
+        out_specs=[inside] * len(outs),
+        scratch_shapes=[pltpu.VMEM(s, d) for s, d in scratch],
+        compiler_params=pltpu.CompilerParams(vmem_limit_bytes=48 * 1024 * 1024),
+    )(*args)
+
+
+def half_lanes(which, size):
+    return pl.ds(pl.multiple_of(which * size, 128), size)
+
+
+def project_kernel(mine_ref, theirs_ref, scale_ref, q_ref, k_ref, v_ref, n_ref, keep_ref, send_ref, buf):
+    core = lax.axis_index("narrow")
+    rows = mine_ref.shape[0]
+    part = n_ref.shape[1]
+    for n, ref in enumerate((mine_ref, theirs_ref)):
+        x = ref[...].astype(F32)
+        r = lax.rsqrt(jnp.mean(x * x, axis=1, keepdims=True) + EPS)
+        buf[n * rows : (n + 1) * rows, :] = (x * r * scale_ref[...]).astype(BF16)
+    normed = buf[:, half_lanes(core, part)]
+    n_ref[...] = normed
+    for n, ref in enumerate((q_ref, k_ref, v_ref)):
+        cols = slice(n * part, (n + 1) * part)
+        send_ref[:, cols] = dot_nn(normed, ref[:, half_lanes(1 - core, part)]).astype(BF16)
+        keep_ref[:, cols] = dot_nn(normed, ref[:, half_lanes(core, part)])
+
+
+def probabilities(q, k, allowed):
+    scores = jnp.where(allowed, dot_nt(q, k), MASKED)
+    weights = jnp.exp(scores - jnp.max(scores, axis=1, keepdims=True))
+    return weights / jnp.sum(weights, axis=1, keepdims=True)
+
+
+def turn(values, cosine, sine_table):
+    return values * cosine + pltpu.roll(values, HEAD_DIM // 2, 1) * sine_table
+
+
+def attend_kernel(
+    keep_ref, got_ref, cos_ref, sin_ref, mask_ref, out_w_ref,
+    q_ref, k_ref, v_ref, o_ref, branch_ref, send_ref,
+):
+    rows, part = q_ref.shape
+    half = rows // 2
+    allowed = mask_ref[...] > 0.5
+    cosine, sine_table = cos_ref[...], sin_ref[...]
+
+    def full(cols):
+        got = jnp.concatenate([got_ref[half:, cols], got_ref[:half, cols]], axis=0)
+        return keep_ref[:, cols] + got.astype(F32)
+
+    for h in range(part // HEAD_DIM):
+        cols = slice(h * HEAD_DIM, (h + 1) * HEAD_DIM)
+        q = full(slice(cols.start, cols.stop))
+        k = full(slice(part + cols.start, part + cols.stop))
+        v = full(slice(2 * part + cols.start, 2 * part + cols.stop)).astype(BF16)
+        q = (turn(q, cosine, sine_table) * HEAD_DIM ** (-0.5)).astype(BF16)
+        k = turn(k, cosine, sine_table).astype(BF16)
+        q_ref[:, cols] = q
+        k_ref[:, cols] = k
+        v_ref[:, cols] = v
+        o_ref[:, cols] = dot_nn(probabilities(q, k, allowed).astype(BF16), v).astype(BF16)
+    send_ref[...] = dot_nn(o_ref[half:, :], out_w_ref[...]).astype(BF16)
+    branch_ref[...] = dot_nn(o_ref[:half, :], out_w_ref[...])
+
+
+def attend_back_kernel(
+    branch_ref, their_ref, q_ref, k_ref, v_ref, o_ref, cos_ref, sin_ref, mask_ref, out_w_ref,
+    grad_w_ref, mine_ref, row_buf, grad_buf,
+):
+    rows, part = q_ref.shape
+    half = rows // 2
+    allowed = mask_ref[...] > 0.5
+    cosine, sine_table = cos_ref[...], -sin_ref[...]
+    row_buf[:half, :] = branch_ref[...]
+    row_buf[half:, :] = their_ref[...]
+    grad_buf[...] = dot_nt(row_buf[...], out_w_ref[...]).astype(BF16)
+    for h in range(part // HEAD_DIM):
+        cols = slice(h * HEAD_DIM, (h + 1) * HEAD_DIM)
+        q, k, v, grad = q_ref[:, cols], k_ref[:, cols], v_ref[:, cols], grad_buf[:, cols]
+        probs = probabilities(q, k, allowed)
+        grad_probs = dot_nt(grad, v)
+        delta = jnp.sum(probs * grad_probs, axis=1, keepdims=True)
+        grad_scores = (probs * (grad_probs - delta)).astype(BF16)
+        grad_q = dot_nn(grad_scores, k) * HEAD_DIM ** (-0.5)
+        mine_ref[0, :, cols] = turn(grad_q, cosine, sine_table).astype(BF16)
+        mine_ref[1, :, cols] = turn(dot_tn(grad_scores, q), cosine, sine_table).astype(BF16)
+        mine_ref[2, :, cols] = dot_tn(probs.astype(BF16), grad).astype(BF16)
+    grad_w_ref[...] = dot_tn(o_ref[...], row_buf[...]).astype(BF16)
+
+
+def dense_back_kernel(
+    mine_ref, their_ref, n_ref, grad_w_ref, q_ref, k_ref, v_ref, dense_ref, part_ref, send_ref, buf
+):
+    core = lax.axis_index("narrow")
+    rows, part = n_ref.shape
+    half = rows // 2
+    total = None
+    for n, ref in enumerate((q_ref, k_ref, v_ref)):
+        buf[n, :, half_lanes(core, part)] = mine_ref[n]
+        buf[n, :half, half_lanes(1 - core, part)] = their_ref[n, half:, :]
+        buf[n, half:, half_lanes(1 - core, part)] = their_ref[n, :half, :]
+        term = dot_nt(buf[n], ref[...])
+        total = term if total is None else total + term
+        dense_ref[n] = dot_tn(n_ref[...], buf[n]).astype(BF16)
+    dense_ref[3] = grad_w_ref[...]
+    part_ref[...] = total[:half]
+    send_ref[...] = total[half:].astype(BF16)
+
+
 def slots_path(
     tokens,
     cotangent,
@@ -1377,7 +1491,6 @@
     local_rows, width = tokens.shape
     row_length = 2 * local_rows
     part = width // 2
-    heads = part // HEAD_DIM
     hidden_part = expert_gate.shape[2]
     stored = shared_gate.shape[1] // 2
     slice_width = -(-stored // (16 * wide_size)) * 16
@@ -1386,9 +1499,6 @@
 
     def swap(value):
         return lax.ppermute(value, "narrow", [(0, 1), (1, 0)])
-
-    def other_rows(value):
-        return jnp.concatenate([value[local_rows:], value[:local_rows]], axis=0)
 
     def in_order(mine, theirs, axis):
         return jnp.where(
@@ -1396,9 +1506,6 @@
             jnp.concatenate([mine, theirs], axis=axis),
             jnp.concatenate([theirs, mine], axis=axis),
         )
-
-    def columns(value, which, size):
-        return lax.dynamic_slice_in_dim(value, which * size, size, axis=1)
 
     picks = (routes[:, :, None] == jnp.arange(experts, dtype=jnp.int32)[None, None, :]).astype(
         jnp.int32
@@ -1423,30 +1530,38 @@
     dense = in_order(jnp.concatenate([gate_mine.T, up_mine.T, w_router.T], axis=0), sent, 1)
     router = dense[2 * slice_width :]
 
-    row_tokens = jnp.concatenate([tokens, swap(tokens)], axis=0).astype(F32)
-    normed, unit_one, scale_one = norm_forward(row_tokens, attn_scale)
-    normed_one = columns(normed.astype(BF16), core, part)
+    inputs = tokens.astype(F32)
+    square, wide_rows = (row_length, part), (local_rows, width)
     projections = [w_query, w_key, w_value]
-    keep_side = jnp.concatenate([columns(w, core, part) for w in projections], axis=1)
-    send_side = jnp.concatenate([columns(w, 1 - core, part) for w in projections], axis=1)
-    arrived = swap(matmul(normed_one, send_side).astype(BF16))
-    qkv = matmul(normed_one, keep_side) + other_rows(arrived).astype(F32)
+    normed_one, qkv, sent = local_call(
+        project_kernel,
+        [(square, BF16), ((row_length, 3 * part), F32), ((row_length, 3 * part), BF16)],
+        [((row_length, width), BF16)],
+        tokens,
+        swap(tokens),
+        attn_scale[None, :],
+        *projections,
+    )
     index = jnp.arange(local_rows, dtype=jnp.int32)
     index = jnp.concatenate([core * local_rows + index, (1 - core) * local_rows + index])
     docs, positions = doc_layout(index, lengths[0])
     allowed = (docs[:, None] == docs[None, :]) & (index[None, :] <= index[:, None])
     cosine, sine_table = rotary_angles(positions)
-    head_shape = (row_length, heads, HEAD_DIM)
-    query_rows = rotate(qkv[:, :part].reshape(head_shape), cosine, sine_table)
-    query_rows = (query_rows * HEAD_DIM ** (-0.5)).astype(BF16)
-    key_rows = rotate(qkv[:, part : 2 * part].reshape(head_shape), cosine, sine_table).astype(BF16)
-    value_rows = qkv[:, 2 * part :].astype(BF16).reshape(head_shape)
-    attended, logsum = attend_block(query_rows, key_rows, value_rows, allowed)
-    attended = attended.reshape(row_length, part)
-    branch = matmul(attended, w_out)
-    arrived = swap(branch[local_rows:].astype(BF16))
-    inputs = row_tokens[:local_rows]
-    hidden = inputs + branch[:local_rows] + arrived.astype(F32)
+    tables = [
+        jnp.concatenate([cosine, cosine], axis=1),
+        jnp.concatenate([-sine_table, sine_table], axis=1),
+        allowed.astype(F32),
+    ]
+    *attention, branch, sent = local_call(
+        attend_kernel,
+        [(square, BF16)] * 4 + [(wide_rows, F32), (wide_rows, BF16)],
+        [],
+        qkv,
+        swap(sent),
+        *tables,
+        w_out,
+    )
+    hidden = inputs + branch + swap(sent).astype(F32)
     normed, unit_two, scale_two = norm_forward(hidden, ffn_scale)
     normed_two = normed.astype(BF16)
 
@@ -1494,30 +1609,30 @@
     grad_hidden_norm, grad_ffn = norm_backward(grad_normed, unit_two, scale_two, ffn_scale)
     grad_hidden = cotangent.astype(F32) + grad_hidden_norm
     grad_branch = grad_hidden.astype(BF16)
-    row_branch = jnp.concatenate([grad_branch, swap(grad_branch)], axis=0)
-
-    grad_w_out = matmul_left(attended, row_branch)
-    grad_attended = matmul_right(row_branch, w_out).astype(BF16).reshape(head_shape)
-    grad_queries, grad_keys, grad_values = attend_back(
-        query_rows, key_rows, value_rows, allowed, logsum, grad_attended
-    )
-    grad_queries = rotate(grad_queries * HEAD_DIM ** (-0.5), cosine, -sine_table)
-    grad_keys = rotate(grad_keys, cosine, -sine_table)
-    mine = jnp.stack([grad_queries, grad_keys, grad_values]).reshape(3, row_length, part)
-    mine = mine.astype(BF16)
-    theirs = swap(mine)
-    theirs = jnp.concatenate([theirs[:, local_rows:], theirs[:, :local_rows]], axis=1)
-    grad_qkv = in_order(mine, theirs, 2)
-    grad_dense = jnp.stack(
-        [matmul_left(normed_one, grad_qkv[k]) for k in range(3)] + [grad_w_out]
-    ).astype(BF16)
-    grad_part = sum(matmul_right(grad_qkv[k], projections[k]) for k in range(3))
-    grad_normed_one = in_order(
-        grad_part[:local_rows], swap(grad_part[local_rows:].astype(BF16)).astype(F32), 1
-    )
-    grad_input_norm, grad_attn = norm_backward(
-        grad_normed_one, unit_one[:local_rows], scale_one[:local_rows], attn_scale
-    )
+
+    grad_w_out, mine = local_call(
+        attend_back_kernel,
+        [((part, width), BF16), ((3, *square), BF16)],
+        [((row_length, width), BF16), (square, BF16)],
+        grad_branch,
+        swap(grad_branch),
+        *attention,
+        *tables,
+        w_out,
+    )
+    grad_dense, grad_part, sent = local_call(
+        dense_back_kernel,
+        [((4, part, width), BF16), ((local_rows, part), F32), ((local_rows, part), BF16)],
+        [((3, row_length, width), BF16)],
+        mine,
+        swap(mine),
+        normed_one,
+        grad_w_out,
+        *projections,
+    )
+    grad_normed_one = in_order(grad_part, swap(sent).astype(F32), 1)
+    _, unit_one, scale_one = norm_forward(inputs, attn_scale)
+    grad_input_norm, grad_attn = norm_backward(grad_normed_one, unit_one, scale_one, attn_scale)
     grad_tokens = grad_hidden + grad_input_norm
 
     small = jnp.concatenate([grad_attn[:, None], grad_ffn[:, None], grad_router], axis=1)

time: 519 us -> 467 us (0.90); the launches traced: 511 us -> 467 us
  local copies, waits for them, and re-layouts: 57.5 us -> 24.1 us
  Pallas kernels: 384 us -> 407 us
  other arithmetic: 39.9 us -> 18.3 us
  matrix products: 17.5 us -> 3.21 us
    pallas_call x0 -> x4, Pallas kernels: none -> 23.7 us  [local_call(): pl.pallas_call(kernel, out_shape=[jax.ShapeDtypeStruct(s, d) for s, d in...]
    unnamed x147 -> x103, local copies, waits for them, and re-layouts: 29.4 us -> 15.3 us
    slice x14 -> x0, local copies, waits for them, and re-layouts: 9.09 us -> none  [the longest x2 3.91 us: rotate(): upper_half = values[..., half_dim:]]
    another operation x5 -> x1, other arithmetic: 6.4 us -> 0.18 us  [the longest x1 3.33 us: tokens_path(): jnp.stack([matmul_left(normed_one, grad_qkv[k]) for k in range(3)] + [gra...]
  transfers between devices with their start and end apart: 11 -> 11, of which waited for: 2 -> 4; matrix products, arithmetic and copies ran while one was open for 11% -> 2% of each run, Pallas kernels for 26% -> 31%
where the time goes in v5:
time: 467 us
  Pallas kernels  407 us (87%)
  local copies, waits for them, and re-layouts  24.1 us (5%)
  other arithmetic  18.3 us (4%)
  starting transfers between devices  8.45 us (2%)
    pallas_call x1, Pallas kernels, exchange_wide(): pl.pallas_call(functools.partial(exchange_kernel, levels), out_shape=[sha...  129 us
    pallas_call x1, Pallas kernels, sum_dense(): pl.pallas_call(functools.partial(dense_kernel, levels, spans), out_shape=...  124 us
    pallas_call x1, Pallas kernels, experts_rows(): pl.pallas_call(functools.partial(experts_kernel, levels, (hidden, used, f...  124 us
    pallas_call x4, Pallas kernels, local_call(): pl.pallas_call(kernel, out_shape=[jax.ShapeDtypeStruct(s, d) for s, d in...  23.7 us
    unnamed x103, local copies, waits for them, and re-layouts  15.3 us
  transfers between devices with their start and end apart: 11, of which 4 were waited for; matrix products, arithmetic and copies ran while one was open for 2% of the time, Pallas kernels for 31%

profile of v5, /device:TPU:0, one launch (start us, length us, event | category | flops | bytes accessed | tf_op | source)
XLA Modules:
  0.0 466.6 jit_solution(10881148312311280555)
XLA Ops:
  2.8 1.4 constant_dynamic-slice_fusion.3
  9.2 1.4 copy-done.2
  12.6 5.0 %shard_map.289 = (bf16[256,640]{1,0:T(8,128)(2,1)S(1)}, f32[256,1920]{1,0:T(8,128)}, bf16[256,1920]{1,0:T(8,128)(2,1)S(1)}) custom-call(bf16[128,1280]{1,0:T(8,128)(2,1)S(1)} %copy-done.3, bf16[128,1280]{1,0:T(8,128)(2,1)S(1)} %copy-done.22, f32[1,1280]{1,0:T(1,128)S(1)} %get-tuple-element.160.scale_ref, bf16[640,1280]{1,0:T(8,128)(2,1)S(1)} %copy-done.1, ...), custom_call_target="tpu_custom_call" | custom-call | tf_op jit(solution)/shard_map/pallas_call | solution.py:1020
  17.8 1.5 dynamic-slice_select_fusion.sd_ref
  20.3 4.2 shard_map.290
  27.9 124.1 %shard_map.291 = (bf16[32,128,1280]{2,1,0:T(8,128)(2,1)}, bf16[32,128,1280]{2,1,0:T(8,128)(2,1)}, f32[32,16,128]{2,1,0:T(8,128)}, bf16[4096,1280]{1,0:T(8,128)(2...) custom-call(bf16[128,1280]{1,0:T(8,128)(2,1)} %multiply_convert_fusi, ...), custom_call_target="tpu_custom_call" | custom-call | tf_op jit(solution)/shard_map/pallas_call | solution.py:616
  152.1 5.7 %all-to-all-start = ((f32[16,2,128]{2,1,0:T(2,128)}), f32[16,2,128]{2,1,0:T(2,128)S(1)}, u32[]{:S(2)}, u32[]{:S(2)}) async-start(f32[16,2,128]{2,1,0:T(2,128)} %bitcast.77), calls=%async_computation | async-start | bytes 32768 | tf_op jit(solution)/shard_map/all_to_all | solution.py:1582
  157.8 128.7 %shard_map.292 = (bf16[128,1280]{1,0:T(8,128)(2,1)}, bf16[128,1280]{1,0:T(8,128)(2,1)}, bf16[16,96,1280]{2,1,0:T(8,128)(2,1)}) custom-call(bf16[32,128,1280]{2,1,0:T(8,128)(2,1)} %bitcast.81, bf16[32,128,1280]{2,1,0:T(8,128)(2,1)} %bitcast.82, bf16[96,1280]{1,0:T(8,128)(2,1)} %get-tuple-element.50.part_ref), custom_call_target="tpu_custom_call" | custom-call | flops 40000000000 | bytes 200000000 | tf_op jit(solution)/shard_map/pallas_call | solution.py:995
  289.0 2.0 multiply_reduce_fusion
  291.6 1.5 collective-permute-done.6.their_ref
  293.1 6.0 %shard_map.293 = (bf16[640,1280]{1,0:T(8,128)(2,1)S(1)}, bf16[3,256,640]{2,1,0:T(8,128)(2,1)}) custom-call(bf16[128,1280]{1,0:T(8,128)(2,1)S(1)} %fusion.18.branch_ref, bf16[128,1280]{1,0:T(8,128)(2,1)S(1)} %collective-permute-done.6.their_ref, bf16[256,640]{1,0:T(8,128)(2,1)S(1)} %copy-done.14, bf16[256,640]{1,0:T(8,128)(2,1)S(1)} %copy-done.16, ...), custom_call_target="tpu_custom_call" | custom-call | tf_op jit(solution)/shard_map/pallas_call | solution.py:1020
  299.2 2.1 copy-done.6
  301.4 6.1 %shard_map.296 = (f32[640,896]{1,0:T(8,128)}, f32[640,896]{1,0:T(8,128)}, f32[448,1280]{1,0:T(8,128)}) custom-call(bf16[16,96,1280]{2,1,0:T(8,128)(2,1)S(1)} %copy-done.6), custom_call_target="tpu_custom_call" | custom-call | tf_op jit(solution)/shard_map/pallas_call | solution.py:690
  307.6 8.5 %shard_map.294 = (bf16[4,640,1280]{2,1,0:T(8,128)(2,1)}, f32[128,640]{1,0:T(8,128)S(1)}, bf16[128,640]{1,0:T(8,128)(2,1)S(1)}) custom-call(bf16[3,256,640]{2,1,0:T(8,128)(2,1)} %get-tuple-element.58.mine_ref, bf16[3,256,640]{2,1,0:T(8,128)(2,1)} %collective-permute-done.7.their_ref, bf16[256,640]{1,0:T(8,128)(2,1)S(1)} %copy-done.12, ...), custom_call_target="tpu_custom_call" | custom-call | tf_op jit(solution)/shard_map/pallas_call | solution.py:1020
  320.8 124.2 %shard_map.295 = (bf16[16,160,1280]{2,1,0:T(8,128)(2,1)}, bf16[16,16,1280]{2,1,0:T(8,128)(2,1)}) custom-call(bf16[16,160,1280]{2,1,0:T(8,128)(2,1)} %bitcast.62, bf16[16,1280]{1,0:T(8,128)(2,1)} %reshape.161.flat_ref), custom_call_target="tpu_custom_call" | custom-call | tf_op jit(solution)/shard_map/pallas_call | solution.py:929
  445.1 1.3 copy.81
  447.9 3.4 fusion.20
  451.3 2.1 bitcast_convert_fusion
  453.3 2.1 bitcast_convert_fusion.1
  455.4 2.1 bitcast_convert_fusion.2
  457.4 2.1 bitcast_convert_fusion.3
  460.2 1.4 copy.85
  462.7 1.4 copy.86
  465.2 1.4 copy.87
  (171 shorter events, 25.6 us)
Async XLA Ops:
  0.7 6.7 %copy-start.41 = (s32[128,7]{0,1:T(8,128)S(1)}, s32[128,7]{0,1:T(8,128)}, u32[]{:S(2)}) copy-start(s32[128,7]{0,1:T(8,128)} %param.22) | copy-start | bytes 10756
  0.7 8.6 %copy-start.1 = (bf16[640,1280]{1,0:T(8,128)(2,1)S(1)}, bf16[640,1280]{1,0:T(8,128)(2,1)}, u32[]{:S(2)}) copy-start(bf16[640,1280]{1,0:T(8,128)(2,1)} %q_ref.3) | copy-start | bytes 4915204
  2.2 6.2 %collective-permute-start.1 = (bf16[2,640]{1,0:T(2,128)(2,1)S(1)}, bf16[2,640]{1,0:T(2,128)(2,1)S(1)}, u32[]{:S(2)}, u32[]{:S(2)}) collective-permute-start(bf16[2,640]{1,0:T(2,128)(2,1)S(1)} %pad_maximum_fusion.4), channel_id=1, source_target_pairs={{0,1},{1,0},{2,3},{3,2},{4,5},{5,4},{6,7},{7,6},{8,9},{9,8},{10,11... | collective-permute-start | bytes 7688 | tf_op jit(solution)/shard_map/ppermute | solution.py:1501
  2.7 5.8 %collective-permute-start = (bf16[128,1280]{1,0:T(8,128)(2,1)}, bf16[128,1280]{1,0:T(8,128)(2,1)S(1)}, u32[]{:S(2)}, u32[]{:S(2)}) collective-permute-start(bf16[128,1280]{1,0:T(8,128)(2,1)} %mine_ref.1), channel_id=1, source_target_pairs={{0,1},{1,0},{2,3},{3,2},{4,5},{5,4},{6,7},{7,6},{8,9},{9,8},{10,11... | collective-permute-start | bytes 983048 | tf_op jit(solution)/shard_map/ppermute | solution.py:1501
  5.3 20.2 %collective-permute-start.4 = (bf16[80,640]{1,0:T(8,128)(2,1)S(1)}, bf16[80,640]{1,0:T(8,128)(2,1)S(1)}, u32[]{:S(2)}, u32[]{:S(2)}) collective-permute-start(bf16[80,640]{1,0:T(8,128)(2,1)S(1)} %pad_maximum_fusion.3), channel_id=1, source_target_pairs={{0,1},{1,0},{2,3},{3,2},{4,5},{5,4},{6,7},{7,6},{8,9},{9,8},{10,11... | collective-permute-start | bytes 307208 | tf_op jit(solution)/shard_map/ppermute | solution.py:1501
  12.6 7.6 %copy-start = (bf16[640,1280]{1,0:T(8,128)(2,1)S(1)}, bf16[640,1280]{1,0:T(8,128)(2,1)}, u32[]{:S(2)}) copy-start(bf16[640,1280]{1,0:T(8,128)(2,1)} %out_w_ref.3) | copy-start | bytes 4915204
  12.6 7.6 %copy-start.7 = (f32[256,128]{1,0:T(8,128)S(1)}, f32[256,128]{1,0:T(8,128)}, u32[]{:S(2)}) copy-start(f32[256,128]{1,0:T(8,128)} %pad_maximum_fusion.1.sin_ref) | copy-start | bytes 393220
  12.6 7.6 %copy-start.9 = (f32[256,128]{1,0:T(8,128)S(1)}, f32[256,128]{1,0:T(8,128)}, u32[]{:S(2)}) copy-start(f32[256,128]{1,0:T(8,128)} %pad_maximum_fusion.cos_ref) | copy-start | bytes 393220
  17.7 6.8 %copy-start.11 = (bf16[256,640]{1,0:T(8,128)(2,1)}, bf16[256,640]{1,0:T(8,128)(2,1)S(1)}, u32[]{:S(2)}) copy-start(bf16[256,640]{1,0:T(8,128)(2,1)S(1)} %get-tuple-element.59.n_ref) | copy-start | bytes 983044
  17.7 2.6 collective-permute-start.2
  24.5 1.7 collective-permute-start.3
  27.0 264.1 %copy-start.23 = (f32[128,1280]{1,0:T(8,128)}, f32[128,1280]{1,0:T(8,128)S(1)}, u32[]{:S(2)}) copy-start(f32[128,1280]{1,0:T(8,128)S(1)} %get-tuple-element.146) | copy-start | bytes 1966084
  27.0 264.1 %copy-start.39 = (f32[128]{0:T(128)}, f32[128]{0:T(128)S(1)}, u32[]{:S(2)}) copy-start(f32[128]{0:T(128)S(1)} %add_rsqrt_fusion.1) | copy-start | bytes 1540
  152.1 135.5 %all-to-all-start = ((f32[16,2,128]{2,1,0:T(2,128)}), f32[16,2,128]{2,1,0:T(2,128)S(1)}, u32[]{:S(2)}, u32[]{:S(2)}) async-start(f32[16,2,128]{2,1,0:T(2,128)} %bitcast.77), calls=%async_computation | async-start | bytes 32768 | tf_op jit(solution)/shard_map/all_to_all | solution.py:1582
  157.8 128.7 %copy-start.27 = (bf16[128,1280]{1,0:T(8,128)(2,1)S(1)}, bf16[128,1280]{1,0:T(8,128)(2,1)}, u32[]{:S(2)}) copy-start(bf16[128,1280]{1,0:T(8,128)(2,1)} %multiply_convert_fusion.x_ref) | copy-start | bytes 983044
  287.7 1.2 collective-permute-start.5
  291.3 1.7 collective-permute-start.6
  299.1 8.4 %collective-permute-start.7 = (bf16[3,256,640]{2,1,0:T(8,128)(2,1)}, bf16[3,256,640]{2,1,0:T(8,128)(2,1)}, u32[]{:S(2)}, u32[]{:S(2)}) collective-permute-start(bf16[3,256,640]{2,1,0:T(8,128)(2,1)} %get-tuple-element.58.mine_ref), channel_id=1, source_target_pairs={{0,1},{1,0},{2,3},{3,2},{4,5},{5,4},{6,7},{7,6},{8,9},{9,8},{10,11... | collective-permute-start | bytes 2949128 | tf_op jit(solution)/shard_map/ppermute | solution.py:1501
  301.3 6.2 %copy-start.12 = (bf16[256,640]{1,0:T(8,128)(2,1)S(1)}, bf16[256,640]{1,0:T(8,128)(2,1)}, u32[]{:S(2)}) copy-start(bf16[256,640]{1,0:T(8,128)(2,1)} %copy-done.11) | copy-start | bytes 983044
  307.5 9.0 %copy-start.28 = (bf16[128,1280]{1,0:T(8,128)(2,1)S(1)}, bf16[128,1280]{1,0:T(8,128)(2,1)}, u32[]{:S(2)}) copy-start(bf16[128,1280]{1,0:T(8,128)(2,1)} %multiply_convert_fusion.x_ref) | copy-start | bytes 983044
  307.5 9.0 %copy-start.37 = (bf16[128,16]{0,1:T(8,128)(2,1)S(1)}, bf16[128,16]{0,1:T(8,128)(2,1)}, u32[]{:S(2)}) copy-start(bf16[128,16]{0,1:T(8,128)(2,1)} %copy-done.36) | copy-start | bytes 12292
  307.5 10.0 %copy-start.5 = (bf16[128,1280]{1,0:T(8,128)(2,1)S(1)}, bf16[128,1280]{1,0:T(8,128)(2,1)}, u32[]{:S(2)}) copy-start(bf16[128,1280]{1,0:T(8,128)(2,1)} %mine_ref.1) | copy-start | bytes 983044
  316.1 1.5 collective-permute-start.8
  318.0 1.7 collective-permute-start.9
  (34 other events, 116.9 us)

commit v6 on v5

--- a/solution.py
+++ b/solution.py
@@ -418,7 +418,7 @@
         if end > row:
             ref[row:end, :] = jnp.zeros((end - row, ref.shape[1]), BF16)
     place = at.level * 4 + at.spot
-    units = 4 * levels
+    units, ahead = 4 * levels, 3
     plan = [(0, 0)]
     for s in range(1, levels + 2):
         if s < levels:
@@ -577,10 +577,16 @@
         copy.wait()
 
     def loop(k, carry):
-        pl.when((k > 0) & (k + 1 < units))(lambda: serve(k + 1))
+        pl.when((k > 0) & (k + 1 < units))(lambda: fetch(k + 1))
         forward(k)
-        pl.when(k == 0)(lambda: serve(1))
-        pl.when(k + 1 < units)(lambda: fetch(k + 1))
+
+        @pl.when(k == 0)
+        def _():
+            for n in range(1, ahead + 1):
+                serve(n)
+            fetch(1)
+
+        pl.when((k > 0) & (k + ahead < units))(lambda: serve(k + ahead))
         backward(k)
         return carry
 
@@ -702,7 +708,7 @@
             vmem((stored, width), BF16),
             pltpu.SemaphoreType.DMA((5 * slices,)),
         ],
-        compiler_params=pltpu.CompilerParams(vmem_limit_bytes=32 * 1024 * 1024),
+        compiler_params=pltpu.CompilerParams(vmem_limit_bytes=60 * 1024 * 1024),
     )(gathered)
 
 
@@ -1127,6 +1133,39 @@
     dense_ref[3] = grad_w_ref[...]
     part_ref[...] = total[:half]
     send_ref[...] = total[half:].astype(BF16)
+
+
+def widen_kernel(steps, x_ref, *refs):
+    count = (len(refs) - 4) // 2
+    step = pl.program_id(0)
+    for n in range(count):
+        refs[count + n][...] = refs[n][...]
+    for n, ref in enumerate(refs[2 * count :]):
+
+        @pl.when(step // steps == n)
+        def _(ref=ref):
+            ref[...] = x_ref[...].reshape(ref.shape).astype(F32)
+
+
+def widen(gathered, passed):
+    blocks, rows, width = gathered.shape
+    each = 2 if blocks % 8 == 0 else 1
+    grid, steps = blocks // each, blocks // each // 4
+    shape = jax.ShapeDtypeStruct
+
+    def spec(n):
+        return pl.BlockSpec((each * rows, width), lambda i: (jnp.clip(i - steps * n, 0, steps - 1), 0))
+
+    copied = [pl.BlockSpec((x.shape[0] // grid, width), lambda i: (i, 0)) for x in passed]
+    return pl.pallas_call(
+        functools.partial(widen_kernel, steps),
+        grid=(grid,),
+        out_shape=[shape(x.shape, x.dtype) for x in passed]
+        + [shape((blocks // 4 * rows, width), F32)] * 4,
+        in_specs=[pl.BlockSpec((each, rows, width), lambda i: (i, 0, 0))] + copied,
+        out_specs=copied + [spec(n) for n in range(4)],
+        compiler_params=pltpu.CompilerParams(vmem_limit_bytes=60 * 1024 * 1024),
+    )(gathered, *passed)
 
 
 def slots_path(
@@ -1590,7 +1629,6 @@
         grad_rows.reshape(block_shape), expert_out.reshape(block_shape), shared_part, levels, 2
     )
     output = (hidden + expert_out.astype(F32)).astype(BF16)
-    grad_expert_gate, grad_expert_up, grad_expert_down = expert_grads
     grad_shared_gate, grad_shared_up, grad_shared_down = shared_grads(
         shared_all, slices, part, stored
     )
@@ -1646,17 +1684,18 @@
     everything, flat = sum_dense(
         grad_dense.reshape(wide_size, sum_rows, width), flat.reshape(extra_rows, width), levels, 3
     )
-    owned = everything.reshape(4, part, width)
+    *expert_grads, grad_query, grad_key, grad_value, grad_out = widen(everything, expert_grads)
+    grad_expert_gate, grad_expert_up, grad_expert_down = expert_grads
     flat = flat.astype(F32).reshape(wide_size, -1)
     small = jnp.sum(flat[:, :size], axis=0).reshape(part, 2 + experts)
     return (
         output,
         grad_tokens,
         small[:, 0],
-        owned[0].astype(F32),
-        owned[1].astype(F32),
-        owned[2].astype(F32),
-        owned[3].astype(F32),
+        grad_query,
+        grad_key,
+        grad_value,
+        grad_out,
         small[:, 1],
         small[:, 2:],
         grad_shared_gate,

time: 467 us -> 461 us (0.987)
  Pallas kernels: 407 us -> 414 us
  other arithmetic: 18.3 us -> 11.4 us
  local copies, waits for them, and re-layouts: 24.1 us -> 18 us
    pallas_call x0 -> x1, Pallas kernels: none -> 13.9 us  [widen(): pl.pallas_call(functools.partial(widen_kernel, steps), grid=(grid,), out_...]
    convert_element_type x4 -> x0, other arithmetic: 8.22 us -> none  [the longest x1 2.05 us: tokens_path(): owned[3].astype(F32)]
    pallas_call x1, Pallas kernels: 124 us -> 117 us  [experts_rows(): pl.pallas_call(functools.partial(experts_kernel, levels, (hidden, used, f...]
    unnamed x103 -> x90, local copies, waits for them, and re-layouts: 15.3 us -> 12.5 us
  transfers between devices with their start and end apart: 11 -> 11, of which waited for: 4 -> 4; matrix products, arithmetic and copies ran while one was open for 2% -> 3% of each run, Pallas kernels for 31% -> 31%
where the time goes in v6:
time: 461 us; the launch traced here: 459 us
  Pallas kernels  414 us (90%)
  local copies, waits for them, and re-layouts  18 us (4%)
  other arithmetic  11.4 us (2%)
  starting transfers between devices  7.53 us (2%)
    pallas_call x1, Pallas kernels, exchange_wide(): pl.pallas_call(functools.partial(exchange_kernel, levels), out_shape=[sha...  129 us
    pallas_call x1, Pallas kernels, sum_dense(): pl.pallas_call(functools.partial(dense_kernel, levels, spans), out_shape=...  124 us
    pallas_call x1, Pallas kernels, experts_rows(): pl.pallas_call(functools.partial(experts_kernel, levels, (hidden, used, f...  117 us
    pallas_call x4, Pallas kernels, local_call(): pl.pallas_call(kernel, out_shape=[jax.ShapeDtypeStruct(s, d) for s, d in...  23.6 us
    pallas_call x1, Pallas kernels, widen(): pl.pallas_call(functools.partial(widen_kernel, steps), grid=(grid,), out_...  13.9 us
    unnamed x90, local copies, waits for them, and re-layouts  12.5 us
  transfers between devices with their start and end apart: 11, of which 4 were waited for; matrix products, arithmetic and copies ran while one was open for 3% of the time, Pallas kernels for 31%

profile of v6, /device:TPU:0, one launch (start us, length us, event | category | flops | bytes accessed | tf_op | source)
XLA Modules:
  0.0 459.5 jit_solution(6239307451895551892)
XLA Ops:
  2.8 1.4 constant_dynamic-slice_fusion.3
  10.5 1.4 copy-done.2
  12.0 1.0 copy-done.3
  12.9 1.0 copy-done.21
  13.9 5.0 %shard_map.289 = (bf16[256,640]{1,0:T(8,128)(2,1)S(1)}, f32[256,1920]{1,0:T(8,128)}, bf16[256,1920]{1,0:T(8,128)(2,1)S(1)}) custom-call(bf16[128,1280]{1,0:T(8,128)(2,1)S(1)} %copy-done.3, bf16[128,1280]{1,0:T(8,128)(2,1)S(1)} %copy-done.21, f32[1,1280]{1,0:T(1,128)S(1)} %get-tuple-element.170.scale_ref, bf16[640,1280]{1,0:T(8,128)(2,1)S(1)} %copy-done.1, ...), custom_call_target="tpu_custom_call" | custom-call | tf_op jit(solution)/shard_map/pallas_call | solution.py:1026
  19.1 1.5 dynamic-slice_select_fusion.sd_ref
  21.5 4.2 shard_map.290
  29.2 117.4 %shard_map.291 = (bf16[32,128,1280]{2,1,0:T(8,128)(2,1)}, bf16[32,128,1280]{2,1,0:T(8,128)(2,1)}, f32[32,16,128]{2,1,0:T(8,128)}, bf16[4096,1280]{1,0:T(8,128)(2...) custom-call(bf16[128,1280]{1,0:T(8,128)(2,1)} %multiply_convert_fusi, ...), custom_call_target="tpu_custom_call" | custom-call | tf_op jit(solution)/shard_map/pallas_call | solution.py:622
  146.6 4.8 %all-to-all-start = ((f32[16,2,128]{2,1,0:T(2,128)}), f32[16,2,128]{2,1,0:T(2,128)S(1)}, u32[]{:S(2)}, u32[]{:S(2)}) async-start(f32[16,2,128]{2,1,0:T(2,128)} %bitcast.62), calls=%async_computation | async-start | bytes 32768 | tf_op jit(solution)/shard_map/all_to_all | solution.py:1621
  151.4 128.7 %shard_map.292 = (bf16[128,1280]{1,0:T(8,128)(2,1)}, bf16[128,1280]{1,0:T(8,128)(2,1)}, bf16[16,96,1280]{2,1,0:T(8,128)(2,1)}) custom-call(bf16[32,128,1280]{2,1,0:T(8,128)(2,1)} %bitcast.66, bf16[32,128,1280]{2,1,0:T(8,128)(2,1)} %bitcast.67, bf16[96,1280]{1,0:T(8,128)(2,1)} %get-tuple-element.57.part_ref), custom_call_target="tpu_custom_call" | custom-call | flops 40000000000 | bytes 200000000 | tf_op jit(solution)/shard_map/pallas_call | solution.py:1001
  280.2 1.0 fusion.21
  281.4 1.1 collective-permute-done.5
  282.6 2.0 multiply_reduce_fusion
  285.1 1.5 collective-permute-done.6.their_ref
  288.4 1.0 copy-done.13
  290.4 1.0 copy-done.17
  291.3 1.0 copy-done.19
  292.3 5.9 %shard_map.293 = (bf16[640,1280]{1,0:T(8,128)(2,1)S(1)}, bf16[3,256,640]{2,1,0:T(8,128)(2,1)}) custom-call(bf16[128,1280]{1,0:T(8,128)(2,1)S(1)} %fusion.18.branch_ref, bf16[128,1280]{1,0:T(8,128)(2,1)S(1)} %collective-permute-done.6.their_ref, bf16[256,640]{1,0:T(8,128)(2,1)S(1)} %copy-done.13, bf16[256,640]{1,0:T(8,128)(2,1)S(1)} %copy-done.15, ...), custom_call_target="tpu_custom_call" | custom-call | tf_op jit(solution)/shard_map/pallas_call | solution.py:1026
  298.4 5.9 %shard_map.297 = (f32[640,896]{1,0:T(8,128)}, f32[640,896]{1,0:T(8,128)}, f32[448,1280]{1,0:T(8,128)}) custom-call(bf16[16,96,1280]{2,1,0:T(8,128)(2,1)} %get-tuple-element.80.x_ref), custom_call_target="tpu_custom_call" | custom-call | tf_op jit(solution)/shard_map/pallas_call | solution.py:696
  304.5 8.5 %shard_map.294 = (bf16[4,640,1280]{2,1,0:T(8,128)(2,1)}, f32[128,640]{1,0:T(8,128)S(1)}, bf16[128,640]{1,0:T(8,128)(2,1)S(1)}) custom-call(bf16[3,256,640]{2,1,0:T(8,128)(2,1)} %get-tuple-element.65.mine_ref, bf16[3,256,640]{2,1,0:T(8,128)(2,1)} %collective-permute-done.7.their_ref, bf16[256,640]{1,0:T(8,128)(2,1)S(1)} %copy-done.11, ...), custom_call_target="tpu_custom_call" | custom-call | tf_op jit(solution)/shard_map/pallas_call | solution.py:1026
  315.3 1.3 fusion.6
  317.8 124.2 %shard_map.295 = (bf16[16,160,1280]{2,1,0:T(8,128)(2,1)}, bf16[16,16,1280]{2,1,0:T(8,128)(2,1)}) custom-call(bf16[16,160,1280]{2,1,0:T(8,128)(2,1)} %bitcast.50, bf16[16,1280]{1,0:T(8,128)(2,1)} %reshape.144.flat_ref), custom_call_target="tpu_custom_call" | custom-call | tf_op jit(solution)/shard_map/pallas_call | solution.py:935
  442.0 1.3 copy.81
  445.6 13.9 %shard_map.296 = (f32[448,1280]{1,0:T(8,128)}, f32[448,1280]{1,0:T(8,128)}, f32[448,1280]{1,0:T(8,128)}, f32[640,1280]{1,0:T(8,128)}, f32[640,1280]{1,0:T(8,128)...) custom-call(bf16[16,160,1280]{2,1,0:T(8,128)(2,1)} %get-tuple-element.72.x_ref, f32[448,1280]{1,0:T(8,128)} %get-tuple-element.73.refs_0_, ...), custom_call_target="tpu_custom_call" | custom-call | tf_op jit(solution)/shard_map/pallas_call | solution.py:1160
  (154 shorter events, 22.2 us)
Async XLA Ops:
  0.6 8.0 %copy-start.37 = (s32[128,7]{0,1:T(8,128)S(1)}, s32[128,7]{0,1:T(8,128)}, u32[]{:S(2)}) copy-start(s32[128,7]{0,1:T(8,128)} %param.22) | copy-start | bytes 10756
  0.7 9.9 %copy-start.1 = (bf16[640,1280]{1,0:T(8,128)(2,1)S(1)}, bf16[640,1280]{1,0:T(8,128)(2,1)}, u32[]{:S(2)}) copy-start(bf16[640,1280]{1,0:T(8,128)(2,1)} %q_ref.3) | copy-start | bytes 4915204
  2.2 7.5 %collective-permute-start.1 = (bf16[2,640]{1,0:T(2,128)(2,1)S(1)}, bf16[2,640]{1,0:T(2,128)(2,1)S(1)}, u32[]{:S(2)}, u32[]{:S(2)}) collective-permute-start(bf16[2,640]{1,0:T(2,128)(2,1)S(1)} %pad_maximum_fusion.4), channel_id=1, source_target_pairs={{0,1},{1,0},{2,3},{3,2},{4,5},{5,4},{6,7},{7,6},{8,9},{9,8},{10,11... | collective-permute-start | bytes 7688 | tf_op jit(solution)/shard_map/ppermute | solution.py:1540
  2.7 7.1 %collective-permute-start = (bf16[128,1280]{1,0:T(8,128)(2,1)}, bf16[128,1280]{1,0:T(8,128)(2,1)S(1)}, u32[]{:S(2)}, u32[]{:S(2)}) collective-permute-start(bf16[128,1280]{1,0:T(8,128)(2,1)} %mine_ref.1), channel_id=1, source_target_pairs={{0,1},{1,0},{2,3},{3,2},{4,5},{5,4},{6,7},{7,6},{8,9},{9,8},{10,11... | collective-permute-start | bytes 983048 | tf_op jit(solution)/shard_map/ppermute | solution.py:1540
  5.3 21.5 %collective-permute-start.4 = (bf16[80,640]{1,0:T(8,128)(2,1)S(1)}, bf16[80,640]{1,0:T(8,128)(2,1)S(1)}, u32[]{:S(2)}, u32[]{:S(2)}) collective-permute-start(bf16[80,640]{1,0:T(8,128)(2,1)S(1)} %pad_maximum_fusion.3), channel_id=1, source_target_pairs={{0,1},{1,0},{2,3},{3,2},{4,5},{5,4},{6,7},{7,6},{8,9},{9,8},{10,11... | collective-permute-start | bytes 307208 | tf_op jit(solution)/shard_map/ppermute | solution.py:1540
  13.9 7.6 %copy-start = (bf16[640,1280]{1,0:T(8,128)(2,1)S(1)}, bf16[640,1280]{1,0:T(8,128)(2,1)}, u32[]{:S(2)}) copy-start(bf16[640,1280]{1,0:T(8,128)(2,1)} %out_w_ref.3) | copy-start | bytes 4915204
  13.9 7.6 %copy-start.6 = (f32[256,128]{1,0:T(8,128)S(1)}, f32[256,128]{1,0:T(8,128)}, u32[]{:S(2)}) copy-start(f32[256,128]{1,0:T(8,128)} %pad_maximum_fusion.1.sin_ref) | copy-start | bytes 393220
  13.9 7.6 %copy-start.8 = (f32[256,128]{1,0:T(8,128)S(1)}, f32[256,128]{1,0:T(8,128)}, u32[]{:S(2)}) copy-start(f32[256,128]{1,0:T(8,128)} %pad_maximum_fusion.cos_ref) | copy-start | bytes 393220
  18.9 2.6 collective-permute-start.2
  25.8 1.7 collective-permute-start.3
  28.3 256.4 %copy-start.22 = (f32[128,1280]{1,0:T(8,128)}, f32[128,1280]{1,0:T(8,128)S(1)}, u32[]{:S(2)}) copy-start(f32[128,1280]{1,0:T(8,128)S(1)} %get-tuple-element.160) | copy-start | bytes 1966084
  28.3 256.3 %copy-start.35 = (f32[128]{0:T(128)}, f32[128]{0:T(128)S(1)}, u32[]{:S(2)}) copy-start(f32[128]{0:T(128)S(1)} %add_rsqrt_fusion.1) | copy-start | bytes 1540
  146.6 134.6 %all-to-all-start = ((f32[16,2,128]{2,1,0:T(2,128)}), f32[16,2,128]{2,1,0:T(2,128)S(1)}, u32[]{:S(2)}, u32[]{:S(2)}) async-start(f32[16,2,128]{2,1,0:T(2,128)} %bitcast.62), calls=%async_computation | async-start | bytes 32768 | tf_op jit(solution)/shard_map/all_to_all | solution.py:1621
  151.4 128.7 %copy-start.26 = (bf16[128,1280]{1,0:T(8,128)(2,1)S(1)}, bf16[128,1280]{1,0:T(8,128)(2,1)}, u32[]{:S(2)}) copy-start(bf16[128,1280]{1,0:T(8,128)(2,1)} %multiply_convert_fusion.x_ref) | copy-start | bytes 983044
  281.3 1.2 collective-permute-start.5
  284.9 1.7 collective-permute-start.6
  298.3 6.2 %collective-permute-start.7 = (bf16[3,256,640]{2,1,0:T(8,128)(2,1)}, bf16[3,256,640]{2,1,0:T(8,128)(2,1)}, u32[]{:S(2)}, u32[]{:S(2)}) collective-permute-start(bf16[3,256,640]{2,1,0:T(8,128)(2,1)} %get-tuple-element.65.mine_ref), channel_id=1, source_target_pairs={{0,1},{1,0},{2,3},{3,2},{4,5},{5,4},{6,7},{7,6},{8,9},{9,8},{10,11... | collective-permute-start | bytes 2949128 | tf_op jit(solution)/shard_map/ppermute | solution.py:1540
  304.4 9.0 %copy-start.27 = (bf16[128,1280]{1,0:T(8,128)(2,1)S(1)}, bf16[128,1280]{1,0:T(8,128)(2,1)}, u32[]{:S(2)}) copy-start(bf16[128,1280]{1,0:T(8,128)(2,1)} %multiply_convert_fusion.x_ref) | copy-start | bytes 983044
  304.4 9.0 %copy-start.33 = (bf16[128,16]{0,1:T(8,128)(2,1)S(1)}, bf16[128,16]{0,1:T(8,128)(2,1)}, u32[]{:S(2)}) copy-start(bf16[128,16]{0,1:T(8,128)(2,1)} %copy-done.32) | copy-start | bytes 12292
  304.5 10.1 %copy-start.5 = (bf16[128,1280]{1,0:T(8,128)(2,1)S(1)}, bf16[128,1280]{1,0:T(8,128)(2,1)}, u32[]{:S(2)}) copy-start(bf16[128,1280]{1,0:T(8,128)(2,1)} %mine_ref.1) | copy-start | bytes 983044
  304.5 10.8 %copy-start.36 = (f32[128]{0:T(128)S(1)}, f32[128]{0:T(128)}, u32[]{:S(2)}) copy-start(f32[128]{0:T(128)} %copy-done.35) | copy-start | bytes 1540
  304.5 10.8 %copy-start.40 = (f32[128]{0:T(128)S(1)}, f32[128]{0:T(128)}, u32[]{:S(2)}) copy-start(f32[128]{0:T(128)} %copy-done.39) | copy-start | bytes 1540
  313.0 1.5 collective-permute-start.8
  314.9 1.7 collective-permute-start.9
  (29 other events, 83.0 us)

commit v7 on v6

--- a/solution.py
+++ b/solution.py
@@ -915,7 +915,7 @@
     for task in scatters:
         task.begin()
     steps = []
-    for n, lag in enumerate((0, 7)):
+    for n, lag in enumerate((0, 5.5)):
         begin = len(scatters[n].steps()) + lag
         steps += [(s + lag, n, step) for s, step in enumerate(scatters[n].steps())]
         steps.append((begin - 0.5, n, gathers[n].begin))
@@ -984,7 +984,7 @@
     gather.begin()
     steps = [(s, 0, step) for s, step in enumerate(first.steps())]
     steps += [(s + 7, 1, step) for s, step in enumerate(second.steps())]
-    steps += [(s + 2, 2, step) for s, step in enumerate(gather.steps())]
+    steps += [(s + 8, 2, step) for s, step in enumerate(gather.steps())]
     for _, _, step in sorted(steps, key=lambda entry: entry[:2]):
         step()
     sent(sends)

time: 461 us -> 456 us (0.989)
  no operation moved by 1% of the time
where the time goes in v7:
time: 456 us; the launch traced here: 455 us
  Pallas kernels  410 us (90%)
  local copies, waits for them, and re-layouts  18 us (4%)
  other arithmetic  11.4 us (2%)
  starting transfers between devices  7.53 us (2%)
    pallas_call x1, Pallas kernels, exchange_wide(): pl.pallas_call(functools.partial(exchange_kernel, levels), out_shape=[sha...  127 us
    pallas_call x1, Pallas kernels, sum_dense(): pl.pallas_call(functools.partial(dense_kernel, levels, spans), out_shape=...  122 us
    pallas_call x1, Pallas kernels, experts_rows(): pl.pallas_call(functools.partial(experts_kernel, levels, (hidden, used, f...  117 us
    pallas_call x4, Pallas kernels, local_call(): pl.pallas_call(kernel, out_shape=[jax.ShapeDtypeStruct(s, d) for s, d in...  23.6 us
    pallas_call x1, Pallas kernels, widen(): pl.pallas_call(functools.partial(widen_kernel, steps), grid=(grid,), out_...  13.9 us
    unnamed x90, local copies, waits for them, and re-layouts  12.5 us
  transfers between devices with their start and end apart: 11, of which 4 were waited for; matrix products, arithmetic and copies ran while one was open for 3% of the time, Pallas kernels for 31%

profile of v7, /device:TPU:0, one launch (start us, length us, event | category | flops | bytes accessed | tf_op | source)
XLA Modules:
  0.0 455.3 jit_solution(12346160551970873102)
XLA Ops:
  2.8 1.4 constant_dynamic-slice_fusion.3
  10.5 1.4 copy-done.2
  12.0 1.0 copy-done.3
  12.9 1.0 copy-done.21
  13.9 5.0 %shard_map.289 = (bf16[256,640]{1,0:T(8,128)(2,1)S(1)}, f32[256,1920]{1,0:T(8,128)}, bf16[256,1920]{1,0:T(8,128)(2,1)S(1)}) custom-call(bf16[128,1280]{1,0:T(8,128)(2,1)S(1)} %copy-done.3, bf16[128,1280]{1,0:T(8,128)(2,1)S(1)} %copy-done.21, f32[1,1280]{1,0:T(1,128)S(1)} %get-tuple-element.170.scale_ref, bf16[640,1280]{1,0:T(8,128)(2,1)S(1)} %copy-done.1, ...), custom_call_target="tpu_custom_call" | custom-call | tf_op jit(solution)/shard_map/pallas_call | solution.py:1026
  19.1 1.5 dynamic-slice_select_fusion.sd_ref
  21.5 4.2 shard_map.290
  29.2 117.4 %shard_map.291 = (bf16[32,128,1280]{2,1,0:T(8,128)(2,1)}, bf16[32,128,1280]{2,1,0:T(8,128)(2,1)}, f32[32,16,128]{2,1,0:T(8,128)}, bf16[4096,1280]{1,0:T(8,128)(2...) custom-call(bf16[128,1280]{1,0:T(8,128)(2,1)} %multiply_convert_fusi, ...), custom_call_target="tpu_custom_call" | custom-call | tf_op jit(solution)/shard_map/pallas_call | solution.py:622
  146.6 4.8 %all-to-all-start = ((f32[16,2,128]{2,1,0:T(2,128)}), f32[16,2,128]{2,1,0:T(2,128)S(1)}, u32[]{:S(2)}, u32[]{:S(2)}) async-start(f32[16,2,128]{2,1,0:T(2,128)} %bitcast.62), calls=%async_computation | async-start | bytes 32768 | tf_op jit(solution)/shard_map/all_to_all | solution.py:1621
  151.4 126.6 %shard_map.292 = (bf16[128,1280]{1,0:T(8,128)(2,1)}, bf16[128,1280]{1,0:T(8,128)(2,1)}, bf16[16,96,1280]{2,1,0:T(8,128)(2,1)}) custom-call(bf16[32,128,1280]{2,1,0:T(8,128)(2,1)} %bitcast.66, bf16[32,128,1280]{2,1,0:T(8,128)(2,1)} %bitcast.67, bf16[96,1280]{1,0:T(8,128)(2,1)} %get-tuple-element.57.part_ref), custom_call_target="tpu_custom_call" | custom-call | flops 40000000000 | bytes 200000000 | tf_op jit(solution)/shard_map/pallas_call | solution.py:1001
  278.1 1.0 fusion.21
  279.3 1.1 collective-permute-done.5
  280.5 2.0 multiply_reduce_fusion
  283.1 1.5 collective-permute-done.6.their_ref
  286.3 1.0 copy-done.13
  287.3 1.0 copy-done.15
  288.3 1.0 copy-done.17
  290.2 5.9 %shard_map.293 = (bf16[640,1280]{1,0:T(8,128)(2,1)S(1)}, bf16[3,256,640]{2,1,0:T(8,128)(2,1)}) custom-call(bf16[128,1280]{1,0:T(8,128)(2,1)S(1)} %fusion.18.branch_ref, bf16[128,1280]{1,0:T(8,128)(2,1)S(1)} %collective-permute-done.6.their_ref, bf16[256,640]{1,0:T(8,128)(2,1)S(1)} %copy-done.13, bf16[256,640]{1,0:T(8,128)(2,1)S(1)} %copy-done.15, ...), custom_call_target="tpu_custom_call" | custom-call | tf_op jit(solution)/shard_map/pallas_call | solution.py:1026
  296.3 5.9 %shard_map.297 = (f32[640,896]{1,0:T(8,128)}, f32[640,896]{1,0:T(8,128)}, f32[448,1280]{1,0:T(8,128)}) custom-call(bf16[16,96,1280]{2,1,0:T(8,128)(2,1)} %get-tuple-element.80.x_ref), custom_call_target="tpu_custom_call" | custom-call | tf_op jit(solution)/shard_map/pallas_call | solution.py:696
  302.4 8.5 %shard_map.294 = (bf16[4,640,1280]{2,1,0:T(8,128)(2,1)}, f32[128,640]{1,0:T(8,128)S(1)}, bf16[128,640]{1,0:T(8,128)(2,1)S(1)}) custom-call(bf16[3,256,640]{2,1,0:T(8,128)(2,1)} %get-tuple-element.65.mine_ref, bf16[3,256,640]{2,1,0:T(8,128)(2,1)} %collective-permute-done.7.their_ref, bf16[256,640]{1,0:T(8,128)(2,1)S(1)} %copy-done.11, ...), custom_call_target="tpu_custom_call" | custom-call | tf_op jit(solution)/shard_map/pallas_call | solution.py:1026
  313.2 1.3 fusion.6
  315.7 122.1 %shard_map.295 = (bf16[16,160,1280]{2,1,0:T(8,128)(2,1)}, bf16[16,16,1280]{2,1,0:T(8,128)(2,1)}) custom-call(bf16[16,160,1280]{2,1,0:T(8,128)(2,1)} %bitcast.50, bf16[16,1280]{1,0:T(8,128)(2,1)} %reshape.144.flat_ref), custom_call_target="tpu_custom_call" | custom-call | tf_op jit(solution)/shard_map/pallas_call | solution.py:935
  437.8 1.3 copy.81
  441.4 13.9 %shard_map.296 = (f32[448,1280]{1,0:T(8,128)}, f32[448,1280]{1,0:T(8,128)}, f32[448,1280]{1,0:T(8,128)}, f32[640,1280]{1,0:T(8,128)}, f32[640,1280]{1,0:T(8,128)...) custom-call(bf16[16,160,1280]{2,1,0:T(8,128)(2,1)} %get-tuple-element.72.x_ref, f32[448,1280]{1,0:T(8,128)} %get-tuple-element.73.refs_0_, ...), custom_call_target="tpu_custom_call" | custom-call | tf_op jit(solution)/shard_map/pallas_call | solution.py:1160
  (154 shorter events, 22.2 us)
Async XLA Ops:
  0.6 8.0 %copy-start.37 = (s32[128,7]{0,1:T(8,128)S(1)}, s32[128,7]{0,1:T(8,128)}, u32[]{:S(2)}) copy-start(s32[128,7]{0,1:T(8,128)} %param.22) | copy-start | bytes 10756
  0.7 9.9 %copy-start.1 = (bf16[640,1280]{1,0:T(8,128)(2,1)S(1)}, bf16[640,1280]{1,0:T(8,128)(2,1)}, u32[]{:S(2)}) copy-start(bf16[640,1280]{1,0:T(8,128)(2,1)} %q_ref.3) | copy-start | bytes 4915204
  2.2 7.5 %collective-permute-start.1 = (bf16[2,640]{1,0:T(2,128)(2,1)S(1)}, bf16[2,640]{1,0:T(2,128)(2,1)S(1)}, u32[]{:S(2)}, u32[]{:S(2)}) collective-permute-start(bf16[2,640]{1,0:T(2,128)(2,1)S(1)} %pad_maximum_fusion.4), channel_id=1, source_target_pairs={{0,1},{1,0},{2,3},{3,2},{4,5},{5,4},{6,7},{7,6},{8,9},{9,8},{10,11... | collective-permute-start | bytes 7688 | tf_op jit(solution)/shard_map/ppermute | solution.py:1540
  2.7 7.1 %collective-permute-start = (bf16[128,1280]{1,0:T(8,128)(2,1)}, bf16[128,1280]{1,0:T(8,128)(2,1)S(1)}, u32[]{:S(2)}, u32[]{:S(2)}) collective-permute-start(bf16[128,1280]{1,0:T(8,128)(2,1)} %mine_ref.1), channel_id=1, source_target_pairs={{0,1},{1,0},{2,3},{3,2},{4,5},{5,4},{6,7},{7,6},{8,9},{9,8},{10,11... | collective-permute-start | bytes 983048 | tf_op jit(solution)/shard_map/ppermute | solution.py:1540
  5.3 21.5 %collective-permute-start.4 = (bf16[80,640]{1,0:T(8,128)(2,1)S(1)}, bf16[80,640]{1,0:T(8,128)(2,1)S(1)}, u32[]{:S(2)}, u32[]{:S(2)}) collective-permute-start(bf16[80,640]{1,0:T(8,128)(2,1)S(1)} %pad_maximum_fusion.3), channel_id=1, source_target_pairs={{0,1},{1,0},{2,3},{3,2},{4,5},{5,4},{6,7},{7,6},{8,9},{9,8},{10,11... | collective-permute-start | bytes 307208 | tf_op jit(solution)/shard_map/ppermute | solution.py:1540
  13.9 7.6 %copy-start = (bf16[640,1280]{1,0:T(8,128)(2,1)S(1)}, bf16[640,1280]{1,0:T(8,128)(2,1)}, u32[]{:S(2)}) copy-start(bf16[640,1280]{1,0:T(8,128)(2,1)} %out_w_ref.3) | copy-start | bytes 4915204
  13.9 7.6 %copy-start.6 = (f32[256,128]{1,0:T(8,128)S(1)}, f32[256,128]{1,0:T(8,128)}, u32[]{:S(2)}) copy-start(f32[256,128]{1,0:T(8,128)} %pad_maximum_fusion.1.sin_ref) | copy-start | bytes 393220
  13.9 7.6 %copy-start.8 = (f32[256,128]{1,0:T(8,128)S(1)}, f32[256,128]{1,0:T(8,128)}, u32[]{:S(2)}) copy-start(f32[256,128]{1,0:T(8,128)} %pad_maximum_fusion.cos_ref) | copy-start | bytes 393220
  18.9 2.6 collective-permute-start.2
  25.8 1.7 collective-permute-start.3
  28.3 254.3 %copy-start.22 = (f32[128,1280]{1,0:T(8,128)}, f32[128,1280]{1,0:T(8,128)S(1)}, u32[]{:S(2)}) copy-start(f32[128,1280]{1,0:T(8,128)S(1)} %get-tuple-element.160) | copy-start | bytes 1966084
  28.3 254.3 %copy-start.35 = (f32[128]{0:T(128)}, f32[128]{0:T(128)S(1)}, u32[]{:S(2)}) copy-start(f32[128]{0:T(128)S(1)} %add_rsqrt_fusion.1) | copy-start | bytes 1540
  146.6 132.6 %all-to-all-start = ((f32[16,2,128]{2,1,0:T(2,128)}), f32[16,2,128]{2,1,0:T(2,128)S(1)}, u32[]{:S(2)}, u32[]{:S(2)}) async-start(f32[16,2,128]{2,1,0:T(2,128)} %bitcast.62), calls=%async_computation | async-start | bytes 32768 | tf_op jit(solution)/shard_map/all_to_all | solution.py:1621
  151.4 126.7 %copy-start.26 = (bf16[128,1280]{1,0:T(8,128)(2,1)S(1)}, bf16[128,1280]{1,0:T(8,128)(2,1)}, u32[]{:S(2)}) copy-start(bf16[128,1280]{1,0:T(8,128)(2,1)} %multiply_convert_fusion.x_ref) | copy-start | bytes 983044
  279.2 1.2 collective-permute-start.5
  282.8 1.7 collective-permute-start.6
  296.2 6.2 %collective-permute-start.7 = (bf16[3,256,640]{2,1,0:T(8,128)(2,1)}, bf16[3,256,640]{2,1,0:T(8,128)(2,1)}, u32[]{:S(2)}, u32[]{:S(2)}) collective-permute-start(bf16[3,256,640]{2,1,0:T(8,128)(2,1)} %get-tuple-element.65.mine_ref), channel_id=1, source_target_pairs={{0,1},{1,0},{2,3},{3,2},{4,5},{5,4},{6,7},{7,6},{8,9},{9,8},{10,11... | collective-permute-start | bytes 2949128 | tf_op jit(solution)/shard_map/ppermute | solution.py:1540
  302.4 9.0 %copy-start.27 = (bf16[128,1280]{1,0:T(8,128)(2,1)S(1)}, bf16[128,1280]{1,0:T(8,128)(2,1)}, u32[]{:S(2)}) copy-start(bf16[128,1280]{1,0:T(8,128)(2,1)} %multiply_convert_fusion.x_ref) | copy-start | bytes 983044
  302.4 9.0 %copy-start.33 = (bf16[128,16]{0,1:T(8,128)(2,1)S(1)}, bf16[128,16]{0,1:T(8,128)(2,1)}, u32[]{:S(2)}) copy-start(bf16[128,16]{0,1:T(8,128)(2,1)} %copy-done.32) | copy-start | bytes 12292
  302.4 10.1 %copy-start.5 = (bf16[128,1280]{1,0:T(8,128)(2,1)S(1)}, bf16[128,1280]{1,0:T(8,128)(2,1)}, u32[]{:S(2)}) copy-start(bf16[128,1280]{1,0:T(8,128)(2,1)} %mine_ref.1) | copy-start | bytes 983044
  302.4 10.8 %copy-start.36 = (f32[128]{0:T(128)S(1)}, f32[128]{0:T(128)}, u32[]{:S(2)}) copy-start(f32[128]{0:T(128)} %copy-done.35) | copy-start | bytes 1540
  302.4 10.8 %copy-start.40 = (f32[128]{0:T(128)S(1)}, f32[128]{0:T(128)}, u32[]{:S(2)}) copy-start(f32[128]{0:T(128)} %copy-done.39) | copy-start | bytes 1540
  310.9 1.5 collective-permute-start.8
  312.8 1.7 collective-permute-start.9
  (29 other events, 83.0 us)
